TPU v7x, 32 devices: a whole 2x2x4 slice. The times are simulated.
32 devices in a mesh: dp: 16 (over z, y, x), seq: 2 (over core).
Axes of the slice: x: 2, y: 2, z: 4, core: 2. Of those that a mesh axis runs over, the one named last changes fastest.
Arguments:
- tokens: bfloat16 [16, 1024, 1024], P('dp', 'seq'), may hold values from -6 to 6
- segments: int32 [16, 1024], P('dp'), may hold values from 0 to 2, never falling along the last dimension, each value on 1 to 512 neighbouring positions
- cotangent: bfloat16 [16, 1024, 1024], P('dp', 'seq'), may hold values from -6 to 6
- query_weight: bfloat16 [1024, 1024], P(('dp', 'seq')), may hold values from -0.1875 to 0.1875
- key_weight: bfloat16 [1024, 1024], P(('dp', 'seq')), may hold values from -0.1875 to 0.1875
- value_weight: bfloat16 [1024, 1024], P(('dp', 'seq')), may hold values from -0.1875 to 0.1875
- out_weight: bfloat16 [1024, 1024], P(('dp', 'seq')), may hold values from -1.5 to 1.5
- up_weight: bfloat16 [1024, 4096], P(('dp', 'seq')), may hold values from -0.1875 to 0.1875
- down_weight: bfloat16 [4096, 1024], P(('dp', 'seq')), may hold values from -0.09375 to 0.09375
- query_bias: bfloat16 [1024], P(('dp', 'seq')), may hold values from -3 to 3
- value_bias: bfloat16 [1024], P(('dp', 'seq')), may hold values from -3 to 3
- out_bias: bfloat16 [1024], P(('dp', 'seq')), may hold values from -3 to 3
- up_bias: bfloat16 [4096], P(('dp', 'seq')), may hold values from -3 to 3
- down_bias: bfloat16 [1024], P(('dp', 'seq')), may hold values from -3 to 3
- first_gain: bfloat16 [1024], P(('dp', 'seq')), may hold values from 0.5 to 1.5
- first_shift: bfloat16 [1024], P(('dp', 'seq')), may hold values from -2 to 2
- second_gain: bfloat16 [1024], P(('dp', 'seq')), may hold values from 0.5 to 1.5
- second_shift: bfloat16 [1024], P(('dp', 'seq')), may hold values from -2 to 2
Outputs:
- output: bfloat16 [16, 1024, 1024], P('dp', 'seq')
- input_grad: float32 [16, 1024, 1024], P('dp', 'seq')
- query_weight_grad: float32 [1024, 1024], P(('dp', 'seq'))
- key_weight_grad: float32 [1024, 1024], P(('dp', 'seq'))
- value_weight_grad: float32 [1024, 1024], P(('dp', 'seq'))
- out_weight_grad: float32 [1024, 1024], P(('dp', 'seq'))
- up_weight_grad: float32 [1024, 4096], P(('dp', 'seq'))
- down_weight_grad: float32 [4096, 1024], P(('dp', 'seq'))
- query_bias_grad: float32 [1024], P(('dp', 'seq'))
- value_bias_grad: float32 [1024], P(('dp', 'seq'))
- out_bias_grad: float32 [1024], P(('dp', 'seq'))
- up_bias_grad: float32 [4096], P(('dp', 'seq'))
- down_bias_grad: float32 [1024], P(('dp', 'seq'))
- first_gain_grad: float32 [1024], P(('dp', 'seq'))
- first_shift_grad: float32 [1024], P(('dp', 'seq'))
- second_gain_grad: float32 [1024], P(('dp', 'seq'))
- second_shift_grad: float32 [1024], P(('dp', 'seq'))
Inputs may be any that keep to these rules, and one draw needn't show every extreme that they name: `segments`: document numbers never fall along a sequence; documents are 1 to 512 tokens long.
All inputs are finite; a program needn't handle non-finite values.
Results may differ from a plain program's by a relative error of at most 0.011.
Values may be sent and summed in bfloat16 or wider, within the bound.
No kernel may reach another device: no remote copies, remote signals or barrier semaphores. Data moves between devices by JAX's collectives and lax.ppermute only.
A program may use at most 192 MiB of HBM per device.

v0:
```python
import jax
import jax.numpy as jnp
from jax import lax
from jax.sharding import PartitionSpec as P

HEADS = 16
HEAD_DIM = 64


EPS = 1e-05
MASKED = -1000000000.0


def layer_norm(matrix, norm_gain, norm_shift):
    row_mean = jnp.mean(matrix, axis=-1, keepdims=True)
    centred = matrix - row_mean
    spread = jnp.mean(centred * centred, axis=-1, keepdims=True)
    return centred * lax.rsqrt(spread + EPS) * norm_gain + norm_shift


def gelu_tanh(matrix):
    return jax.nn.gelu(matrix, approximate=True)


def head_major(blocked, head_count):
    sequences, length, model_width = blocked.shape
    return blocked.reshape(sequences, length, head_count, model_width // head_count).transpose(
        2, 0, 1, 3
    )


def head_minor(blocked):
    head_count, sequences, length, head_size = blocked.shape
    return blocked.transpose(1, 2, 0, 3).reshape(sequences, length, head_count * head_size)


def masked_scores(query_head, key_head, head_slope, allowed, offsets):
    scores = jnp.einsum(
        "sid,sjd->sij", query_head, key_head, preferred_element_type=jnp.float32
    ) * HEAD_DIM ** (-0.5)
    scores = scores - head_slope * offsets
    return jnp.where(allowed, scores, MASKED)


def matmul(left, right):
    return jnp.dot(left, right, preferred_element_type=jnp.float32)


def column_sums(matrix):
    return jnp.sum(matrix.astype(jnp.float32), axis=0)


def make_attend_back(allowed, offsets):

    def attend_back(operands):
        query_head, key_head, value_head, head_slope, log_total, grad_head = operands
        scores = masked_scores(query_head, key_head, head_slope, allowed, offsets)
        chances = jnp.exp(scores - log_total[..., None])
        grad_chances = jnp.einsum(
            "sid,sjd->sij", grad_head, value_head, preferred_element_type=jnp.float32
        )
        centred = grad_chances - jnp.sum(chances * grad_chances, axis=-1, keepdims=True)
        grad_scores = (chances * centred).astype(jnp.bfloat16)
        grad_query = jnp.einsum(
            "sij,sjd->sid", grad_scores, key_head, preferred_element_type=jnp.float32
        ) * HEAD_DIM ** (-0.5)
        grad_key = jnp.einsum(
            "sij,sid->sjd", grad_scores, query_head, preferred_element_type=jnp.float32
        ) * HEAD_DIM ** (-0.5)
        grad_value = jnp.einsum(
            "sij,sid->sjd",
            chances.astype(jnp.bfloat16),
            grad_head,
            preferred_element_type=jnp.float32,
        )
        return (grad_query, grad_key, grad_value)

    return attend_back


def body(
    tokens,
    segments,
    cotangent,
    query_weight,
    key_weight,
    value_weight,
    out_weight,
    up_weight,
    down_weight,
    query_bias,
    value_bias,
    out_bias,
    up_bias,
    down_bias,
    first_gain,
    first_shift,
    second_gain,
    second_shift,
):
    shards = (
        query_weight,
        key_weight,
        value_weight,
        out_weight,
        up_weight,
        down_weight,
        query_bias,
        value_bias,
        out_bias,
        up_bias,
        down_bias,
        first_gain,
        first_shift,
        second_gain,
        second_shift,
    )
    whole = (
        lax.all_gather(shards[0], ("dp", "seq"), axis=0, tiled=True),
        lax.all_gather(shards[1], ("dp", "seq"), axis=0, tiled=True),
        lax.all_gather(shards[2], ("dp", "seq"), axis=0, tiled=True),
        lax.all_gather(shards[3], ("dp", "seq"), axis=0, tiled=True),
        lax.all_gather(shards[4], ("dp", "seq"), axis=0, tiled=True),
        lax.all_gather(shards[5], ("dp", "seq"), axis=0, tiled=True),
        lax.all_gather(shards[6], ("dp", "seq"), axis=0, tiled=True),
        lax.all_gather(shards[7], ("dp", "seq"), axis=0, tiled=True),
        lax.all_gather(shards[8], ("dp", "seq"), axis=0, tiled=True),
        lax.all_gather(shards[9], ("dp", "seq"), axis=0, tiled=True),
        lax.all_gather(shards[10], ("dp", "seq"), axis=0, tiled=True),
        lax.all_gather(shards[11], ("dp", "seq"), axis=0, tiled=True),
        lax.all_gather(shards[12], ("dp", "seq"), axis=0, tiled=True),
        lax.all_gather(shards[13], ("dp", "seq"), axis=0, tiled=True),
        lax.all_gather(shards[14], ("dp", "seq"), axis=0, tiled=True),
    )
    (
        query_full,
        key_full,
        value_full,
        out_full,
        up_full,
        down_full,
        query_shift,
        value_shift,
        out_shift,
        up_shift,
        down_shift,
        gain_one,
        shift_one,
        gain_two,
        shift_two,
    ) = whole
    sequences, local_rows, model_width = tokens.shape
    length = segments.shape[1]
    head_count = HEADS
    total_rows = sequences * local_rows
    row_start = lax.axis_index("seq") * local_rows
    inputs = tokens.astype(jnp.float32).reshape(total_rows, model_width)
    first_norm, first_back = jax.vjp(
        layer_norm, inputs, gain_one.astype(jnp.float32), shift_one.astype(jnp.float32)
    )
    first_low = first_norm.astype(jnp.bfloat16)
    queries = (matmul(first_low, query_full) + query_shift.astype(jnp.float32)).astype(jnp.bfloat16)
    keys_local = matmul(first_low, key_full).astype(jnp.bfloat16)
    values_local = (matmul(first_low, value_full) + value_shift.astype(jnp.float32)).astype(
        jnp.bfloat16
    )
    keys_all, values_all = (
        lax.all_gather(
            keys_local.reshape(sequences, local_rows, model_width), "seq", axis=1, tiled=True
        ),
        lax.all_gather(
            values_local.reshape(sequences, local_rows, model_width), "seq", axis=1, tiled=True
        ),
    )
    query_positions = row_start + jnp.arange(local_rows, dtype=jnp.int32)
    key_positions = jnp.arange(length, dtype=jnp.int32)
    query_segments = lax.dynamic_slice_in_dim(segments, row_start, local_rows, 1)
    allowed = (query_positions[:, None] >= key_positions[None, :])[None] & (
        query_segments[:, :, None] == segments[:, None, :]
    )
    offsets = (query_positions[:, None] - key_positions[None, :]).astype(jnp.float32)
    slopes = 2.0 ** (-8.0 * (jnp.arange(head_count, dtype=jnp.float32) + 1.0) / head_count)
    query_heads = head_major(queries.reshape(sequences, local_rows, model_width), head_count)
    key_heads = head_major(keys_all, head_count)
    value_heads = head_major(values_all, head_count)

    def attend(operands):
        query_head, key_head, value_head, head_slope = operands
        scores = masked_scores(query_head, key_head, head_slope, allowed, offsets)
        row_top = jnp.max(scores, axis=-1, keepdims=True)
        log_total = jnp.log(jnp.sum(jnp.exp(scores - row_top), axis=-1, keepdims=True)) + row_top
        shares = jnp.exp(scores - log_total).astype(jnp.bfloat16)
        mixed_head = jnp.einsum(
            "sij,sjd->sid", shares, value_head, preferred_element_type=jnp.float32
        )
        return (mixed_head.astype(jnp.bfloat16), log_total[..., 0])

    mixed_heads, log_totals = lax.map(attend, (query_heads, key_heads, value_heads, slopes))
    mixed = head_minor(mixed_heads).reshape(total_rows, model_width)
    middle = inputs + matmul(mixed, out_full) + out_shift.astype(jnp.float32)
    second_norm, second_back = jax.vjp(
        layer_norm, middle, gain_two.astype(jnp.float32), shift_two.astype(jnp.float32)
    )
    second_low = second_norm.astype(jnp.bfloat16)
    hidden_pre = matmul(second_low, up_full) + up_shift.astype(jnp.float32)
    activated, gelu_back = jax.vjp(gelu_tanh, hidden_pre)
    activated_low = activated.astype(jnp.bfloat16)
    result = middle + matmul(activated_low, down_full) + down_shift.astype(jnp.float32)
    output = result.astype(jnp.bfloat16).reshape(sequences, local_rows, model_width)
    back_full = (
        lax.all_gather(shards[0], ("dp", "seq"), axis=0, tiled=True),
        lax.all_gather(shards[1], ("dp", "seq"), axis=0, tiled=True),
        lax.all_gather(shards[2], ("dp", "seq"), axis=0, tiled=True),
        lax.all_gather(shards[3], ("dp", "seq"), axis=0, tiled=True),
        lax.all_gather(shards[4], ("dp", "seq"), axis=0, tiled=True),
        lax.all_gather(shards[5], ("dp", "seq"), axis=0, tiled=True),
        lax.all_gather(shards[6], ("dp", "seq"), axis=0, tiled=True),
        lax.all_gather(shards[7], ("dp", "seq"), axis=0, tiled=True),
        lax.all_gather(shards[8], ("dp", "seq"), axis=0, tiled=True),
        lax.all_gather(shards[9], ("dp", "seq"), axis=0, tiled=True),
        lax.all_gather(shards[10], ("dp", "seq"), axis=0, tiled=True),
        lax.all_gather(shards[11], ("dp", "seq"), axis=0, tiled=True),
        lax.all_gather(shards[12], ("dp", "seq"), axis=0, tiled=True),
        lax.all_gather(shards[13], ("dp", "seq"), axis=0, tiled=True),
        lax.all_gather(shards[14], ("dp", "seq"), axis=0, tiled=True),
    )
    query_back, key_back, value_back, out_back, up_back, down_back = back_full[:6]
    grad_output = cotangent.astype(jnp.float32).reshape(total_rows, model_width)
    grad_down = grad_output.astype(jnp.bfloat16)
    grad_down_weight = matmul(activated_low.T, grad_down)
    grad_down_bias = column_sums(grad_down)
    grad_activated = matmul(grad_down, down_back.T)
    (grad_hidden,) = gelu_back(grad_activated)
    grad_hidden_low = grad_hidden.astype(jnp.bfloat16)
    grad_up_weight = matmul(second_low.T, grad_hidden_low)
    grad_up_bias = column_sums(grad_hidden_low)
    grad_second = matmul(grad_hidden_low, up_back.T)
    grad_middle_norm, grad_second_gain, grad_second_shift = second_back(grad_second)
    grad_middle = grad_output + grad_middle_norm
    grad_attended = grad_middle.astype(jnp.bfloat16)
    grad_out_weight = matmul(mixed.T, grad_attended)
    grad_out_bias = column_sums(grad_attended)
    grad_mixed = matmul(grad_attended, out_back.T).astype(jnp.bfloat16)
    grad_mixed_heads = head_major(
        grad_mixed.reshape(sequences, local_rows, model_width), head_count
    )
    grad_query_heads, grad_key_heads, grad_value_heads = lax.map(
        make_attend_back(allowed, offsets),
        (query_heads, key_heads, value_heads, slopes, log_totals, grad_mixed_heads),
    )
    grad_keys, grad_values = (
        lax.psum_scatter(
            head_minor(grad_key_heads).astype(jnp.bfloat16), "seq", scatter_dimension=1, tiled=True
        ).astype(jnp.float32),
        lax.psum_scatter(
            head_minor(grad_value_heads).astype(jnp.bfloat16),
            "seq",
            scatter_dimension=1,
            tiled=True,
        ).astype(jnp.float32),
    )
    grad_queries = (
        head_minor(grad_query_heads).reshape(total_rows, model_width).astype(jnp.bfloat16)
    )
    grad_keys = grad_keys.reshape(total_rows, model_width).astype(jnp.bfloat16)
    grad_values = grad_values.reshape(total_rows, model_width).astype(jnp.bfloat16)
    grad_query_weight = matmul(first_low.T, grad_queries)
    grad_key_weight = matmul(first_low.T, grad_keys)
    grad_value_weight = matmul(first_low.T, grad_values)
    grad_query_bias = column_sums(grad_queries)
    grad_value_bias = column_sums(grad_values)
    grad_first = (
        matmul(grad_queries, query_back.T)
        + matmul(grad_keys, key_back.T)
        + matmul(grad_values, value_back.T)
    )
    grad_inputs_norm, grad_first_gain, grad_first_shift = first_back(grad_first)
    input_grad = (grad_middle + grad_inputs_norm).reshape(sequences, local_rows, model_width)
    owned = (
        lax.psum_scatter(grad_query_weight, ("dp", "seq"), scatter_dimension=0, tiled=True),
        lax.psum_scatter(grad_key_weight, ("dp", "seq"), scatter_dimension=0, tiled=True),
        lax.psum_scatter(grad_value_weight, ("dp", "seq"), scatter_dimension=0, tiled=True),
        lax.psum_scatter(grad_out_weight, ("dp", "seq"), scatter_dimension=0, tiled=True),
        lax.psum_scatter(grad_up_weight, ("dp", "seq"), scatter_dimension=0, tiled=True),
        lax.psum_scatter(grad_down_weight, ("dp", "seq"), scatter_dimension=0, tiled=True),
        lax.psum_scatter(grad_query_bias, ("dp", "seq"), scatter_dimension=0, tiled=True),
        lax.psum_scatter(grad_value_bias, ("dp", "seq"), scatter_dimension=0, tiled=True),
        lax.psum_scatter(grad_out_bias, ("dp", "seq"), scatter_dimension=0, tiled=True),
        lax.psum_scatter(grad_up_bias, ("dp", "seq"), scatter_dimension=0, tiled=True),
        lax.psum_scatter(grad_down_bias, ("dp", "seq"), scatter_dimension=0, tiled=True),
        lax.psum_scatter(grad_first_gain, ("dp", "seq"), scatter_dimension=0, tiled=True),
        lax.psum_scatter(grad_first_shift, ("dp", "seq"), scatter_dimension=0, tiled=True),
        lax.psum_scatter(grad_second_gain, ("dp", "seq"), scatter_dimension=0, tiled=True),
        lax.psum_scatter(grad_second_shift, ("dp", "seq"), scatter_dimension=0, tiled=True),
    )
    return (
        output,
        input_grad,
        owned[0],
        owned[1],
        owned[2],
        owned[3],
        owned[4],
        owned[5],
        owned[6],
        owned[7],
        owned[8],
        owned[9],
        owned[10],
        owned[11],
        owned[12],
        owned[13],
        owned[14],
    )


def solution(mesh):
    placed = (
        P("dp", "seq", None),
        P("dp", None),
        P("dp", "seq", None),
        P(("dp", "seq"), None),
        P(("dp", "seq"), None),
        P(("dp", "seq"), None),
        P(("dp", "seq"), None),
        P(("dp", "seq"), None),
        P(("dp", "seq"), None),
        P(("dp", "seq")),
        P(("dp", "seq")),
        P(("dp", "seq")),
        P(("dp", "seq")),
        P(("dp", "seq")),
        P(("dp", "seq")),
        P(("dp", "seq")),
        P(("dp", "seq")),
        P(("dp", "seq")),
    )
    return jax.shard_map(
        body,
        mesh=mesh,
        in_specs=placed,
        out_specs=(
            P("dp", "seq", None),
            P("dp", "seq", None),
            P(("dp", "seq"), None),
            P(("dp", "seq"), None),
            P(("dp", "seq"), None),
            P(("dp", "seq"), None),
            P(("dp", "seq"), None),
            P(("dp", "seq"), None),
            P(("dp", "seq")),
            P(("dp", "seq")),
            P(("dp", "seq")),
            P(("dp", "seq")),
            P(("dp", "seq")),
            P(("dp", "seq")),
            P(("dp", "seq")),
            P(("dp", "seq")),
            P(("dp", "seq")),
        ),
        check_vma=False,
    )
```

profile of v0, /device:TPU:13, one launch (start us, length us, event | category | flops | bytes accessed | tf_op | source)
XLA Modules:
  0.0 1600.6 jit_solution(12220650040272183881)
XLA Ops:
  16.2 40.6 %all-reduce.18 = (bf16[1024]{0:T(1024)(128)(2,1)S(1)}, bf16[1024]{0:T(1024)(128)(2,1)S(1)}, bf16[1024]{0:T(1024)(128)(2,1)S(1)}, bf16[1024]{0:T(1024)(128)(2,1)S...) all-reduce(bf16[1024]{0:T(1024)(128)(2,1)S(1)} %dynamic-update-slic, ...), channel_id=1, replica_groups=mesh['dp'=16,'seq'=2] {'dp','seq'}, use_global_device_ids=true, to_apply=%add.2 | all-reduce | flops 8192 | bytes 32768
  59.9 7.8 all-gather.16.cloned.1.call-done
  67.7 3.9 add_convert_fusion.2
  71.7 54.1 %all-gather.14.cloned.1.call-done = bf16[1024,1024]{1,0:T(8,128)(2,1)} async-done(((bf16[32,1024]{1,0:T(8,128)(2,1)}), bf16[1024,1024]{1,0:T(8,128)(2,1)}) %all-gather.14.cloned.1.call-update) | async-done | bytes 2097168 | tf_op jit(solution)/shard_map/all_gather | solution.py:120
  125.8 3.9 convolution_convert_fusion.2
  131.9 30.6 %all-gather.2 = bf16[32,1,128]{2,1,0:T(2,128)(2,1)S(1)} all-gather(bf16[1,1,128]{2,1,0:T(2,128)(2,1)S(1)} %bitcast.245), channel_id=1, replica_groups=mesh['dp'=16,'seq'=2] {'dp','seq'}, dimensions={0}, use_global_device_ids=true | all-gather | bytes 8448 | tf_op jit(solution)/shard_map/all_gather | solution.py:128
  162.5 21.2 %all-gather.12.cloned.1.call-done = bf16[1024,1024]{1,0:T(8,128)(2,1)} async-done(((bf16[32,1024]{1,0:T(8,128)(2,1)}), bf16[1024,1024]{1,0:T(8,128)(2,1)}) %all-gather.12.cloned.1.call-update) | async-done | bytes 2097168 | tf_op jit(solution)/shard_map/all_gather | solution.py:119
  189.1 6.7 all-gather.26.cloned.1.call-done
  201.9 7.1 all-gather.24.cloned.1.call-done
  215.1 95.2 %while.30 = (s32[]{:T(128)}, bf16[16,1,512,64]{2,3,1,0:T(8,128)(2,1)}, f32[16,1,512]{2,1,0:T(1,128)S(1)}, bf16[16,1,512,64]{3,2,1,0:T(8,128)(2,1)}, bf16[16,1,10...) while((s32[]{:T(128)}, ...), condition=%wide.region_5.6_spmd.clone.clone, body=%wide.region_2.5_spmd.clone.clone.sunk | while | flops 141590016 | bytes 7043709 | solution.py:198
  313.9 33.9 %all-gather.20.cloned.1.call-done = bf16[1024,4096]{1,0:T(8,128)(2,1)} async-done(((bf16[32,4096]{1,0:T(8,128)(2,1)}), bf16[1024,4096]{1,0:T(8,128)(2,1)}) %all-gather.20.cloned.1.call-update) | async-done | bytes 8388624 | tf_op jit(solution)/shard_map/all_gather | solution.py:123
  347.8 10.2 fusion.100
  358.0 68.3 %all-gather.22.cloned.1.call-done = bf16[4096,1024]{1,0:T(8,128)(2,1)} async-done(((bf16[128,1024]{1,0:T(8,128)(2,1)}), bf16[4096,1024]{1,0:T(8,128)(2,1)}) %all-gather.22.cloned.1.call-update) | async-done | bytes 8388624 | tf_op jit(solution)/shard_map/all_gather | solution.py:124
  426.3 13.7 convert_reduce_fusion
  440.0 5.0 multiply_reduce_fusion.1
  454.0 177.1 %while.31 = (s32[]{:T(128)}, bf16[16,1,512,64]{2,3,1,0:T(8,128)(2,1)}, bf16[16,1,1024,64]{2,3,1,0:T(8,128)(2,1)}, bf16[16,1,1024,64]{2,3,1,0:T(8,128)(2,1)}, bf1...) while((s32[]{:T(128)}, ...), condition=%wide.region_12.13_spmd.clone.clone, body=%wide.region_10.12_spmd.clone.clone.sunk | while | flops 344030720 | bytes 17589908 | solution.py:247
  631.7 4.9 fusion.114
  636.6 4.7 fusion.103
  641.9 4.7 fusion.86
  646.6 6.1 reduce-scatter.11.cloned.1.call-done
  652.7 4.7 fusion.83
  657.5 13.3 fusion.99
  671.0 15.7 fusion.90
  688.9 3.4 fusion.113
  692.3 12.5 fusion.80
  711.8 39.9 %all-reduce.17 = (f32[1024]{0:T(1024)S(1)}, f32[1024]{0:T(1024)S(1)}, f32[1024]{0:T(1024)S(1)}, f32[4096]{0:T(1024)S(1)}, f32[1024]{0:T(1024)S(1)}, /*index=5*/f...) all-reduce(f32[1024]{0:T(1024)S(1)} %reduce_sum.186, ...), channel_id=12, replica_groups=mesh['dp'=16,'seq'=2] {'dp','seq'}, use_global_device_ids=true, to_apply=%region_24.25.clone | all-reduce | flops 12288 | bytes 98304
  756.9 8.9 reduce-scatter.19.cloned.1.call-done
  765.9 141.1 %reduce-scatter.13.cloned.1.call-done = f32[32,1024]{1,0:T(8,128)} async-done(((f32[1024,1024]{1,0:T(8,128)}), f32[32,1024]{1,0:T(8,128)}) %reduce-scatter.13.cloned.1.call-update) | async-done | bytes 131088 | tf_op jit(solution)/shard_map/reduce_scatter | solution.py:280
  906.9 141.4 %reduce-scatter.15.cloned.1.call-done = f32[32,1024]{1,0:T(8,128)} async-done(((f32[1024,1024]{1,0:T(8,128)}), f32[32,1024]{1,0:T(8,128)}) %reduce-scatter.15.cloned.1.call-update) | async-done | bytes 131088 | tf_op jit(solution)/shard_map/reduce_scatter | solution.py:281
  1048.3 141.2 %reduce-scatter.17.cloned.1.call-done = f32[32,1024]{1,0:T(8,128)} async-done(((f32[1024,1024]{1,0:T(8,128)}), f32[32,1024]{1,0:T(8,128)}) %reduce-scatter.17.cloned.1.call-update) | async-done | bytes 131088 | tf_op jit(solution)/shard_map/reduce_scatter | solution.py:282
  1189.5 217.0 %reduce-scatter.21.cloned.1.call-done = f32[32,4096]{1,0:T(8,128)} async-done(((f32[1024,4096]{1,0:T(8,128)}), f32[32,4096]{1,0:T(8,128)}) %reduce-scatter.21.cloned.1.call-update) | async-done | bytes 524304 | tf_op jit(solution)/shard_map/reduce_scatter | solution.py:284
  1406.5 187.4 %reduce-scatter.23.cloned.1.call-done = f32[128,1024]{1,0:T(8,128)} async-done(((f32[4096,1024]{1,0:T(8,128)}), f32[128,1024]{1,0:T(8,128)}) %reduce-scatter.23.cloned.1.call-update) | async-done | bytes 524304 | tf_op jit(solution)/shard_map/reduce_scatter | solution.py:285
  (366 shorter events, 332.0 us)
Async XLA Ops:
  7.2 60.5 %copy-start = (bf16[1,512,1024]{2,1,0:T(8,128)(2,1)S(1)}, bf16[1,512,1024]{2,1,0:T(8,128)(2,1)}, u32[]{:S(2)}) copy-start(bf16[1,512,1024]{2,1,0:T(8,128)(2,1)} %param.22) | copy-start | bytes 3145732
  7.2 60.5 %all-gather.16.cloned.1.call-start = ((), (), s32[]{:S(2)}) async-start(), calls=%async_computation.10 | async-start | bytes 2162688 | tf_op jit(solution)/shard_map/all_gather | solution.py:121
  7.9 117.8 %all-gather.14.cloned.1.call-start = ((), (), s32[]{:S(2)}) async-start(), calls=%async_computation.9 | async-start | bytes 2162688 | tf_op jit(solution)/shard_map/all_gather | solution.py:120
  8.7 175.0 %all-gather.12.cloned.1.call-start = ((), (), s32[]{:S(2)}) async-start(), calls=%async_computation.8 | async-start | bytes 2162688 | tf_op jit(solution)/shard_map/all_gather | solution.py:119
  9.4 186.4 %all-gather.26.cloned.1.call-start = ((), (), s32[]{:S(2)}) async-start(), calls=%async_computation.23 | async-start | bytes 3145728 | tf_op jit(solution)/shard_map/all_gather | solution.py:171
  59.9 11.7 copy-start.9
  71.6 60.3 %copy-start.13 = (bf16[128]{0:T(256)(128)(2,1)S(1)}, bf16[128]{0:T(256)(128)(2,1)}, u32[]{:S(2)}) copy-start(bf16[128]{0:T(256)(128)(2,1)} %param.34) | copy-start | bytes 772
  71.6 90.9 %copy-start.12 = (s32[1,1024]{1,0:T(1,128)S(1)}, s32[1,1024]{1,0:T(1,128)}, u32[]{:S(2)}) copy-start(s32[1,1024]{1,0:T(1,128)} %param.23) | copy-start | bytes 12292
  71.7 137.4 %all-gather.24.cloned.1.call-start = ((), (), s32[]{:S(2)}) async-start(), calls=%async_computation.22 | async-start | bytes 3145728 | tf_op jit(solution)/shard_map/all_gather | solution.py:168
  129.7 180.6 %all-gather.18.cloned.1.call-start = ((), (), s32[]{:S(2)}) async-start(), calls=%async_computation.11 | async-start | bytes 2162688 | tf_op jit(solution)/shard_map/all_gather | solution.py:122
  130.3 217.5 %all-gather.20.cloned.1.call-start = ((), (), s32[]{:S(2)}) async-start(), calls=%async_computation.12 | async-start | bytes 8650752 | tf_op jit(solution)/shard_map/all_gather | solution.py:123
  131.0 295.3 %all-gather.22.cloned.1.call-start = ((), (), s32[]{:S(2)}) async-start(), calls=%async_computation.13 | async-start | bytes 8650752 | tf_op jit(solution)/shard_map/all_gather | solution.py:124
  131.8 510.1 %reduce-scatter.9.cloned.1.call-start = ((), (), s32[]{:S(2)}) async-start(), calls=%async_computation.14 | async-start | bytes 3145728 | tf_op jit(solution)/shard_map/reduce_scatter | solution.py:252
  313.5 126.5 %copy-start.1 = (f32[512,1024]{1,0:T(8,128)}, f32[512,1024]{1,0:T(8,128)S(1)}, u32[]{:S(2)}) copy-start(f32[512,1024]{1,0:T(8,128)S(1)} %get-tuple-element.381) | copy-start | bytes 6291460
  426.3 13.7 copy-start.14
  440.0 5.0 copy-start.17
  445.0 2.4 copy-start.3
  447.4 2.0 copy-start.6
  631.0 21.7 %reduce-scatter.11.cloned.1.call-start = ((), (), s32[]{:S(2)}) async-start(), calls=%async_computation.15 | async-start | bytes 3145728 | tf_op jit(solution)/shard_map/reduce_scatter | solution.py:255
  631.6 134.2 %reduce-scatter.19.cloned.1.call-start = ((), (), s32[]{:S(2)}) async-start(), calls=%async_computation.19 | async-start | bytes 4325376 | tf_op jit(solution)/shard_map/reduce_scatter | solution.py:283
  636.6 270.3 %reduce-scatter.13.cloned.1.call-start = ((), (), s32[]{:S(2)}) async-start(), calls=%async_computation.16 | async-start | bytes 4325376 | tf_op jit(solution)/shard_map/reduce_scatter | solution.py:280
  641.4 406.9 %reduce-scatter.15.cloned.1.call-start = ((), (), s32[]{:S(2)}) async-start(), calls=%async_computation.17 | async-start | bytes 4325376 | tf_op jit(solution)/shard_map/reduce_scatter | solution.py:281
  646.6 542.9 %reduce-scatter.17.cloned.1.call-start = ((), (), s32[]{:S(2)}) async-start(), calls=%async_computation.18 | async-start | bytes 4325376 | tf_op jit(solution)/shard_map/reduce_scatter | solution.py:282
  657.4 749.1 %reduce-scatter.21.cloned.1.call-start = ((), (), s32[]{:S(2)}) async-start(), calls=%async_computation.20 | async-start | bytes 17301504 | tf_op jit(solution)/shard_map/reduce_scatter | solution.py:284
  670.8 923.1 %reduce-scatter.23.cloned.1.call-start = ((), (), s32[]{:S(2)}) async-start(), calls=%async_computation.21 | async-start | bytes 17301504 | tf_op jit(solution)/shard_map/reduce_scatter | solution.py:285
  688.9 3.4 copy-start.2
  692.3 12.5 copy-start.5
  692.3 12.7 copy-start.15
  692.3 12.7 copy-start.16
  705.0 1.6 copy-start.7
  706.6 1.8 copy-start.10
  708.4 1.2 copy-start.4
  (2 other events, 1.7 us)
Sparse Core Ops, SparseCore 0:
  10.9 56.7 all-gather.15
  70.6 55.1 all-gather.13
  128.6 55.0 all-gather.11
  185.1 10.7 all-gather.25
  197.2 11.7 all-gather.23
  211.7 56.1 all-gather.17
  270.8 76.9 all-gather.19
  350.6 75.6 all-gather.21
  631.2 8.4 reduce-scatter.8
  641.8 10.8 reduce-scatter.10
  655.6 110.2 reduce-scatter.18
  768.6 138.3 reduce-scatter.12
  909.8 138.4 reduce-scatter.14
  1051.0 138.4 reduce-scatter.16
  1192.2 214.2 reduce-scatter.20
  1409.2 184.6 reduce-scatter.22
where the time goes:
time: 1610 us; the launch traced here: 1600 us
  waiting for transfers between devices  1050 us (65%)
  matrix products  353 us (22%)
  blocking collectives  111 us (7%)
  local copies, waits for them, and re-layouts  50.4 us (3%)
  other arithmetic  23.5 us (1%)
    reduce_scatter x1, waiting for transfers between devices, body(): lax.psum_scatter(grad_up_weight, ('dp', 'seq'), scatter_dimension=0, tile...  217 us
    reduce_scatter x1, waiting for transfers between devices, body(): lax.psum_scatter(grad_down_weight, ('dp', 'seq'), scatter_dimension=0, ti...  187 us
    reduce_scatter x1, waiting for transfers between devices, body(): lax.psum_scatter(grad_key_weight, ('dp', 'seq'), scatter_dimension=0, til...  141 us
    reduce_scatter x1, waiting for transfers between devices, body(): lax.psum_scatter(grad_value_weight, ('dp', 'seq'), scatter_dimension=0, t...  141 us
    reduce_scatter x1, waiting for transfers between devices, body(): lax.psum_scatter(grad_query_weight, ('dp', 'seq'), scatter_dimension=0, t...  141 us
    dot_general x18, matrix products, matmul(): return jnp.dot(left, right, preferred_element_type=jnp.float32)  112 us
    dot_general x32, matrix products, masked_scores(): jnp.einsum('sid,sjd->sij', query_head, key_head, preferred_element_type=j...  91.3 us
    unnamed x2, blocking collectives  80.5 us
  transfers between devices with their start and end apart: 16, of which 14 were waited for; matrix products, arithmetic and copies ran while one was open for 14% of the time, Pallas kernels for 0%

commit v1 on v0

v1 whole, which is shorter than its diff:
```python
import functools

import jax
import jax.numpy as jnp
from jax import lax
from jax.experimental import pallas as pl
from jax.experimental.pallas import tpu as pltpu
from jax.sharding import PartitionSpec as P


HEADS = 16
HEAD_DIM = 64
EPS = 1e-05
FAR = 1e30
BLOCK = 256
REACH = 512
BF = jnp.bfloat16
F32 = jnp.float32


def dot(left, right, contract):
    return lax.dot_general(left, right, (contract, ((), ())), preferred_element_type=F32)


def matmul(left, right):
    return dot(left, right, ((1,), (0,)))


def pick(array, index, axis):
    return lax.dynamic_index_in_dim(array, index, axis, keepdims=False)


def trade(array):
    return lax.ppermute(array, "seq", [(0, 1), (1, 0)])


def seq_gather(block, seq):
    if seq == 2:
        other = trade(block)
        first = lax.axis_index("seq") == 0
        return jnp.where(first, jnp.stack([block, other]), jnp.stack([other, block]))
    return lax.all_gather(block, "seq", axis=0)


def seq_columns(block, seq):
    if seq == 2:
        other = trade(block)
        first = lax.axis_index("seq") == 0
        return jnp.where(
            first,
            jnp.concatenate([block, other], axis=1),
            jnp.concatenate([other, block], axis=1),
        )
    return lax.all_gather(block, "seq", axis=1, tiled=True)


def seq_swap(blocks, seq):
    if seq == 2:
        me = lax.axis_index("seq")
        own, other = pick(blocks, me, 0), trade(pick(blocks, 1 - me, 0))
        return jnp.where(me == 0, jnp.stack([own, other]), jnp.stack([other, own]))
    return lax.all_to_all(blocks, "seq", 0, 0)


def seq_reduce(blocks, seq, send):
    if seq == 2:
        me = lax.axis_index("seq")
        other = trade(pick(blocks, 1 - me, 0).astype(send))
        return pick(blocks, me, 0).astype(F32) + other.astype(F32)
    return lax.psum_scatter(blocks.astype(F32), "seq", scatter_dimension=0, tiled=False)


def seq_total(partial, seq, send):
    if seq == 2:
        return partial + trade(partial.astype(send)).astype(F32)
    return lax.psum(partial, "seq")


def flip(array, bits, count):
    return lax.ppermute(array, "dp", [(i, i ^ bits) for i in range(count)])


def boxed(count):
    return count >= 4 and not count & (count - 1)


def place_kernel(widths, me_ref, *refs):
    near, got = (refs[0], refs[2]), (refs[1], refs[3])
    outs = refs[4:]
    me = me_ref[0]
    coords = (me % 2, (me // 2) % 2)
    for colour in range(2):
        for piece, late in ((near[colour], 0), (got[colour], 1)):
            for early in range(2):
                flips = (early, late) if colour == 0 else (late, early)
                low, side = coords[0] ^ flips[0], coords[1] ^ flips[1]
                start = 0
                for out, width in zip(outs, widths):
                    half = width // 2
                    out[0, side, low, :, colour * half : (colour + 1) * half] = piece[
                        early, 0, :, start : start + half
                    ]
                    start += half


def gather_blocks(blocks, count, after=None):
    rows, widths = blocks[0].shape[0], [b.shape[1] for b in blocks]
    if not boxed(count) or any(w % 256 for w in widths):
        return [lax.all_gather(b, "dp", axis=0, tiled=True) for b in blocks], blocks[0]
    n_far, half = count // 4, sum(widths) // 2
    block = jnp.concatenate([b[:, : w // 2] for b, w in zip(blocks, widths)]
                            + [b[:, w // 2 :] for b, w in zip(blocks, widths)], axis=1)
    if after is not None:
        block, _ = lax.optimization_barrier((block, after))
    slots = [block] + [flip(block, 4 * k, count) for k in range(1, n_far)]
    pieces = []
    for colour in range(2):
        far = jnp.stack([slot[:, colour * half : (colour + 1) * half] for slot in slots])
        first, second = (1, 2) if colour == 0 else (2, 1)
        near = jnp.stack([far, flip(far, first, count)])
        pieces += [near, flip(near, second, count)]
    out_specs = [
        pl.BlockSpec((1, 2, 2, rows, w), lambda k, me: ((me[0] // 4) ^ k, 0, 0, 0, 0))
        for w in widths
    ]
    outs = pl.pallas_call(
        functools.partial(place_kernel, widths),
        grid_spec=pltpu.PrefetchScalarGridSpec(
            num_scalar_prefetch=1,
            grid=(n_far,),
            in_specs=[pl.BlockSpec((2, 1, rows, half), lambda k, me: (0, k, 0, 0))] * 4,
            out_specs=out_specs,
        ),
        out_shape=[jax.ShapeDtypeStruct((n_far, 2, 2, rows, w), block.dtype) for w in widths],
    )(lax.axis_index("dp").astype(jnp.int32)[None], *pieces)
    return [out.reshape(count * rows, w) for out, w in zip(outs, widths)], slots[-1]


def gather_small(block, count):
    if not boxed(count):
        return lax.all_gather(block, "dp", axis=0)
    slots = jnp.stack([block] + [flip(block, 4 * k, count) for k in range(1, count // 4)])
    near = jnp.stack([slots, flip(slots, 2, count)], 1)
    whole = jnp.stack([near, flip(near, 1, count)], 2)
    whole = whole.reshape((count,) + block.shape).astype(F32)
    ids = jnp.arange(count)
    order = ((ids[:, None] ^ lax.axis_index("dp")) == ids[None, :]).astype(F32)
    return jnp.sum(order.reshape(count, count, 1, 1) * whole[None], axis=1)


def add_low(a, b):
    return (a.astype(F32) + b.astype(F32)).astype(b.dtype)


def scatter_near(grads, count, colour):
    me = lax.axis_index("dp")
    side, low = (me // 2) % 2, me % 2
    box = grads.reshape((count // 4, 2, 2) + grads.shape[1:])
    if colour == 0:
        order = ((1, 2, side), (1, 1, low))
    else:
        order = ((2, 1, low), (1, 2, side))
    for axis, bit, mine in order:
        got = flip(pick(box, 1 - mine, axis), bit, count)
        box = add_low(pick(box, mine, axis), got)
    return box


def scatter_far(box, count):
    far = lax.axis_index("dp") // 4
    total = pick(box, far, 0).astype(F32)
    for k in range(1, count // 4):
        total = total + flip(pick(box, far ^ k, 0), 4 * k, count).astype(F32)
    return total


def grad_kernel(widths, me_ref, *refs):
    n = len(widths)
    lefts, rights = refs[:n], refs[n : 2 * n]
    outs = refs[2 * n :]
    me = me_ref[0]
    coords = (me % 2, (me // 2) % 2)
    start = 0
    for left, right, width in zip(lefts, rights, widths):
        half = width // 2
        grads = dot(left[...], right[...], ((0,), (0,))).astype(BF)
        rows = grads.shape[0] // 4
        for side in range(2):
            for low in range(2):
                block = grads[(2 * side + low) * rows : (2 * side + low + 1) * rows]
                for colour in range(2):
                    mine = (coords[0] ^ low, coords[1] ^ side)
                    first, second = (mine[1], mine[0]) if colour == 0 else mine
                    part = block[:, colour * half : (colour + 1) * half]
                    outs[colour][first, second, 0, :, start : start + half] = part
        start += half


def grad_blocks(lefts, rights, count, columns=None):
    length, widths = lefts[0].shape[0], [r.shape[1] for r in rights]
    if columns is not None:
        widths[-1] = columns[1]
    n_far = count // 4
    depth = lefts[0].shape[1] // n_far
    half = sum(widths) // 2
    shape = (2, 2, n_far, depth // 4, half)
    in_specs = [pl.BlockSpec((length, depth), lambda k, me: (0, (me[0] // 4) ^ k)) for _ in lefts]
    in_specs += [pl.BlockSpec((length, w), lambda k, me: (0, 0)) for w in widths]
    if columns is not None:
        in_specs[-1] = pl.BlockSpec((length, widths[-1]), lambda k, me: (0, me[1]))
    out_spec = pl.BlockSpec((2, 2, 1) + shape[3:], lambda k, me: (0, 0, k, 0, 0))
    me = [lax.axis_index("dp").astype(jnp.int32), lax.axis_index("seq").astype(jnp.int32)]
    return pl.pallas_call(
        functools.partial(grad_kernel, widths),
        grid_spec=pltpu.PrefetchScalarGridSpec(
            num_scalar_prefetch=1, grid=(n_far,), in_specs=in_specs, out_specs=[out_spec] * 2
        ),
        out_shape=[jax.ShapeDtypeStruct(shape, BF)] * 2,
    )(jnp.stack(me), *lefts, *rights)


def scatter_grads(lefts, rights, count, columns=None):
    widths = [r.shape[1] for r in rights]
    if columns is not None:
        widths[-1] = columns[1]
    if not boxed(count) or any(w % 256 for w in widths):
        if columns is not None:
            last = lax.dynamic_slice_in_dim(rights[-1], columns[0] * columns[1], columns[1], 1)
            rights = rights[:-1] + [last]
        return [
            lax.psum_scatter(
                dot(a, b, ((0,), (0,))), "dp", scatter_dimension=0, tiled=True
            )
            for a, b in zip(lefts, rights)
        ]
    pieces = []
    for colour, grads in enumerate(grad_blocks(lefts, rights, count, columns)):
        first, second = (2, 1) if colour == 0 else (1, 2)
        got = flip(grads[1], first, count)
        keep, send = add_low(grads[0, 0], got[0]), add_low(grads[0, 1], got[1])
        pieces.append(add_low(keep, flip(send, second, count)))
    total = jnp.concatenate([p[0] for p in pieces], axis=1).astype(F32)
    for k in range(1, count // 4):
        part = jnp.concatenate([p[k] for p in pieces], axis=1)
        total = total + flip(part, 4 * k, count).astype(F32)
    sums, start, half = [], 0, sum(widths) // 2
    for width in widths:
        step = width // 2
        sums.append(
            jnp.concatenate(
                [total[:, start : start + step], total[:, half + start : half + start + step]], axis=1
            )
        )
        start += step
    return sums


PAIR = 2 * HEAD_DIM


def window(block):
    return max(0, block - REACH // BLOCK) * BLOCK, (block + 1) * BLOCK


def distances(row_ref, col_ref, block):
    start, stop = window(block)
    shape = (stop - start, BLOCK)
    key = lax.broadcasted_iota(jnp.int32, shape, 0) + start
    query = lax.broadcasted_iota(jnp.int32, shape, 1) + block * BLOCK
    same = col_ref[start:stop, :] == row_ref[:, block * BLOCK : (block + 1) * BLOCK]
    return jnp.where((query >= key) & same, (query - key).astype(F32), FAR)


def chances_of(query, key, far, slope):
    scores = dot(key, query, ((1,), (1,))) - slope * far
    top = jnp.max(scores, axis=0, keepdims=True)
    grown = jnp.exp(scores - top)
    return grown * (1.0 / jnp.sum(grown, axis=0, keepdims=True))


def attend_kernel(n_blocks, first, slope_ref, row_ref, col_ref, qkv_ref, o_ref, *far_refs):
    pair = pl.program_id(0)

    @pl.when(pair == 0)
    def _():
        for block in range(n_blocks):
            far_refs[block][...] = distances(row_ref, col_ref, block)

    left = lax.broadcasted_iota(jnp.int32, (BLOCK, PAIR), 1) < HEAD_DIM
    for block in range(n_blocks):
        start, stop = window(block)
        rows = slice(block * BLOCK, (block + 1) * BLOCK)
        query = qkv_ref[rows, :PAIR] * BF(HEAD_DIM**-0.5)
        key, value = qkv_ref[start:stop, PAIR : 2 * PAIR], qkv_ref[start:stop, 2 * PAIR :]
        parts = []
        for side in range(2):
            mine = jnp.where(left if side == 0 else ~left, query, 0)
            slope = slope_ref[2 * (pair + first) + side]
            share = chances_of(mine, key, far_refs[block][...], slope).astype(BF)
            parts.append(dot(share, value, ((0,), (0,))))
        o_ref[rows, :] = jnp.where(left, parts[0], parts[1]).astype(BF)


def attend_back_kernel(
    n_blocks, first, slope_ref, row_ref, col_ref, qkv_ref, g_ref, d_ref, k_sum, v_sum, *far_refs
):
    pair = pl.program_id(0)

    @pl.when(pair == 0)
    def _():
        for block in range(n_blocks):
            far_refs[block][...] = distances(row_ref, col_ref, block)

    left = lax.broadcasted_iota(jnp.int32, (BLOCK, PAIR), 1) < HEAD_DIM
    scale = HEAD_DIM**-0.5
    for block in range(n_blocks):
        start, stop = window(block)
        rows = slice(block * BLOCK, (block + 1) * BLOCK)
        wide = lax.broadcasted_iota(jnp.int32, (stop - start, PAIR), 1) < HEAD_DIM
        query = qkv_ref[rows, :PAIR] * BF(scale)
        grad = g_ref[rows, :]
        key, value = qkv_ref[start:stop, PAIR : 2 * PAIR], qkv_ref[start:stop, 2 * PAIR :]
        dq, dk, dv = [], [], []
        for side in range(2):
            keep = left if side == 0 else ~left
            slope = slope_ref[2 * (pair + first) + side]
            chances = chances_of(jnp.where(keep, query, 0), key, far_refs[block][...], slope)
            g_chances = dot(value, jnp.where(keep, grad, 0), ((1,), (1,)))
            product = chances * g_chances
            inner = jnp.sum(product, axis=0, keepdims=True)
            g_scores = (product - chances * inner).astype(BF)
            dv.append(matmul(chances.astype(BF), grad))
            dk.append(matmul(g_scores, query))
            dq.append(dot(g_scores, key, ((0,), (0,))))
        d_ref[rows, :PAIR] = (jnp.where(left, dq[0], dq[1]) * scale).astype(BF)
        dk, dv = jnp.where(wide, dk[0], dk[1]), jnp.where(wide, dv[0], dv[1])
        old = block * BLOCK - start
        if old:
            k_sum[start : start + old, :] += dk[:old]
            v_sum[start : start + old, :] += dv[:old]
        k_sum[rows, :] = dk[old:]
        v_sum[rows, :] = dv[old:]
    d_ref[:, PAIR : 2 * PAIR] = k_sum[...].astype(BF)
    d_ref[:, 2 * PAIR :] = v_sum[...].astype(BF)


def far_scratch(length):
    return [
        pltpu.VMEM((window(block)[1] - window(block)[0], BLOCK), F32)
        for block in range(length // BLOCK)
    ]


def attend_specs(length, first, widths):
    fixed = [
        pl.BlockSpec(memory_space=pltpu.SMEM),
        pl.BlockSpec((1, length), lambda p: (0, 0)),
        pl.BlockSpec((length, 1), lambda p: (0, 0)),
    ]
    return fixed + [pl.BlockSpec((length, w), lambda p: (0, p + first)) for w in widths]


def attend(slopes, row, col, qkv, pairs):
    length = qkv.shape[0]
    return pl.pallas_call(
        functools.partial(attend_kernel, length // BLOCK, pairs[0]),
        out_shape=jax.ShapeDtypeStruct((length, len(pairs) * PAIR), BF),
        grid=(len(pairs),),
        in_specs=attend_specs(length, pairs[0], [3 * PAIR]),
        out_specs=pl.BlockSpec((length, PAIR), lambda p: (0, p)),
        scratch_shapes=far_scratch(length),
    )(slopes, row, col, qkv)


def attend_back(slopes, row, col, qkv, grads, pairs):
    length = qkv.shape[0]
    return pl.pallas_call(
        functools.partial(attend_back_kernel, length // BLOCK, pairs[0]),
        out_shape=jax.ShapeDtypeStruct((length, len(pairs) * 3 * PAIR), BF),
        grid=(len(pairs),),
        in_specs=attend_specs(length, pairs[0], [3 * PAIR, PAIR]),
        out_specs=pl.BlockSpec((length, 3 * PAIR), lambda p: (0, p)),
        scratch_shapes=[pltpu.VMEM((length, PAIR), F32)] * 2 + far_scratch(length),
    )(slopes, row, col, qkv, grads)


def normed(matrix):
    centred = matrix - jnp.mean(matrix, axis=-1, keepdims=True)
    spread = jnp.mean(centred * centred, axis=-1, keepdims=True)
    inverse = lax.rsqrt(spread + EPS)
    return centred * inverse, inverse


def norm_back(grad, gain, unit, inverse):
    scaled = grad * gain
    return inverse * (
        scaled
        - jnp.mean(scaled, axis=-1, keepdims=True)
        - unit * jnp.mean(scaled * unit, axis=-1, keepdims=True)
    )


def gelu_and_slope(u):
    c = 0.7978845608
    t = jnp.tanh(c * (u + 0.044715 * u * u * u))
    slope = 0.5 * (1.0 + t) + 0.5 * u * (1.0 - t * t) * (c * (1.0 + 3 * 0.044715 * u * u))
    return 0.5 * u * (1.0 + t), slope


def make_body(dp, seq):
    def body(
        tokens, segments, cotangent,
        query_weight, key_weight, value_weight, out_weight, up_weight, down_weight,
        query_bias, value_bias, out_bias, up_bias, down_bias,
        first_gain, first_shift, second_gain, second_shift,
    ):
        me_seq = lax.axis_index("seq")
        _, local, width = tokens.shape
        length = segments.shape[1]
        rows = query_weight.shape[0]
        hidden = up_weight.shape[1]
        hidden_rows = down_weight.shape[0]
        head_cols = width // seq
        heads = HEADS // seq
        hidden_cols = hidden // seq

        pairs = heads // 2
        small_params = (
            query_bias, value_bias, out_bias, up_bias, down_bias,
            first_gain, first_shift, second_gain, second_shift,
        )
        small_sizes = [v.shape[0] for v in small_params]
        offsets = [sum(small_sizes[:i]) for i in range(len(small_sizes))]

        qkv_own = jnp.stack(
            [w.reshape(rows, seq, pairs, PAIR) for w in (query_weight, key_weight, value_weight)], 3
        ).transpose(1, 0, 2, 3, 4)
        qkv_own = seq_swap(qkv_own.reshape(seq, rows, 3 * head_cols), seq)
        (qkv_full,), mark = gather_blocks([qkv_own.reshape(seq * rows, 3 * head_cols)], dp)

        small = jnp.concatenate(small_params)
        small_all = seq_gather(small, seq).reshape(-1, 128)
        small_all = gather_small(small_all, dp).reshape(dp * seq, -1)

        up_own = up_weight.reshape(rows, dp, seq, hidden_rows).transpose(2, 0, 1, 3)
        out_own = out_weight.reshape(rows, seq, head_cols).transpose(1, 0, 2)
        up_own = jnp.concatenate([up_own.reshape(seq, rows, hidden_cols), out_own], axis=2)
        up_own = seq_swap(up_own, seq).reshape(seq * rows, -1)
        (up_full, out_half), mark = gather_blocks(
            [up_own[:, :hidden_cols], up_own[:, hidden_cols:]], dp, mark
        )
        out_full = seq_columns(out_half, seq)
        (down_full,), _ = gather_blocks([down_weight], dp, mark)

        tokens_all = seq_gather(tokens[0], seq).reshape(length, width)
        grad_output = seq_gather(cotangent[0], seq).reshape(length, width)

        def small_of(index):
            return small_all[:, offsets[index] : offsets[index] + small_sizes[index]].reshape(-1)

        (q_shift, v_shift, o_shift, u_shift, d_shift, gain_one, shift_one, gain_two, shift_two) = [
            small_of(i) for i in range(9)
        ]

        def own_pairs(vector):
            return lax.dynamic_slice_in_dim(vector, me_seq * head_cols, head_cols, 0).reshape(pairs, PAIR)

        u_own = pick(u_shift.reshape(dp, seq, hidden_rows), me_seq, 1).reshape(-1)
        qkv_shift = jnp.stack(
            [own_pairs(q_shift), jnp.zeros((pairs, PAIR), F32), own_pairs(v_shift)], axis=1
        ).reshape(-1)

        inputs = tokens_all.astype(F32)
        unit_one, _ = normed(inputs)
        first_low = (unit_one * gain_one + shift_one).astype(BF)
        qkv = (matmul(first_low, qkv_full) + qkv_shift).astype(BF)
        ids = (me_seq * heads + jnp.arange(heads) + 1).astype(F32)
        slopes = 2.0 ** (-8.0 * ids / HEADS)
        row, col = segments.reshape(1, length), segments.reshape(length, 1)
        mixed_own = attend(slopes, row, col, qkv, range(pairs))
        mixed = seq_columns(mixed_own, seq)
        middle = inputs + matmul(mixed, out_full) + o_shift
        unit_two, inverse_two = normed(middle)
        second_low = (unit_two * gain_two + shift_two).astype(BF)
        hidden_pre = matmul(second_low, up_full) + u_own
        activated, hidden_slope = gelu_and_slope(hidden_pre)
        activated = activated.astype(BF)
        hidden_slope = hidden_slope.astype(BF)

        (down_sum,) = scatter_grads([activated], [grad_output], dp)
        g_hidden = (dot(grad_output, down_full, ((1,), (1,))) * hidden_slope.astype(F32)).astype(BF)
        (up_sum,) = scatter_grads([second_low], [g_hidden], dp)
        g_second = seq_total(dot(g_hidden, up_full, ((1,), (1,))), seq, BF)
        g_middle = grad_output.astype(F32) + norm_back(g_second, gain_two, unit_two, inverse_two)
        g_attn = g_middle.astype(BF)
        out_own = lax.dynamic_slice_in_dim(out_full, me_seq * head_cols, head_cols, 0)
        g_mixed = dot(g_attn, out_own, ((1,), (1,))).astype(BF)
        groups = [range(pairs // 2), range(pairs // 2, pairs)] if pairs > 1 else [range(pairs)]
        g_qkv = [attend_back(slopes, row, col, qkv, g_mixed, group) for group in groups]
        first_sum, out_sum = scatter_grads(
            [first_low, mixed], [g_qkv[0], g_attn], dp, (me_seq, head_cols)
        )
        qkv_sums = [first_sum] + [scatter_grads([first_low], [part], dp)[0] for part in g_qkv[1:]]
        g_qkv = jnp.concatenate(g_qkv, axis=1)
        g_first = dot(g_qkv, qkv_full, ((1,), (1,))).reshape(seq, local, width)
        g_first = seq_reduce(g_first, seq, BF)
        unit_own, inverse_own = normed(tokens[0].astype(F32))
        g_middle_own = pick(g_middle.reshape(seq, local, width), me_seq, 0)
        input_grad = g_middle_own + norm_back(g_first, gain_one, unit_own, inverse_own)

        lowered = matmul(activated, down_full).reshape(seq, local, width)
        middle_own = pick(middle.reshape(seq, local, width), me_seq, 0)
        output = (middle_own + seq_reduce(lowered, seq, F32) + d_shift).astype(BF)[None]

        def to_rows(total):
            return seq_swap(total.reshape(seq, rows, -1), seq).transpose(1, 0, 2)

        qkv_rows = to_rows(jnp.concatenate(qkv_sums, axis=1))
        qkv_rows = qkv_rows.reshape(rows, seq, pairs, 3, PAIR)
        weight_grads = [qkv_rows[:, :, :, i].reshape(rows, width) for i in range(3)]
        up_rows = to_rows(jnp.concatenate([up_sum, out_sum], axis=1))
        up_grad = (
            up_rows[:, :, :hidden_cols]
            .reshape(rows, seq, dp, hidden_rows)
            .transpose(0, 2, 1, 3)
            .reshape(rows, hidden)
        )
        out_grad = up_rows[:, :, hidden_cols:].reshape(rows, width)

        def sums(matrix):
            return jnp.sum(matrix.astype(F32), axis=0)

        mine = jnp.arange(seq) == me_seq

        def heads_only(vector):
            return jnp.where(mine[:, None], vector.reshape(1, -1), 0.0).reshape(-1)

        share = 1.0 / seq
        qkv_columns = sums(g_qkv).reshape(pairs, 3, PAIR)
        up_bias_grad = jnp.where(
            mine[None, :, None], sums(g_hidden).reshape(dp, 1, hidden_rows), 0.0
        )
        vectors = [
            heads_only(qkv_columns[:, 0]), heads_only(qkv_columns[:, 2]), sums(g_attn) * share,
            up_bias_grad, sums(cotangent[0]), sums(g_first * unit_own), sums(g_first),
            sums(g_second * unit_two) * share, sums(g_second) * share,
        ]
        packed = jnp.concatenate(
            [v.reshape(dp, seq, m) for v, m in zip(vectors, small_sizes)], axis=2
        ).reshape(dp, seq * sum(small_sizes) // 128, 128)
        if boxed(dp):
            small_sum = scatter_far(scatter_near(packed, dp, 0), dp)
        else:
            small_sum = lax.psum_scatter(packed, "dp", scatter_dimension=0, tiled=False)
        small_grad = seq_reduce(small_sum.reshape(seq, -1), seq, F32)
        small_grads = [
            small_grad[offsets[i] : offsets[i] + small_sizes[i]] for i in range(9)
        ]
        return (
            output, input_grad[None], *weight_grads, out_grad, up_grad, down_sum, *small_grads
        )

    return body


def solution(mesh):
    both = ("dp", "seq")
    matrix, vector = P(both, None), P(both)
    dp, seq = mesh.shape["dp"], mesh.shape["seq"]
    layer = make_body(dp, seq)

    return jax.shard_map(
        layer,
        mesh=mesh,
        in_specs=(P("dp", "seq", None), P("dp", None), P("dp", "seq", None))
        + (matrix,) * 6
        + (vector,) * 9,
        out_specs=(P("dp", "seq", None),) * 2 + (matrix,) * 6 + (vector,) * 9,
        check_vma=False,
    )
```

time: 1610 us -> 524 us (0.33)
  the two profiles are of different devices: /device:TPU:13 before, /device:TPU:0 now
where the time goes in v1:
time: 524 us; the launch traced here: 515 us
  waiting for transfers between devices  157 us (30%)
  starting transfers between devices  105 us (20%)
  Pallas kernels  91.3 us (17%)
  other arithmetic  67.6 us (13%)
  matrix products  47.2 us (9%)
  local copies, waits for them, and re-layouts  44.1 us (8%)
    ppermute x59, waiting for transfers between devices, flip(): return lax.ppermute(array, 'dp', [(i, i ^ bits) for i in range(count)])  156 us
    ppermute x59, starting transfers between devices, flip(): return lax.ppermute(array, 'dp', [(i, i ^ bits) for i in range(count)])  103 us
    dot_general x8, matrix products, dot(): lax.dot_general(left, right, (contract, ((), ())), preferred_element_type...  47.2 us
    pallas_call x4, Pallas kernels, grad_blocks(): pl.pallas_call(functools.partial(grad_kernel, widths), grid_spec=pltpu.Pr...  33.1 us
    pallas_call x2, Pallas kernels, attend_back(): pl.pallas_call(functools.partial(attend_back_kernel, length // BLOCK, pai...  29.6 us
    pallas_call x3, Pallas kernels, gather_blocks(): pl.pallas_call(functools.partial(place_kernel, widths), grid_spec=pltpu.P...  15 us
    pallas_call x1, Pallas kernels, attend(): pl.pallas_call(functools.partial(attend_kernel, length // BLOCK, pairs[0]...  13.6 us
    reduce_sum x5, other arithmetic, sums(): return jnp.sum(matrix.astype(F32), axis=0)  12.9 us
  transfers between devices with their start and end apart: 72, of which 29 were waited for; matrix products, arithmetic and copies ran while one was open for 22% of the time, Pallas kernels for 18%

profile of v1, /device:TPU:0, one launch (start us, length us, event | category | flops | bytes accessed | tf_op | source)
XLA Modules:
  0.0 515.0 jit_solution(5862222555583159085)
XLA Ops:
  40.3 8.0 %collective-permute-start.17 = (bf16[64,2560]{1,0:T(8,128)(2,1)S(1)}, bf16[64,2560]{1,0:T(8,128)(2,1)S(1)}, u32[]{:S(2)}, u32[]{:S(2)}) collective-permute-start(bf16[64,2560]{1,0:T(8,128)(2,1)S(1)} %pad_maximum_fusion.15), channel_id=1, source_target_pairs={{0,8},{2,10},{4,12},{6,14},{8,0},{10,2},{12,4},{14,6},{16,24},{18,... | collective-permute-start | bytes 983048 | tf_op jit(solution)/shard_map/ppermute | solution.py:80
  48.5 7.7 %collective-permute-done.9 = bf16[64,1536]{1,0:T(8,128)(2,1)S(1)} collective-permute-done((bf16[64,1536]{1,0:T(8,128)(2,1)S(1)}, bf16[64,1536]{1,0:T(8,128)(2,1)S(1)}, u32[]{:S(2)}, u32[]{:S(2)}) %collective-permute-start.9) | collective-permute-done | bytes 196640 | tf_op jit(solution)/shard_map/ppermute | solution.py:80
  60.0 11.4 %collective-permute-start.25 = (bf16[128,1024]{1,0:T(8,128)(2,1)S(1)}, bf16[128,1024]{1,0:T(8,128)(2,1)S(1)}, u32[]{:S(2)}, u32[]{:S(2)}) collective-permute-start(bf16[128,1024]{1,0:T(8,128)(2,1)S(1)} %copy-done.39), channel_id=1, source_target_pairs={{0,8},{2,10},{4,12},{6,14},{8,0},{10,2},{12,4},{14,6},{16,24},{18,... | collective-permute-start | bytes 786440 | tf_op jit(solution)/shard_map/ppermute | solution.py:80
  83.2 9.9 %collective-permute-done.26 = bf16[128,1024]{1,0:T(8,128)(2,1)S(1)} collective-permute-done((bf16[128,1024]{1,0:T(8,128)(2,1)S(1)}, bf16[128,1024]{1,0:T(8,128)(2,1)S(1)}, u32[]{:S(2)}, u32[]{:S(2)}) %collective-permute-start.26) | collective-permute-done | bytes 262176 | tf_op jit(solution)/shard_map/ppermute | solution.py:80
  106.8 16.4 %collective-permute-done.30 = bf16[4,128,512]{2,1,0:T(8,128)(2,1)S(1)} collective-permute-done((bf16[4,128,512]{2,1,0:T(8,128)(2,1)S(1)}, bf16[4,128,512]{2,1,0:T(8,128)(2,1)S(1)}, u32[]{:S(2)}, u32[]{:S(2)}) %collective-permute-start.30) | collective-permute-done | bytes 524320 | tf_op jit(solution)/shard_map/ppermute | solution.py:80
  132.4 4.8 shard_map.305
  137.2 7.5 %add_convert_fusion.qkv_ref = bf16[1024,1536]{1,0:T(8,128)(2,1)} fusion(bf16[1024,1024]{1,0:T(8,128)(2,1)} %bitcast.470, bf16[1024,1536]{1,0:T(8,128)(2,1)} %bitcast.466, f32[1536]{0:T(1024)S(1)} %copy-done.44), kind=kOutput, calls=%fused_computation.13 | convolution fusion | flops 3224371200 | bytes 8394752 | tf_op jit(solution)/shard_map/dot_general | solution.py:22
  144.8 13.6 %shard_map.306 = bf16[1024,512]{1,0:T(8,128)(2,1)} custom-call(f32[8]{0:T(128)} %multiply_power_fusion.slope_ref, s32[1,1024]{1,0:T(1,128)} %row_ref.5, s32[1024,1]{1,0:T(8,128)} %copy.114.col_ref, bf16[1024,1536]{1,0:T(8,128)(2,1)} %add_convert_fusion.qkv_ref), custom_call_target="tpu_custom_call" | custom-call | tf_op jit(solution)/shard_map/pallas_call | solution.py:365
  158.8 5.3 %shard_map.307 = (bf16[4,2,2,64,2048]{4,3,2,1,0:T(8,128)(2,1)}, bf16[4,2,2,64,512]{4,3,2,1,0:T(8,128)(2,1)}) custom-call(s32[1]{0:T(128)} %bitcast.13.me_ref, bf16[2,4,64,1280]{3,2,1,0:T(8,128)(2,1)} %pad_maximum_fusion.1.refs_0_, bf16[2,4,64,1280]{3,2,1,0:T(8,128)(2,1)} %collective-permute-done.21.refs_1_, ...), custom_call_target="tpu_custom_call" | custom-call | tf_op jit(solution)/shard_map/pallas_call | solution.py:126
  171.2 4.3 collective-permute-done.31.refs_3_
  175.5 4.9 shard_map.308
  193.5 7.8 %multiply_convert_fusion.1 = (bf16[1024,2048]{1,0:T(8,128)(2,1)}, f32[1024,2048]{1,0:T(8,128)S(1)}) fusion(f32[2048]{0:T(1024)S(1)} %bitcast.506, bf16[1024,1024]{1,0:T(8,128)(2,1)S(1)} %add_convert_fusion.1.refs_0_, bf16[1024,2048]{1,0:T(8,128)(2,1)S(1)} %bitcast.512), kind=kOutput, calls=%fused_computation.11 | convolution fusion | flops 4315938816 | bytes 18882560 | tf_op jit(solution)/shard_map/dot_general | solution.py:22
  201.3 9.7 %convert_reduce_fusion = (f32[2048]{0:T(1024)S(1)}, bf16[1024,2048]{1,0:T(8,128)(2,1)S(1)}) fusion(f32[1024,2048]{1,0:T(8,128)S(1)} %get-tuple-element.178, f32[2048]{0:T(1024)S(1)} %bitcast.507, bf16[1024,1024]{1,0:T(8,128)(2,1)S(1)} %bitcast.461, bf16[2048,1024]{1,0:T(8,128)(2,1)S(1)} %bitcast.464), kind=kOutput, calls=%fused_computation.9 | convolution fusion | flops 4345296896 | bytes 18890752 | tf_op jit(solution)/shard_map/dot_general | solution.py:22
  211.0 6.6 %fusion.87 = (bf16[1024,1024]{1,0:T(8,128)(2,1)}, f32[1024,1024]{1,0:T(8,128)}) fusion(bf16[1024,2048]{1,0:T(8,128)(2,1)S(1)} %get-tuple-element.182.refs_1_, bf16[1024,2048]{1,0:T(8,128)(2,1)S(1)} %bitcast.513), kind=kOutput, calls=%fused_computation.314 | convolution fusion | flops 4296015872 | bytes 14680064 | tf_op jit(solution)/shard_map/dot_general | solution.py:22
  217.6 9.6 %shard_map.313 = (bf16[2,2,4,64,1024]{4,3,2,1,0:T(8,128)(2,1)}, bf16[2,2,4,64,1024]{4,3,2,1,0:T(8,128)(2,1)}) custom-call(s32[2]{0:T(128)} %pad_add_fusion.me_ref, bf16[1024,1024]{1,0:T(8,128)(2,1)} %copy-done.8, bf16[1024,2048]{1,0:T(8,128)(2,1)} %copy-done.13), custom_call_target="tpu_custom_call" | custom-call | tf_op jit(solution)/shard_map/pallas_call | solution.py:213
  227.2 9.2 %shard_map.314 = (bf16[2,2,4,128,512]{4,3,2,1,0:T(8,128)(2,1)}, bf16[2,2,4,128,512]{4,3,2,1,0:T(8,128)(2,1)}) custom-call(s32[2]{0:T(128)} %pad_add_fusion.me_ref, bf16[1024,2048]{1,0:T(8,128)(2,1)} %get-tuple-element.177.refs_0_, bf16[1024,1024]{1,0:T(8,128)(2,1)} %bitcast.460), custom_call_target="tpu_custom_call" | custom-call | tf_op jit(solution)/shard_map/pallas_call | solution.py:213
  246.8 4.5 fusion.88
  252.0 11.9 %collective-permute-done.59 = bf16[2,4,128,512]{3,2,1,0:T(8,128)(2,1)S(1)} collective-permute-done((bf16[2,4,128,512]{3,2,1,0:T(8,128)(2,1)S(1)}, bf16[2,4,128,512]{3,2,1,0:T(8,128)(2,1)S(1)}, u32[]{:S(2)}, u32[]{:S(2)}) %collective-permute-start.59) | collective-permute-done | bytes 1048608 | tf_op jit(solution)/shard_map/ppermute | solution.py:80
  268.3 18.1 %collective-permute-done.51 = bf16[2,4,64,1024]{3,2,1,0:T(8,128)(2,1)S(1)} collective-permute-done((bf16[2,4,64,1024]{3,2,1,0:T(8,128)(2,1)S(1)}, bf16[2,4,64,1024]{3,2,1,0:T(8,128)(2,1)S(1)}, u32[]{:S(2)}, u32[]{:S(2)}) %collective-permute-start.51) | collective-permute-done | bytes 1048608 | tf_op jit(solution)/shard_map/ppermute | solution.py:80
  290.8 9.7 %collective-permute-done.60 = bf16[4,128,512]{2,1,0:T(8,128)(2,1)S(1)} collective-permute-done((bf16[4,128,512]{2,1,0:T(8,128)(2,1)S(1)}, bf16[4,128,512]{2,1,0:T(8,128)(2,1)S(1)}, u32[]{:S(2)}, u32[]{:S(2)}) %collective-permute-start.60) | collective-permute-done | bytes 524320 | tf_op jit(solution)/shard_map/ppermute | solution.py:80
  301.1 5.8 %collective-permute-start.63 = (bf16[128,1024]{1,0:T(8,128)(2,1)S(1)}, bf16[128,1024]{1,0:T(8,128)(2,1)S(1)}, u32[]{:S(2)}, u32[]{:S(2)}) collective-permute-start(bf16[128,1024]{1,0:T(8,128)(2,1)S(1)} %pad_maximum_fusion.19), channel_id=1, source_target_pairs={{0,8},{2,10},{4,12},{6,14},{8,0},{10,2},{12,4},{14,6},{16,24},{18,... | collective-permute-start | bytes 786440 | tf_op jit(solution)/shard_map/ppermute | solution.py:80
  319.1 8.7 %collective-permute-done.64 = bf16[128,1024]{1,0:T(8,128)(2,1)S(1)} collective-permute-done((bf16[128,1024]{1,0:T(8,128)(2,1)S(1)}, bf16[128,1024]{1,0:T(8,128)(2,1)S(1)}, u32[]{:S(2)}, u32[]{:S(2)}) %collective-permute-start.64) | collective-permute-done | bytes 262176 | tf_op jit(solution)/shard_map/ppermute | solution.py:80
  330.8 18.6 %collective-permute-done.56 = bf16[64,2048]{1,0:T(8,128)(2,1)S(1)} collective-permute-done((bf16[64,2048]{1,0:T(8,128)(2,1)S(1)}, bf16[64,2048]{1,0:T(8,128)(2,1)S(1)}, u32[]{:S(2)}, u32[]{:S(2)}) %collective-permute-start.56) | collective-permute-done | bytes 262176 | tf_op jit(solution)/shard_map/ppermute | solution.py:80
  360.5 14.6 %shard_map.309.refs_2_ = bf16[1024,768]{1,0:T(8,128)(2,1)} custom-call(f32[8]{0:T(128)} %multiply_power_fusion.slope_ref, s32[1,1024]{1,0:T(1,128)} %row_ref.5, s32[1024,1]{1,0:T(8,128)} %copy.114.col_ref, bf16[1024,1536]{1,0:T(8,128)(2,1)} %add_convert_fusion.qkv_ref, bf16[1024,512]{1,0:T(8,128)(2,1)} %convolution_convert_fusion.g_ref), custom_call_target="tpu_custom_call" | custom-call | tf_op jit(solution)/shard_map/pallas_call | solution.py:377
  375.2 15.0 %shard_map.310.refs_1_ = bf16[1024,768]{1,0:T(8,128)(2,1)} custom-call(f32[8]{0:T(128)} %multiply_power_fusion.slope_ref, s32[1,1024]{1,0:T(1,128)} %row_ref.5, s32[1024,1]{1,0:T(8,128)} %copy.114.col_ref, bf16[1024,1536]{1,0:T(8,128)(2,1)} %add_convert_fusion.qkv_ref, bf16[1024,512]{1,0:T(8,128)(2,1)} %convolution_convert_fusion.g_ref), custom_call_target="tpu_custom_call" | custom-call | tf_op jit(solution)/shard_map/pallas_call | solution.py:377
  394.0 7.9 %shard_map.311 = (bf16[2,2,4,64,640]{4,3,2,1,0:T(8,128)(2,1)}, bf16[2,2,4,64,640]{4,3,2,1,0:T(8,128)(2,1)}) custom-call(s32[2]{0:T(128)} %pad_add_fusion.me_ref, bf16[1024,1024]{1,0:T(8,128)(2,1)} %fusion.17.refs_0_, bf16[1024,1024]{1,0:T(8,128)(2,1)} %copy-done.10, bf16[1024,768]{1,0:T(8,128)(2,1)} %shard_map.309.refs_2_, bf16[1024,1024]{1,0:T(8,128)(2,1)} %copy-done.9), custom_call_target="tpu_custom_call" | custom-call | tf_op jit(solution)/shard_map/pallas_call | solution.py:213
  401.9 6.4 %shard_map.312 = (bf16[2,2,4,64,384]{4,3,2,1,0:T(8,128)(2,1)}, bf16[2,2,4,64,384]{4,3,2,1,0:T(8,128)(2,1)}) custom-call(s32[2]{0:T(128)} %pad_add_fusion.me_ref, bf16[1024,1024]{1,0:T(8,128)(2,1)} %fusion.17.refs_0_, bf16[1024,768]{1,0:T(8,128)(2,1)} %shard_map.310.refs_1_), custom_call_target="tpu_custom_call" | custom-call | tf_op jit(solution)/shard_map/pallas_call | solution.py:213
  409.7 6.4 %fusion.89 = f32[2,512,1024]{2,1,0:T(8,128)S(1)} fusion(bf16[2,512,1536]{2,1,0:T(8,128)(2,1)} %bitcast.468, bf16[1024,1536,1]{1,0,2:T(8,128)(2,1)} %bitcast.467), kind=kOutput, calls=%fused_computation.316 | convolution fusion | flops 3221225472 | bytes 10485760 | tf_op jit(solution)/shard_map/dot_general | solution.py:22
  429.9 4.7 fusion.34
  434.6 12.3 %collective-permute-done.43 = bf16[2,4,64,384]{3,2,1,0:T(8,128)(2,1)} collective-permute-done((bf16[2,4,64,384]{3,2,1,0:T(8,128)(2,1)}, bf16[2,4,64,384]{3,2,1,0:T(8,128)(2,1)}, u32[]{:S(2)}, u32[]{:S(2)}) %collective-permute-start.43) | collective-permute-done | bytes 393248 | tf_op jit(solution)/shard_map/ppermute | solution.py:80
  449.5 4.8 collective-permute-done.44
  455.5 5.0 collective-permute-start.47
  (454 shorter events, 221.4 us)
Async XLA Ops:
  3.7 31.1 %collective-permute-start.16 = (bf16[32,2560]{1,0:T(8,128)(2,1)}, bf16[32,2560]{1,0:T(8,128)(2,1)}, u32[]{:S(2)}, u32[]{:S(2)}) collective-permute-start(bf16[32,2560]{1,0:T(8,128)(2,1)} %get-tuple-element.119), channel_id=1, source_target_pairs={{0,1},{1,0},{2,3},{3,2},{4,5},{5,4},{6,7},{7,6},{8,9},{9,8},{10,11... | collective-permute-start | bytes 491528 | tf_op jit(solution)/shard_map/ppermute | solution.py:34
  7.8 22.5 %collective-permute-start.7 = (bf16[32,1536]{1,0:T(8,128)(2,1)S(1)}, bf16[32,1536]{1,0:T(8,128)(2,1)S(1)}, u32[]{:S(2)}, u32[]{:S(2)}) collective-permute-start(bf16[32,1536]{1,0:T(8,128)(2,1)S(1)} %get-tuple-element.145), channel_id=1, source_target_pairs={{0,1},{1,0},{2,3},{3,2},{4,5},{5,4},{6,7},{7,6},{8,9},{9,8},{10,11... | collective-permute-start | bytes 294920 | tf_op jit(solution)/shard_map/ppermute | solution.py:34
  15.7 80.6 %collective-permute-start = (bf16[512,1024]{1,0:T(8,128)(2,1)S(1)}, bf16[512,1024]{1,0:T(8,128)(2,1)S(1)}, u32[]{:S(2)}, u32[]{:S(2)}) collective-permute-start(bf16[512,1024]{1,0:T(8,128)(2,1)S(1)} %bitcast.459), channel_id=1, source_target_pairs={{0,1},{1,0},{2,3},{3,2},{4,5},{5,4},{6,7},{7,6},{8,9},{9,8},{10,11... | collective-permute-start | bytes 3145736 | tf_op jit(solution)/shard_map/ppermute | solution.py:34
  30.7 25.6 %collective-permute-start.9 = (bf16[64,1536]{1,0:T(8,128)(2,1)S(1)}, bf16[64,1536]{1,0:T(8,128)(2,1)S(1)}, u32[]{:S(2)}, u32[]{:S(2)}) collective-permute-start(bf16[64,1536]{1,0:T(8,128)(2,1)S(1)} %bitcast.483), channel_id=1, source_target_pairs={{0,16},{2,18},{4,20},{6,22},{8,24},{10,26},{12,28},{14,30},{16,0},... | collective-permute-start | bytes 589832 | tf_op jit(solution)/shard_map/ppermute | solution.py:80
  48.4 26.9 %collective-permute-start.18 = (bf16[64,2560]{1,0:T(8,128)(2,1)S(1)}, bf16[64,2560]{1,0:T(8,128)(2,1)S(1)}, u32[]{:S(2)}, u32[]{:S(2)}) collective-permute-start(bf16[64,2560]{1,0:T(8,128)(2,1)S(1)} %pad_maximum_fusion.15), channel_id=1, source_target_pairs={{0,16},{2,18},{4,20},{6,22},{8,24},{10,26},{12,28},{14,30},{16,0},... | collective-permute-start | bytes 983048 | tf_op jit(solution)/shard_map/ppermute | solution.py:80
  76.1 26.3 %collective-permute-start.22 = (bf16[4,64,1280]{2,1,0:T(8,128)(2,1)S(1)}, bf16[4,64,1280]{2,1,0:T(8,128)(2,1)S(1)}, u32[]{:S(2)}, u32[]{:S(2)}) collective-permute-start(bf16[4,64,1280]{2,1,0:T(8,128)(2,1)S(1)} %get-tuple-element.62), channel_id=1, source_target_pairs={{0,4},{2,6},{4,0},{6,2},{8,12},{10,14},{12,8},{14,10},{16,20},{18,... | collective-permute-start | bytes 1966088 | tf_op jit(solution)/shard_map/ppermute | solution.py:80
  80.0 24.3 %collective-permute-start.20 = (bf16[4,64,1280]{2,1,0:T(8,128)(2,1)S(1)}, bf16[4,64,1280]{2,1,0:T(8,128)(2,1)S(1)}, u32[]{:S(2)}, u32[]{:S(2)}) collective-permute-start(bf16[4,64,1280]{2,1,0:T(8,128)(2,1)S(1)} %get-tuple-element.64), channel_id=1, source_target_pairs={{0,2},{2,0},{4,6},{6,4},{8,10},{10,8},{12,14},{14,12},{16,18},{18,... | collective-permute-start | bytes 1966088 | tf_op jit(solution)/shard_map/ppermute | solution.py:80
  93.1 34.9 %collective-permute-start.14 = (bf16[2,4,64,768]{3,2,1,0:T(8,128)(2,1)S(1)}, bf16[2,4,64,768]{3,2,1,0:T(8,128)(2,1)S(1)}, u32[]{:S(2)}, u32[]{:S(2)}) collective-permute-start(bf16[2,4,64,768]{3,2,1,0:T(8,128)(2,1)S(1)} %pad_maximum_fusion.6.refs_2_), channel_id=1, source_target_pairs={{0,2},{2,0},{4,6},{6,4},{8,10},{10,8},{12,14},{14,12},{16,18},{18,... | collective-permute-start | bytes 2359304 | tf_op jit(solution)/shard_map/ppermute | solution.py:80
  94.5 35.5 %collective-permute-start.12 = (bf16[2,4,64,768]{3,2,1,0:T(8,128)(2,1)S(1)}, bf16[2,4,64,768]{3,2,1,0:T(8,128)(2,1)S(1)}, u32[]{:S(2)}, u32[]{:S(2)}) collective-permute-start(bf16[2,4,64,768]{3,2,1,0:T(8,128)(2,1)S(1)} %pad_maximum_fusion.5.refs_0_), channel_id=1, source_target_pairs={{0,4},{2,6},{4,0},{6,2},{8,12},{10,14},{12,8},{14,10},{16,20},{18,... | collective-permute-start | bytes 2359304 | tf_op jit(solution)/shard_map/ppermute | solution.py:80
  96.3 27.0 %collective-permute-start.30 = (bf16[4,128,512]{2,1,0:T(8,128)(2,1)S(1)}, bf16[4,128,512]{2,1,0:T(8,128)(2,1)S(1)}, u32[]{:S(2)}, u32[]{:S(2)}) collective-permute-start(bf16[4,128,512]{2,1,0:T(8,128)(2,1)S(1)} %get-tuple-element.85), channel_id=1, source_target_pairs={{0,4},{2,6},{4,0},{6,2},{8,12},{10,14},{12,8},{14,10},{16,20},{18,... | collective-permute-start | bytes 1572872 | tf_op jit(solution)/shard_map/ppermute | solution.py:80
  102.4 24.4 %collective-permute-start.28 = (bf16[4,128,512]{2,1,0:T(8,128)(2,1)S(1)}, bf16[4,128,512]{2,1,0:T(8,128)(2,1)S(1)}, u32[]{:S(2)}, u32[]{:S(2)}) collective-permute-start(bf16[4,128,512]{2,1,0:T(8,128)(2,1)S(1)} %get-tuple-element.87), channel_id=1, source_target_pairs={{0,2},{2,0},{4,6},{6,4},{8,10},{10,8},{12,14},{14,12},{16,18},{18,... | collective-permute-start | bytes 1572872 | tf_op jit(solution)/shard_map/ppermute | solution.py:80
  104.3 54.1 %collective-permute-start.23 = (bf16[2,4,64,1280]{3,2,1,0:T(8,128)(2,1)}, bf16[2,4,64,1280]{3,2,1,0:T(8,128)(2,1)}, u32[]{:S(2)}, u32[]{:S(2)}) collective-permute-start(bf16[2,4,64,1280]{3,2,1,0:T(8,128)(2,1)} %pad_maximum_fusion.2.refs_2_), channel_id=1, source_target_pairs={{0,2},{2,0},{4,6},{6,4},{8,10},{10,8},{12,14},{14,12},{16,18},{18,... | collective-permute-start | bytes 3932168 | tf_op jit(solution)/shard_map/ppermute | solution.py:80
  123.3 35.5 %collective-permute-start.21 = (bf16[2,4,64,1280]{3,2,1,0:T(8,128)(2,1)}, bf16[2,4,64,1280]{3,2,1,0:T(8,128)(2,1)}, u32[]{:S(2)}, u32[]{:S(2)}) collective-permute-start(bf16[2,4,64,1280]{3,2,1,0:T(8,128)(2,1)} %pad_maximum_fusion.1.refs_0_), channel_id=1, source_target_pairs={{0,4},{2,6},{4,0},{6,2},{8,12},{10,14},{12,8},{14,10},{16,20},{18,... | collective-permute-start | bytes 3932168 | tf_op jit(solution)/shard_map/ppermute | solution.py:80
  126.9 38.2 %collective-permute-start.33 = (bf16[512,1024]{1,0:T(8,128)(2,1)}, bf16[512,1024]{1,0:T(8,128)(2,1)}, u32[]{:S(2)}, u32[]{:S(2)}) collective-permute-start(bf16[512,1024]{1,0:T(8,128)(2,1)} %bitcast.74), channel_id=1, source_target_pairs={{0,1},{1,0},{2,3},{3,2},{4,5},{5,4},{6,7},{7,6},{8,9},{9,8},{10,11... | collective-permute-start | bytes 3145736 | tf_op jit(solution)/shard_map/ppermute | solution.py:34
  128.0 47.5 %collective-permute-start.31 = (bf16[2,4,128,512]{3,2,1,0:T(8,128)(2,1)}, bf16[2,4,128,512]{3,2,1,0:T(8,128)(2,1)}, u32[]{:S(2)}, u32[]{:S(2)}) collective-permute-start(bf16[2,4,128,512]{3,2,1,0:T(8,128)(2,1)} %pad_maximum_fusion.4.refs_2_), channel_id=1, source_target_pairs={{0,2},{2,0},{4,6},{6,4},{8,10},{10,8},{12,14},{14,12},{16,18},{18,... | collective-permute-start | bytes 3145736 | tf_op jit(solution)/shard_map/ppermute | solution.py:80
  130.9 44.6 %collective-permute-start.29 = (bf16[2,4,128,512]{3,2,1,0:T(8,128)(2,1)}, bf16[2,4,128,512]{3,2,1,0:T(8,128)(2,1)}, u32[]{:S(2)}, u32[]{:S(2)}) collective-permute-start(bf16[2,4,128,512]{3,2,1,0:T(8,128)(2,1)} %pad_maximum_fusion.3.refs_0_), channel_id=1, source_target_pairs={{0,4},{2,6},{4,0},{6,2},{8,12},{10,14},{12,8},{14,10},{16,20},{18,... | collective-permute-start | bytes 3145736 | tf_op jit(solution)/shard_map/ppermute | solution.py:80
  217.6 132.8 %collective-permute-start.34 = (bf16[1024,1024]{1,0:T(8,128)(2,1)}, bf16[1024,1024]{1,0:T(8,128)(2,1)S(1)}, u32[]{:S(2)}, u32[]{:S(2)}) collective-permute-start(bf16[1024,1024]{1,0:T(8,128)(2,1)} %get-tuple-element.179), channel_id=1, source_target_pairs={{0,1},{1,0},{2,3},{3,2},{4,5},{5,4},{6,7},{7,6},{8,9},{9,8},{10,11... | collective-permute-start | bytes 6291464 | tf_op jit(solution)/shard_map/ppermute | solution.py:34
  237.9 26.1 %collective-permute-start.59 = (bf16[2,4,128,512]{3,2,1,0:T(8,128)(2,1)S(1)}, bf16[2,4,128,512]{3,2,1,0:T(8,128)(2,1)S(1)}, u32[]{:S(2)}, u32[]{:S(2)}) collective-permute-start(bf16[2,4,128,512]{3,2,1,0:T(8,128)(2,1)S(1)} %slice_bitcast_fusion.1), channel_id=1, source_target_pairs={{0,4},{2,6},{4,0},{6,2},{8,12},{10,14},{12,8},{14,10},{16,20},{18,... | collective-permute-start | bytes 3145736 | tf_op jit(solution)/shard_map/ppermute | solution.py:80
  240.7 26.1 %collective-permute-start.61 = (bf16[2,4,128,512]{3,2,1,0:T(8,128)(2,1)S(1)}, bf16[2,4,128,512]{3,2,1,0:T(8,128)(2,1)S(1)}, u32[]{:S(2)}, u32[]{:S(2)}) collective-permute-start(bf16[2,4,128,512]{3,2,1,0:T(8,128)(2,1)S(1)} %slice_bitcast_fusion), channel_id=1, source_target_pairs={{0,2},{2,0},{4,6},{6,4},{8,10},{10,8},{12,14},{14,12},{16,18},{18,... | collective-permute-start | bytes 3145736 | tf_op jit(solution)/shard_map/ppermute | solution.py:80
  243.8 42.6 %collective-permute-start.51 = (bf16[2,4,64,1024]{3,2,1,0:T(8,128)(2,1)S(1)}, bf16[2,4,64,1024]{3,2,1,0:T(8,128)(2,1)S(1)}, u32[]{:S(2)}, u32[]{:S(2)}) collective-permute-start(bf16[2,4,64,1024]{3,2,1,0:T(8,128)(2,1)S(1)} %slice_bitcast_fusion.3), channel_id=1, source_target_pairs={{0,4},{2,6},{4,0},{6,2},{8,12},{10,14},{12,8},{14,10},{16,20},{18,... | collective-permute-start | bytes 3145736 | tf_op jit(solution)/shard_map/ppermute | solution.py:80
  246.5 42.8 %collective-permute-start.53 = (bf16[2,4,64,1024]{3,2,1,0:T(8,128)(2,1)S(1)}, bf16[2,4,64,1024]{3,2,1,0:T(8,128)(2,1)S(1)}, u32[]{:S(2)}, u32[]{:S(2)}) collective-permute-start(bf16[2,4,64,1024]{3,2,1,0:T(8,128)(2,1)S(1)} %slice_bitcast_fusion.2), channel_id=1, source_target_pairs={{0,2},{2,0},{4,6},{6,4},{8,10},{10,8},{12,14},{14,12},{16,18},{18,... | collective-permute-start | bytes 3145736 | tf_op jit(solution)/shard_map/ppermute | solution.py:80
  264.1 36.4 %collective-permute-start.60 = (bf16[4,128,512]{2,1,0:T(8,128)(2,1)S(1)}, bf16[4,128,512]{2,1,0:T(8,128)(2,1)S(1)}, u32[]{:S(2)}, u32[]{:S(2)}) collective-permute-start(bf16[4,128,512]{2,1,0:T(8,128)(2,1)S(1)} %fusion.37), channel_id=1, source_target_pairs={{0,2},{2,0},{4,6},{6,4},{8,10},{10,8},{12,14},{14,12},{16,18},{18,... | collective-permute-start | bytes 1572872 | tf_op jit(solution)/shard_map/ppermute | solution.py:80
  267.0 33.8 %collective-permute-start.62 = (bf16[4,128,512]{2,1,0:T(8,128)(2,1)S(1)}, bf16[4,128,512]{2,1,0:T(8,128)(2,1)S(1)}, u32[]{:S(2)}, u32[]{:S(2)}) collective-permute-start(bf16[4,128,512]{2,1,0:T(8,128)(2,1)S(1)} %fusion.35), channel_id=1, source_target_pairs={{0,4},{2,6},{4,0},{6,2},{8,12},{10,14},{12,8},{14,10},{16,20},{18,... | collective-permute-start | bytes 1572872 | tf_op jit(solution)/shard_map/ppermute | solution.py:80
  286.6 24.4 %collective-permute-start.52 = (bf16[4,64,1024]{2,1,0:T(8,128)(2,1)S(1)}, bf16[4,64,1024]{2,1,0:T(8,128)(2,1)S(1)}, u32[]{:S(2)}, u32[]{:S(2)}) collective-permute-start(bf16[4,64,1024]{2,1,0:T(8,128)(2,1)S(1)} %fusion.41), channel_id=1, source_target_pairs={{0,2},{2,0},{4,6},{6,4},{8,10},{10,8},{12,14},{14,12},{16,18},{18,... | collective-permute-start | bytes 1572872 | tf_op jit(solution)/shard_map/ppermute | solution.py:80
  289.5 23.7 %collective-permute-start.54 = (bf16[4,64,1024]{2,1,0:T(8,128)(2,1)S(1)}, bf16[4,64,1024]{2,1,0:T(8,128)(2,1)S(1)}, u32[]{:S(2)}, u32[]{:S(2)}) collective-permute-start(bf16[4,64,1024]{2,1,0:T(8,128)(2,1)S(1)} %fusion.39), channel_id=1, source_target_pairs={{0,4},{2,6},{4,0},{6,2},{8,12},{10,14},{12,8},{14,10},{16,20},{18,... | collective-permute-start | bytes 1572872 | tf_op jit(solution)/shard_map/ppermute | solution.py:80
  317.5 31.9 %collective-permute-start.56 = (bf16[64,2048]{1,0:T(8,128)(2,1)S(1)}, bf16[64,2048]{1,0:T(8,128)(2,1)S(1)}, u32[]{:S(2)}, u32[]{:S(2)}) collective-permute-start(bf16[64,2048]{1,0:T(8,128)(2,1)S(1)} %pad_maximum_fusion.17), channel_id=1, source_target_pairs={{0,16},{2,18},{4,20},{6,22},{8,24},{10,26},{12,28},{14,30},{16,0},... | collective-permute-start | bytes 786440 | tf_op jit(solution)/shard_map/ppermute | solution.py:80
  329.4 98.6 %collective-permute-start.32 = (f32[512,1024]{1,0:T(8,128)}, f32[512,1024]{1,0:T(8,128)}, u32[]{:S(2)}, u32[]{:S(2)}) collective-permute-start(f32[512,1024]{1,0:T(8,128)} %dynamic-slice_bitcast_fusion), channel_id=1, source_target_pairs={{0,1},{1,0},{2,3},{3,2},{4,5},{5,4},{6,7},{7,6},{8,9},{9,8},{10,11... | collective-permute-start | bytes 6291464 | tf_op jit(solution)/shard_map/ppermute | solution.py:34
  418.2 60.8 %collective-permute-start.35 = (bf16[512,1024]{1,0:T(8,128)(2,1)S(1)}, bf16[512,1024]{1,0:T(8,128)(2,1)}, u32[]{:S(2)}, u32[]{:S(2)}) collective-permute-start(bf16[512,1024]{1,0:T(8,128)(2,1)S(1)} %fusion.33), channel_id=1, source_target_pairs={{0,1},{1,0},{2,3},{3,2},{4,5},{5,4},{6,7},{7,6},{8,9},{9,8},{10,11... | collective-permute-start | bytes 3145736 | tf_op jit(solution)/shard_map/ppermute | solution.py:34
  421.0 39.6 %collective-permute-start.36 = (bf16[2,4,64,640]{3,2,1,0:T(8,128)(2,1)}, bf16[2,4,64,640]{3,2,1,0:T(8,128)(2,1)}, u32[]{:S(2)}, u32[]{:S(2)}) collective-permute-start(bf16[2,4,64,640]{3,2,1,0:T(8,128)(2,1)} %slice_bitcast_fusion.5), channel_id=1, source_target_pairs={{0,4},{2,6},{4,0},{6,2},{8,12},{10,14},{12,8},{14,10},{16,20},{18,... | collective-permute-start | bytes 1966088 | tf_op jit(solution)/shard_map/ppermute | solution.py:80
  423.1 41.0 %collective-permute-start.38 = (bf16[2,4,64,640]{3,2,1,0:T(8,128)(2,1)}, bf16[2,4,64,640]{3,2,1,0:T(8,128)(2,1)}, u32[]{:S(2)}, u32[]{:S(2)}) collective-permute-start(bf16[2,4,64,640]{3,2,1,0:T(8,128)(2,1)} %slice_bitcast_fusion.4), channel_id=1, source_target_pairs={{0,2},{2,0},{4,6},{6,4},{8,10},{10,8},{12,14},{14,12},{16,18},{18,... | collective-permute-start | bytes 1966088 | tf_op jit(solution)/shard_map/ppermute | solution.py:80
  476.3 30.3 %collective-permute-start.40 = (bf16[64,1280]{1,0:T(8,128)(2,1)}, bf16[64,1280]{1,0:T(8,128)(2,1)}, u32[]{:S(2)}, u32[]{:S(2)}) collective-permute-start(bf16[64,1280]{1,0:T(8,128)(2,1)} %pad_maximum_fusion.22), channel_id=1, source_target_pairs={{0,8},{2,10},{4,12},{6,14},{8,0},{10,2},{12,4},{14,6},{16,24},{18,... | collective-permute-start | bytes 491528 | tf_op jit(solution)/shard_map/ppermute | solution.py:80
  477.8 28.8 %collective-permute-start.41 = (bf16[64,1280]{1,0:T(8,128)(2,1)}, bf16[64,1280]{1,0:T(8,128)(2,1)}, u32[]{:S(2)}, u32[]{:S(2)}) collective-permute-start(bf16[64,1280]{1,0:T(8,128)(2,1)} %pad_maximum_fusion.23), channel_id=1, source_target_pairs={{0,16},{2,18},{4,20},{6,22},{8,24},{10,26},{12,28},{14,30},{16,0},... | collective-permute-start | bytes 491528 | tf_op jit(solution)/shard_map/ppermute | solution.py:80
  (98 other events, 2448.1 us)

commit v2 on v1

v2 whole, which is shorter than its diff:
```python
import functools

import jax
import jax.numpy as jnp
from jax import lax
from jax.experimental import pallas as pl
from jax.experimental.pallas import tpu as pltpu
from jax.sharding import PartitionSpec as P


HEADS = 16
HEAD_DIM = 64
EPS = 1e-05
FAR = 1e30
BLOCK = 256
REACH = 512
BF = jnp.bfloat16
F32 = jnp.float32


def dot(left, right, contract):
    return lax.dot_general(left, right, (contract, ((), ())), preferred_element_type=F32)


def matmul(left, right):
    return dot(left, right, ((1,), (0,)))


def pick(array, index, axis):
    return lax.dynamic_index_in_dim(array, index, axis, keepdims=False)


def trade(array):
    return lax.ppermute(array, "seq", [(0, 1), (1, 0)])


def seq_gather(block, seq):
    if seq == 2:
        other = trade(block)
        first = lax.axis_index("seq") == 0
        return jnp.where(first, jnp.stack([block, other]), jnp.stack([other, block]))
    return lax.all_gather(block, "seq", axis=0)


def seq_swap(blocks, seq):
    if seq == 2:
        me = lax.axis_index("seq")
        own, other = pick(blocks, me, 0), trade(pick(blocks, 1 - me, 0))
        return jnp.where(me == 0, jnp.stack([own, other]), jnp.stack([other, own]))
    return lax.all_to_all(blocks, "seq", 0, 0)


def seq_reduce(blocks, seq, send):
    if seq == 2:
        me = lax.axis_index("seq")
        other = trade(pick(blocks, 1 - me, 0).astype(send))
        return pick(blocks, me, 0).astype(F32) + other.astype(F32)
    return lax.psum_scatter(blocks.astype(F32), "seq", scatter_dimension=0, tiled=False)


def flip(array, bits, count):
    return lax.ppermute(array, "dp", [(i, i ^ bits) for i in range(count)])


def boxed(count):
    return count >= 4 and not count & (count - 1)


def vmem_specs(count):
    return [pl.BlockSpec(memory_space=pltpu.VMEM)] * count


def split_kernel(me_ref, *refs):
    weights, up_ref, targets = refs[:4], refs[4], refs[5:]
    me, cols = me_ref[0], targets[0].shape[1] // 4
    tile = PAIR
    for away in range(2):
        first_ref, up_out = targets[away], targets[2 + away]
        base, start = (me ^ away) * cols, 0
        for colour in range(2):
            for at in range(colour * cols // 2, (colour + 1) * cols // 2, PAIR):
                for weight in weights[:3]:
                    column = pl.multiple_of(base + at, PAIR)
                    first_ref[:, start : start + PAIR] = weight[:, pl.ds(column, PAIR)]
                    start += PAIR
            column = pl.multiple_of(base + colour * (cols // 2), cols // 2)
            first_ref[:, start : start + cols // 2] = weights[3][:, pl.ds(column, cols // 2)]
            start += cols // 2
        for at in range(0, up_out.shape[1], tile):
            column = pl.multiple_of(2 * at + (me ^ away) * tile, tile)
            up_out[:, at : at + tile] = up_ref[:, pl.ds(column, tile)]


def split_weights(me, weights, up_weight):
    rows, width = weights[0].shape
    shapes = [(rows, 2 * width)] * 2 + [(rows, up_weight.shape[1] // 2)] * 2
    return pl.pallas_call(
        split_kernel,
        in_specs=[pl.BlockSpec(memory_space=pltpu.SMEM)] + vmem_specs(5),
        out_specs=vmem_specs(4),
        out_shape=[jax.ShapeDtypeStruct(shape, BF) for shape in shapes],
    )(me.astype(jnp.int32)[None], *weights, up_weight)


def two_rows(own, other, me):
    return jnp.where(
        me == 0, jnp.concatenate([own, other], axis=0), jnp.concatenate([other, own], axis=0)
    )


def pack_kernel(*refs):
    slots, outs = refs[:-2], refs[-2:]
    half = outs[0].shape[2]
    for k, slot in enumerate(slots):
        for colour in range(2):
            outs[colour][k] = slot[:, colour * half : (colour + 1) * half]


def put_pieces(me, pieces, targets):
    low, side, far = me % 2, (me // 2) % 2, me // 4
    n_far, rows, _ = pieces[0].shape
    for colour in range(2):
        for late in range(2):
            for early in range(2):
                piece = pieces[4 * colour + 2 * late + early]
                away = (early, late) if colour == 0 else (late, early)
                for k in range(n_far):
                    block = (far ^ k) * 4 + (side ^ away[1]) * 2 + (low ^ away[0])
                    at = pl.multiple_of(block * rows, rows)
                    start = 0
                    for ref, column, width in targets:
                        half = width // 2
                        first = column + colour * half
                        ref[pl.ds(at, rows), first : first + half] = piece[k, :, start : start + half]
                        start += half


def whole_spec(array):
    return pl.BlockSpec(array.shape, lambda i, *_: (0,) * array.ndim)


def gather_blocks(block, widths, count, after=None):
    rows, half = block.shape[0], block.shape[1] // 2
    if not boxed(count) or any(w % 256 for w in widths):
        whole = lax.all_gather(block, "dp", axis=0, tiled=True)
        starts = [sum(widths[:i]) // 2 for i in range(len(widths))]
        return [
            jnp.concatenate(
                [whole[:, at : at + w // 2], whole[:, half + at : half + at + w // 2]], axis=1
            )
            for at, w in zip(starts, widths)
        ], block
    n_far = count // 4
    if after is not None:
        block, _ = lax.optimization_barrier((block, after))
    slots = [block] + [flip(block, 4 * k, count) for k in range(1, n_far)]
    fars = pl.pallas_call(
        pack_kernel,
        in_specs=vmem_specs(n_far),
        out_specs=vmem_specs(2),
        out_shape=[jax.ShapeDtypeStruct((n_far, rows, half), block.dtype)] * 2,
    )(*slots)
    pieces = []
    for colour, far in enumerate(fars):
        first, second = (1, 2) if colour == 0 else (2, 1)
        got = flip(far, first, count)
        pieces += [far, got, flip(far, second, count)]
        pieces += [flip(got, second, count)]
    return pieces, slots[-1]


def gather_small(block, count):
    if not boxed(count):
        return lax.all_gather(block, "dp", axis=0)
    near = jnp.stack([block, flip(block, 1, count)])
    near = jnp.stack([near, flip(near, 2, count)])
    whole = jnp.stack([near] + [flip(near, 4 * k, count) for k in range(1, count // 4)]).reshape((count,) + block.shape)
    ids = jnp.arange(count)
    order = ((ids[:, None] ^ lax.axis_index("dp")) == ids[None, :]).astype(F32)
    return jnp.sum(order.reshape(count, count, 1, 1) * whole[None], axis=1)


def add_low(a, b):
    return (a.astype(F32) + b.astype(F32)).astype(b.dtype)


def scatter_near(grads, count, colour):
    me = lax.axis_index("dp")
    side, low = (me // 2) % 2, me % 2
    box = grads.reshape((count // 4, 2, 2) + grads.shape[1:])
    if colour == 0:
        order = ((1, 2, side), (1, 1, low))
    else:
        order = ((2, 1, low), (1, 2, side))
    for axis, bit, mine in order:
        got = flip(pick(box, 1 - mine, axis), bit, count)
        box = add_low(pick(box, mine, axis), got)
    return box


def scatter_far(box, count):
    far = lax.axis_index("dp") // 4
    total = pick(box, far, 0).astype(F32)
    for k in range(1, count // 4):
        total = total + flip(pick(box, far ^ k, 0), 4 * k, count).astype(F32)
    return total


def grad_kernel(widths, ways, me_ref, *refs):
    n = len(widths)
    lefts, rights, outs, scratch = refs[:n], refs[n : 2 * n], refs[2 * n : -1], refs[-1]
    low, side = me_ref[0] % 2, (me_ref[0] // 2) % 2
    rows, start = scratch.shape[1] // 4, 0
    for left, right, width in zip(lefts, rights, widths):
        for away in range(2):
            at = pl.multiple_of((side ^ away) * 2 * rows, 2 * rows)
            if rows % 128:
                part = left[:, pl.ds(at, 2 * rows)]
                turned = jnp.concatenate([part[:, rows:], part[:, :rows]], axis=1)
                scratch[:, 2 * away * rows : 2 * (away + 1) * rows] = jnp.where(low == 0, part, turned)
            else:
                for step in range(2):
                    at_low = pl.multiple_of(at + (low ^ step) * rows, rows)
                    scratch[:, (2 * away + step) * rows : (2 * away + step + 1) * rows] = left[
                        :, pl.ds(at_low, rows)
                    ]
        grads = dot(scratch[...], right[...], ((0,), (0,)))
        for side_away in range(2):
            for low_away in range(2):
                at = (2 * side_away + low_away) * rows
                for way, (colour, low_column, high_column) in enumerate(ways):
                    first, second = (side_away, low_away) if colour == 0 else (low_away, side_away)
                    lo, hi = max(start, low_column), min(start + width, high_column)
                    outs[2 * way + first][second, 0, :, lo - low_column : hi - low_column] = grads[
                        at : at + rows, lo - start : hi - start
                    ].astype(BF)
        start += width


def grad_blocks(lefts, rights, widths, column, count, ways):
    length, n_far = lefts[0].shape[0], count // 4
    depth = lefts[0].shape[1] // n_far
    shapes = [(2, n_far, depth // 4, high - low) for _, low, high in ways for _ in range(2)]
    in_specs = [pl.BlockSpec((length, depth), lambda k, me: (0, (me[0] // 4) ^ k)) for _ in lefts]
    in_specs += [pl.BlockSpec((length, w), lambda k, me: (0, 0)) for w in widths]
    if column:
        in_specs[-1] = pl.BlockSpec((length, widths[-1]), lambda k, me: (0, me[1]))
    me = [lax.axis_index("dp").astype(jnp.int32), lax.axis_index("seq").astype(jnp.int32)]
    return pl.pallas_call(
        functools.partial(grad_kernel, widths, ways),
        grid_spec=pltpu.PrefetchScalarGridSpec(
            num_scalar_prefetch=1,
            grid=(n_far,),
            in_specs=in_specs,
            out_specs=[
                pl.BlockSpec((2, 1) + shape[2:], lambda k, me: (0, k, 0, 0)) for shape in shapes
            ],
            scratch_shapes=[pltpu.VMEM((length, depth), BF)],
        ),
        out_shape=[jax.ShapeDtypeStruct(shape, BF) for shape in shapes],
    )(jnp.stack(me), *lefts, *rights)


def scatter_grads(lefts, rights, count, colours, column=0):
    widths = [r.shape[1] for r in rights]
    if column:
        widths[-1] = column
    if not boxed(count) or any(w % 128 for w in widths) or any(a.shape[1] % (64 * count) for a in lefts):
        if column:
            last = lax.dynamic_slice_in_dim(
                rights[-1], lax.axis_index("seq") * column, column, 1
            )
            rights = rights[:-1] + [last]
        return [
            lax.psum_scatter(dot(a, b, ((0,), (0,))), "dp", scatter_dimension=0, tiled=True)
            for a, b in zip(lefts, rights)
        ]
    step = sum(widths) // len(colours)
    ways = [(colour, i * step, (i + 1) * step) for i, colour in enumerate(colours)]
    grads = grad_blocks(lefts, rights, widths, column, count, ways)
    ends = []
    for way, colour in enumerate(colours):
        keep, give = grads[2 * way : 2 * way + 2]
        first, second = (2, 1) if colour == 0 else (1, 2)
        got = flip(give, first, count)
        late = flip(add_low(keep[1], got[1]), second, count)
        ends.append((add_low(keep[0], got[0]), late))
    total = jnp.concatenate([k[0].astype(F32) + l[0].astype(F32) for k, l in ends], axis=1)
    for k in range(1, count // 4):
        part = jnp.concatenate([add_low(keep[k], late[k]) for keep, late in ends], axis=1)
        total = total + flip(part, 4 * k, count).astype(F32)
    sums, start = [], 0
    for width in widths:
        sums.append(total[:, start : start + width])
        start += width
    return sums


PAIR = 2 * HEAD_DIM


def window(block):
    return max(0, block - REACH // BLOCK) * BLOCK, (block + 1) * BLOCK


def distances(row_ref, col_ref, block, out_ref):
    start, stop = window(block)
    shape = (stop - start, BLOCK)
    key = lax.broadcasted_iota(jnp.int32, shape, 0) + start
    query = lax.broadcasted_iota(jnp.int32, shape, 1) + block * BLOCK
    same = col_ref[start:stop, :] == row_ref[:, block * BLOCK : (block + 1) * BLOCK]
    out_ref[...] = jnp.where((query >= key) & same, (query - key).astype(F32), FAR)


def all_distances(row_ref, col_ref, n_blocks, near_refs, far_ref):
    @pl.when(pl.program_id(0) == 0)
    def _():
        for block in range(n_blocks):
            wide = block - REACH // BLOCK
            target = far_ref.at[wide] if wide >= 0 else near_refs[block]
            distances(row_ref, col_ref, block, target)


def each_block(n_blocks, near_refs, far_ref, work):
    back = REACH // BLOCK
    for block in range(back):
        start, stop = window(block)
        work(block * BLOCK, start, stop - start, near_refs[block])

    for block in range(back, n_blocks):
        work(block * BLOCK, block * BLOCK - REACH, REACH + BLOCK, far_ref.at[block - back])


def chances_of(query, key, far, slope):
    scores = dot(key, query, ((1,), (1,))) - slope * far
    top = jnp.max(scores, axis=0, keepdims=True)
    grown = jnp.exp(scores - top)
    return grown * (1.0 / jnp.sum(grown, axis=0, keepdims=True))


def attend_kernel(n_blocks, first_ref, slope_ref, row_ref, col_ref, qkv_ref, o_ref, far_ref, *near_refs):
    pair = pl.program_id(0) + first_ref[0]
    all_distances(row_ref, col_ref, n_blocks, near_refs, far_ref)
    left = lax.broadcasted_iota(jnp.int32, (BLOCK, PAIR), 1) < HEAD_DIM

    def work(at, start, keys, distance_ref):
        rows, cols = pl.ds(at, BLOCK), pl.ds(start, keys)
        query = qkv_ref[rows, :PAIR] * BF(HEAD_DIM**-0.5)
        key, value = qkv_ref[cols, PAIR : 2 * PAIR], qkv_ref[cols, 2 * PAIR :]
        parts = []
        for side in range(2):
            mine = jnp.where(left if side == 0 else ~left, query, 0)
            share = chances_of(mine, key, distance_ref[...], slope_ref[2 * pair + side]).astype(BF)
            parts.append(dot(share, value, ((0,), (0,))))
        o_ref[rows, :] = jnp.where(left, parts[0], parts[1]).astype(BF)

    each_block(n_blocks, near_refs, far_ref, work)


def attend_back_kernel(
    n_blocks, first_ref, slope_ref, row_ref, col_ref, qkv_ref, g_ref, d_ref, k_sum, v_sum, far_ref, *near_refs
):
    pair = pl.program_id(0) + first_ref[0]
    all_distances(row_ref, col_ref, n_blocks, near_refs, far_ref)
    left = lax.broadcasted_iota(jnp.int32, (BLOCK, PAIR), 1) < HEAD_DIM
    scale = HEAD_DIM**-0.5

    def work(at, start, keys, distance_ref):
        rows, cols = pl.ds(at, BLOCK), pl.ds(start, keys)
        wide = lax.broadcasted_iota(jnp.int32, (keys, PAIR), 1) < HEAD_DIM
        query = qkv_ref[rows, :PAIR] * BF(scale)
        grad = g_ref[rows, :]
        key, value = qkv_ref[cols, PAIR : 2 * PAIR], qkv_ref[cols, 2 * PAIR :]
        dq, dk, dv = [], [], []
        for side in range(2):
            keep = left if side == 0 else ~left
            chances = chances_of(
                jnp.where(keep, query, 0), key, distance_ref[...], slope_ref[2 * pair + side]
            )
            g_chances = dot(value, jnp.where(keep, grad, 0), ((1,), (1,)))
            product = chances * g_chances
            inner = jnp.sum(product, axis=0, keepdims=True)
            g_scores = (product - chances * inner).astype(BF)
            dv.append(matmul(chances.astype(BF), grad))
            dk.append(matmul(g_scores, query))
            dq.append(dot(g_scores, key, ((0,), (0,))))
        d_ref[rows, :PAIR] = (jnp.where(left, dq[0], dq[1]) * scale).astype(BF)
        dk, dv = jnp.where(wide, dk[0], dk[1]), jnp.where(wide, dv[0], dv[1])
        old = keys - BLOCK
        if old:
            k_sum[pl.ds(start, old), :] += dk[:old]
            v_sum[pl.ds(start, old), :] += dv[:old]
        k_sum[rows, :] = dk[old:]
        v_sum[rows, :] = dv[old:]

    each_block(n_blocks, near_refs, far_ref, work)
    d_ref[:, PAIR : 2 * PAIR] = k_sum[...].astype(BF)
    d_ref[:, 2 * PAIR :] = v_sum[...].astype(BF)


def distance_scratch(length):
    back = REACH // BLOCK
    near = [pltpu.VMEM((window(block)[1] - window(block)[0], BLOCK), F32) for block in range(back)]
    return [pltpu.VMEM((length // BLOCK - back, REACH + BLOCK, BLOCK), F32)] + near


def attend_call(kernel, slopes, row, col, arrays, widths, out_width, sums, pairs):
    length = row.shape[1]
    in_specs = [
        pl.BlockSpec(memory_space=pltpu.SMEM),
        pl.BlockSpec((1, length), lambda p, first: (0, 0)),
        pl.BlockSpec((length, 1), lambda p, first: (0, 0)),
    ] + [pl.BlockSpec((length, w), lambda p, first: (0, p + first[0])) for w in widths]
    return pl.pallas_call(
        functools.partial(kernel, length // BLOCK),
        grid_spec=pltpu.PrefetchScalarGridSpec(
            num_scalar_prefetch=1,
            grid=(len(pairs),),
            in_specs=in_specs,
            out_specs=pl.BlockSpec((length, out_width), lambda p, first: (0, p)),
            scratch_shapes=[pltpu.VMEM((length, PAIR), F32)] * sums + distance_scratch(length),
        ),
        out_shape=jax.ShapeDtypeStruct((length, len(pairs) * out_width), BF),
    )(jnp.full((1,), pairs[0], jnp.int32), slopes, row, col, *arrays)


def attend(slopes, row, col, qkv, pairs):
    return attend_call(attend_kernel, slopes, row, col, [qkv], [3 * PAIR], PAIR, 0, pairs)


def attend_back(slopes, row, col, qkv, grads, pairs):
    return attend_call(attend_back_kernel, slopes, row, col, [qkv, grads], [3 * PAIR, PAIR], 3 * PAIR, 2, pairs)


def normed(matrix):
    centred = matrix - jnp.mean(matrix, axis=-1, keepdims=True)
    spread = jnp.mean(centred * centred, axis=-1, keepdims=True)
    inverse = lax.rsqrt(spread + EPS)
    return centred * inverse, inverse


def norm_back(grad, gain, unit, inverse):
    scaled = grad * gain
    return inverse * (
        scaled
        - jnp.mean(scaled, axis=-1, keepdims=True)
        - unit * jnp.mean(scaled * unit, axis=-1, keepdims=True)
    )


def gelu_and_slope(u):
    c = 0.7978845608
    square = u * u
    t = jnp.tanh(u * (c + (c * 0.044715) * square))
    half = 0.5 + 0.5 * t
    slope = half + (u - u * (t * t)) * (0.5 * c + (1.5 * c * 0.044715) * square)
    return u * half, slope


ROWS = 256
COLS = 512


def middle_kernel(n, me_ref, *refs):
    mixed_parts, weights = refs[:n], refs[n : 2 * n]
    x_ref, shift_ref, gain_ref, bias_ref, mixed_ref, middle_ref, low_ref = refs[2 * n :]
    for i in range(n):
        width = mixed_parts[i].shape[1]
        at = pl.multiple_of(me_ref[1 + i] * width, width)
        mixed_ref[:, pl.ds(at, width)] = mixed_parts[i][...]
    mixed = mixed_ref[...]
    for i in range(n):
        width = weights[i].shape[1]
        at = pl.multiple_of(me_ref[1 + i] * width, width)
        middle_ref[:, pl.ds(at, width)] = matmul(mixed, weights[i][...])
    middle = x_ref[...].astype(F32) + middle_ref[...] + shift_ref[...]
    middle_ref[...] = middle
    unit, _ = normed(middle)
    low_ref[...] = (unit * gain_ref[...] + bias_ref[...]).astype(BF)


def middle_of(me, mixed_parts, weights, inputs, shift, gain, bias):
    n, (length, width) = len(weights), inputs.shape
    rows = lambda w: pl.BlockSpec((ROWS, w), lambda i, me: (i, 0))
    whole = lambda r, w: pl.BlockSpec((r, w), lambda i, me: (0, 0))
    return pl.pallas_call(
        functools.partial(middle_kernel, n),
        grid_spec=pltpu.PrefetchScalarGridSpec(
            num_scalar_prefetch=1,
            grid=(length // ROWS,),
            in_specs=[rows(p.shape[1]) for p in mixed_parts]
            + [whole(*w.shape) for w in weights]
            + [rows(width)]
            + [whole(1, width)] * 3,
            out_specs=[rows(width)] * 3,
        ),
        out_shape=[jax.ShapeDtypeStruct((length, width), t) for t in (BF, F32, BF)],
    )(me, *mixed_parts, *weights, inputs, shift[None], gain[None], bias[None])


def qkv_kernel(me_ref, *refs):
    pieces, (low_ref, bias_ref, qkv_ref, full_ref, out_ref, scratch) = refs[:8], refs[8:]
    step = pl.program_id(0)
    width = scratch.shape[1]

    @pl.when(step == 0)
    def _():
        put_pieces(me_ref[0], pieces, [(scratch, 0, width), (out_ref, 0, out_ref.shape[1])])

    cols = qkv_ref.shape[1]
    weight = scratch[:, pl.ds(pl.multiple_of(step * cols, cols), cols)]
    full_ref[...] = weight
    qkv_ref[...] = (matmul(low_ref[...], weight) + bias_ref[...]).astype(BF)


def qkv_of(me, pieces, first_low, bias, head_cols):
    if len(pieces) == 2:
        return (matmul(first_low, pieces[0]) + bias).astype(BF), *pieces
    length, width = first_low.shape
    cols = pl.BlockSpec((length, head_cols), lambda i, me: (0, i))
    full = pl.BlockSpec((width, head_cols), lambda i, me: (0, i))
    return pl.pallas_call(
        qkv_kernel,
        grid_spec=pltpu.PrefetchScalarGridSpec(
            num_scalar_prefetch=1,
            grid=(3,),
            in_specs=[whole_spec(p) for p in pieces]
            + [whole_spec(first_low), pl.BlockSpec((1, head_cols), lambda i, me: (0, i))],
            out_specs=[cols, full, pl.BlockSpec((width, head_cols), lambda i, me: (0, 0))],
            scratch_shapes=[pltpu.VMEM((width, 3 * head_cols), BF)],
        ),
        out_shape=[
            jax.ShapeDtypeStruct((length, 3 * head_cols), BF),
            jax.ShapeDtypeStruct((width, 3 * head_cols), BF),
            jax.ShapeDtypeStruct((width, head_cols), BF),
        ],
    )(me, *pieces, first_low, bias[None])


def up_kernel(me_ref, *refs):
    pieces, (low_ref, bias_ref, act_ref, slope_ref, full_ref, scratch) = refs[:8], refs[8:]
    step = pl.program_id(0)

    @pl.when(step == 0)
    def _():
        put_pieces(me_ref[0], pieces, [(scratch, 0, scratch.shape[1])])

    cols = act_ref.shape[1]
    weight = scratch[:, pl.ds(pl.multiple_of(step * cols, cols), cols)]
    full_ref[...] = weight
    for at in range(0, act_ref.shape[0], ROWS):
        rows = slice(at, at + ROWS)
        act, slope = gelu_and_slope(matmul(low_ref[rows, :], weight) + bias_ref[...])
        act_ref[rows, :] = act.astype(BF)
        slope_ref[rows, :] = slope.astype(BF)


def up_of(me, pieces, second_low, bias):
    if len(pieces) == 1:
        act, slope = gelu_and_slope(matmul(second_low, pieces[0]) + bias)
        return act.astype(BF), slope.astype(BF), pieces[0]
    length, width = second_low.shape
    hidden = bias.shape[0]
    cols = pl.BlockSpec((length, COLS), lambda i, me: (0, i))
    return pl.pallas_call(
        up_kernel,
        grid_spec=pltpu.PrefetchScalarGridSpec(
            num_scalar_prefetch=1,
            grid=(hidden // COLS,),
            in_specs=[whole_spec(p) for p in pieces]
            + [whole_spec(second_low), pl.BlockSpec((1, COLS), lambda i, me: (0, i))],
            out_specs=[cols, cols, pl.BlockSpec((width, COLS), lambda i, me: (0, i))],
            scratch_shapes=[pltpu.VMEM((width, hidden), BF)],
        ),
        out_shape=[
            jax.ShapeDtypeStruct((length, hidden), BF),
            jax.ShapeDtypeStruct((length, hidden), BF),
            jax.ShapeDtypeStruct((width, hidden), BF),
        ],
    )(me, *pieces, second_low, bias[None])


def back_kernel(n_steps, me_ref, *refs):
    pieces, refs = refs[:8], refs[8:]
    dy_ref, slope_ref, up_ref, hidden_ref, sum_ref, full_ref, z_ref, scratch, held = refs
    step = pl.program_id(0)

    @pl.when(step == 0)
    def _():
        put_pieces(me_ref[0], pieces, [(scratch, 0, scratch.shape[1])])

    cols = hidden_ref.shape[1]

    @pl.when(step < n_steps)
    def _():
        at = pl.multiple_of(step * cols, cols)
        weight = scratch[pl.ds(at, cols), :]
        full_ref[...] = weight
        total = None
        for start in range(0, dy_ref.shape[0], ROWS):
            rows = slice(start, start + ROWS)
            g_act = dot(dy_ref[rows, :], weight, ((1,), (1,)))
            g_hidden = (g_act * slope_ref[rows, :].astype(F32)).astype(BF)
            hidden_ref[rows, :] = g_hidden
            held[rows, pl.ds(at, cols)] = g_hidden
            part = jnp.sum(g_hidden.astype(F32), axis=0, keepdims=True)
            total = part if total is None else total + part
        sum_ref[...] = total

    @pl.when(step >= n_steps)
    def _():
        z_ref[...] = dot(held[...], up_ref[...], ((1,), (1,))).astype(BF)


def back_of(me, pieces, grad_output, slope, up_full):
    length, width = grad_output.shape
    hidden = slope.shape[1]
    if len(pieces) == 1:
        g_hidden = (dot(grad_output, pieces[0], ((1,), (1,))) * slope.astype(F32)).astype(BF)
        z = dot(g_hidden, up_full, ((1,), (1,))).astype(BF)
        return g_hidden, jnp.sum(g_hidden.astype(F32), axis=0), pieces[0], z
    n_steps, n_late = hidden // COLS, width // ROWS
    early = lambda i: jnp.minimum(i, n_steps - 1)
    late = lambda i: jnp.maximum(i - n_steps, 0)
    cols = pl.BlockSpec((length, COLS), lambda i, me: (0, early(i)))
    return pl.pallas_call(
        functools.partial(back_kernel, n_steps),
        grid_spec=pltpu.PrefetchScalarGridSpec(
            num_scalar_prefetch=1,
            grid=(n_steps + n_late,),
            in_specs=[whole_spec(p) for p in pieces]
            + [whole_spec(grad_output), cols]
            + [pl.BlockSpec((ROWS, hidden), lambda i, me: (late(i), 0))],
            out_specs=[
                cols,
                pl.BlockSpec((1, COLS), lambda i, me: (0, early(i))),
                pl.BlockSpec((COLS, width), lambda i, me: (early(i), 0)),
                pl.BlockSpec((length, ROWS), lambda i, me: (0, late(i))),
            ],
            scratch_shapes=[pltpu.VMEM((hidden, width), BF), pltpu.VMEM((length, hidden), BF)],
        ),
        out_shape=[
            jax.ShapeDtypeStruct((length, hidden), BF),
            jax.ShapeDtypeStruct((1, hidden), F32),
            jax.ShapeDtypeStruct((hidden, width), BF),
            jax.ShapeDtypeStruct((length, width), BF),
        ],
    )(me, *pieces, grad_output, slope, up_full)


def turn_kernel(n, me_ref, *refs):
    own_ref, other_ref, middle_ref, dy_ref, gain_ref = refs[:5]
    weights = refs[5 : 5 + n]
    g_middle_ref, g_attn_ref, g_mixed_ref, sum_ref = refs[5 + n :]
    grad = own_ref[...].astype(F32) + other_ref[...].astype(F32)
    unit, inverse = normed(middle_ref[...])
    g_middle = dy_ref[...].astype(F32) + norm_back(grad, gain_ref[...], unit, inverse)
    g_middle_ref[...] = g_middle
    g_attn = g_middle.astype(BF)
    g_attn_ref[...] = g_attn
    total = None
    for i in range(n):
        width = weights[i].shape[1]
        at = pl.multiple_of(me_ref[1 + i] * width, width)
        part = dot(g_attn_ref[:, pl.ds(at, width)], weights[i][...], ((1,), (1,)))
        total = part if total is None else total + part
    g_mixed_ref[...] = total.astype(BF)
    sums = jnp.concatenate(
        [
            jnp.sum(v, axis=0, keepdims=True)
            for v in (grad * unit, grad, g_attn.astype(F32))
        ]
        + [jnp.zeros((5, grad.shape[1]), F32)],
        axis=0,
    )

    @pl.when(pl.program_id(0) == 0)
    def _():
        sum_ref[...] = sums

    @pl.when(pl.program_id(0) > 0)
    def _():
        sum_ref[...] += sums


def turn_of(me, own, other, middle, grad_output, gain, weights, head_cols):
    n, (length, width) = len(weights), middle.shape
    rows = lambda w: pl.BlockSpec((ROWS, w), lambda i, me: (i, 0))
    return pl.pallas_call(
        functools.partial(turn_kernel, n),
        grid_spec=pltpu.PrefetchScalarGridSpec(
            num_scalar_prefetch=1,
            grid=(length // ROWS,),
            in_specs=[rows(width)] * 4
            + [pl.BlockSpec((1, width), lambda i, me: (0, 0))]
            + [pl.BlockSpec((head_cols, w.shape[1]), lambda i, me: (me[0], 0)) for w in weights],
            out_specs=[rows(width), rows(width), rows(head_cols)]
            + [pl.BlockSpec((8, width), lambda i, me: (0, 0))],
        ),
        out_shape=[
            jax.ShapeDtypeStruct((length, width), F32),
            jax.ShapeDtypeStruct((length, width), BF),
            jax.ShapeDtypeStruct((length, head_cols), BF),
            jax.ShapeDtypeStruct((8, width), F32),
        ],
    )(me, own, other, middle, grad_output, gain[None], *weights)


def make_body(dp, seq):
    def body(
        tokens, segments, cotangent,
        query_weight, key_weight, value_weight, out_weight, up_weight, down_weight,
        query_bias, value_bias, out_bias, up_bias, down_bias,
        first_gain, first_shift, second_gain, second_shift,
    ):
        me_seq = lax.axis_index("seq")
        _, local, width = tokens.shape
        length = segments.shape[1]
        rows = query_weight.shape[0]
        hidden = up_weight.shape[1]
        hidden_rows = down_weight.shape[0]
        head_cols = width // seq
        heads = HEADS // seq
        hidden_cols = hidden // seq

        pairs = heads // 2
        small_params = (
            query_bias, value_bias, out_bias, up_bias, down_bias,
            first_gain, first_shift, second_gain, second_shift,
        )
        small_sizes = [v.shape[0] for v in small_params]
        offsets = [sum(small_sizes[:i]) for i in range(len(small_sizes))]

        def first_columns(s, colour):
            at, half = s * head_cols, head_cols // 2
            span = [pairs * colour // 2, pairs * (colour + 1) // 2] if pairs > 1 else [0, 1]
            parts = [
                w[:, at + p * PAIR : at + (p + 1) * PAIR]
                for p in range(*span)
                for w in (query_weight, key_weight, value_weight)
            ]
            if pairs == 1:
                joined = jnp.concatenate(parts, axis=1)
                parts = [joined[:, colour * 3 * half : (colour + 1) * 3 * half]]
            return parts + [out_weight[:, at + colour * half : at + (colour + 1) * half]]

        quick = seq == 2 and hidden_rows == PAIR and pairs > 1
        if quick:
            own, send, up_mine, up_send = split_weights(
                me_seq, (query_weight, key_weight, value_weight, out_weight), up_weight
            )
            first_own = two_rows(own, trade(send), me_seq)
        else:
            first_own = jnp.stack(
                [jnp.concatenate(first_columns(i, 0) + first_columns(i, 1), axis=1) for i in range(seq)]
            )
            first_own = seq_swap(first_own, seq).reshape(seq * rows, -1)
        q_pieces, mark = gather_blocks(first_own, [3 * head_cols, head_cols], dp)

        total = sum(small_sizes)
        small = sum(
            jnp.pad(v.astype(F32), (at, total - at - size))
            for v, at, size in zip(small_params, offsets, small_sizes)
        )
        small_all = seq_gather(small, seq).reshape(-1, 128)
        small_all = gather_small(small_all, dp).reshape(dp * seq, -1)

        if quick:
            up_own = two_rows(up_mine, trade(up_send), me_seq)
        else:
            up_own = up_weight.reshape(rows, dp, seq, hidden_rows).transpose(2, 0, 1, 3)
            up_own = seq_swap(up_own.reshape(seq, rows, hidden_cols), seq).reshape(seq * rows, -1)
        up_pieces, mark = gather_blocks(up_own, [hidden_cols], dp, mark)
        down_pieces, _ = gather_blocks(down_weight, [width], dp, mark)
        tokens_all = seq_gather(tokens[0], seq).reshape(length, width)
        grad_output = seq_gather(cotangent[0], seq).reshape(length, width)

        def small_of(index):
            return small_all[:, offsets[index] : offsets[index] + small_sizes[index]].reshape(-1)

        (q_shift, v_shift, o_shift, u_shift, d_shift, gain_one, shift_one, gain_two, shift_two) = [
            small_of(i) for i in range(9)
        ]

        def own_pairs(vector):
            return lax.dynamic_slice_in_dim(vector, me_seq * head_cols, head_cols, 0).reshape(pairs, PAIR)

        u_own = pick(u_shift.reshape(dp, seq, hidden_rows), me_seq, 1).reshape(-1)
        qkv_shift = jnp.stack(
            [own_pairs(q_shift), jnp.zeros((pairs, PAIR), F32), own_pairs(v_shift)], axis=1
        ).reshape(-1)

        inputs = tokens_all.astype(F32)
        unit_one, _ = normed(inputs)
        me_dp = lax.axis_index("dp").astype(jnp.int32)[None]
        first_low = (unit_one * gain_one + shift_one).astype(BF)
        ids = (me_seq * heads + jnp.arange(heads) + 1).astype(F32)
        slopes = 2.0 ** (-8.0 * ids / HEADS)
        row, col = segments.reshape(1, length), segments.reshape(length, 1)
        ready = (first_low, grad_output, qkv_shift, slopes, row, col, o_shift, u_own, d_shift)
        ready = lax.optimization_barrier(ready)
        first_low, grad_output, qkv_shift, slopes, row, col, o_shift, u_own, d_shift = ready
        qkv, qkv_full, out_half = qkv_of(me_dp, q_pieces, first_low, qkv_shift, head_cols)
        if seq == 2:
            out_parts = [out_half, trade(out_half)]
            me_parts = jnp.stack([me_seq, me_seq, 1 - me_seq]).astype(jnp.int32)
        else:
            out_parts = [lax.all_gather(out_half, "seq", axis=1, tiled=True)]
            me_parts = jnp.stack([me_seq, 0]).astype(jnp.int32)

        mixed_own = attend(slopes, row, col, qkv, range(pairs))
        if seq == 2:
            mixed_parts = [mixed_own, trade(mixed_own)]
        else:
            mixed_parts = [lax.all_gather(mixed_own, "seq", axis=1, tiled=True)]
        mixed, middle, second_low = middle_of(
            me_parts, mixed_parts, out_parts, tokens_all, o_shift, gain_two, shift_two
        )
        activated, hidden_slope, up_full = up_of(me_dp, up_pieces, second_low, u_own)

        (down_sum,) = scatter_grads([activated], [grad_output], dp, (0, 1))
        g_hidden, up_bias_sum, down_full, z_own = back_of(
            me_dp, down_pieces, grad_output, hidden_slope, up_full
        )
        (up_sum,) = scatter_grads([second_low], [g_hidden], dp, (0, 1))
        if seq == 2:
            z_other = trade(z_own)
        else:
            z_other = lax.psum(z_own.astype(F32), "seq") - z_own.astype(F32)
        g_middle, g_attn, g_mixed, turn_sums = turn_of(
            me_parts, z_own, z_other, middle, grad_output, gain_two, out_parts, head_cols
        )
        groups = [range(pairs // 2), range(pairs // 2, pairs)] if pairs > 1 else [range(pairs)]
        g_qkv = [attend_back(slopes, row, col, qkv, g_mixed, group) for group in groups]
        first_sum, out_sum = scatter_grads([first_low, mixed], [g_qkv[0], g_attn], dp, (0,), head_cols)
        qkv_sums = [first_sum] + [scatter_grads([first_low], [part], dp, (1,))[0] for part in g_qkv[1:]]
        g_qkv = jnp.concatenate(g_qkv, axis=1)
        g_first_part = dot(g_qkv, qkv_full, ((1,), (1,)))
        first_sums = (jnp.sum(g_first_part * unit_one, axis=0), jnp.sum(g_first_part, axis=0))
        g_first = seq_reduce(g_first_part.reshape(seq, local, width), seq, BF)
        unit_own, inverse_own = normed(tokens[0].astype(F32))
        g_middle_own = pick(g_middle.reshape(seq, local, width), me_seq, 0)
        input_grad = g_middle_own + norm_back(g_first, gain_one, unit_own, inverse_own)

        late, _ = lax.optimization_barrier((activated, g_qkv))
        lowered = matmul(late, down_full)
        lowered = lowered.reshape(seq, local, width)
        lowered = seq_reduce(lowered, seq, F32)
        middle_own = pick(middle.reshape(seq, local, width), me_seq, 0)
        output = (middle_own + lowered + d_shift).astype(BF)[None]

        def to_rows(total):
            return seq_swap(total.reshape(seq, rows, -1), seq).transpose(1, 0, 2)

        up_rows = to_rows(up_sum).reshape(rows, seq, dp, hidden_rows)
        up_grad = up_rows.transpose(0, 2, 1, 3).reshape(rows, hidden)
        last_rows = to_rows(jnp.concatenate(qkv_sums + [out_sum], axis=1))
        out_grad = last_rows[:, :, 3 * head_cols :].reshape(rows, width)
        qkv_rows = last_rows[:, :, : 3 * head_cols].reshape(rows, seq, pairs, 3, PAIR)
        weight_grads = [qkv_rows[:, :, :, i].reshape(rows, width) for i in range(3)]

        def sums(matrix):
            return jnp.sum(matrix.astype(F32), axis=0)

        mine = jnp.arange(seq) == me_seq

        def heads_only(vector):
            return jnp.where(mine[:, None], vector.reshape(1, -1), 0.0).reshape(-1)

        share = 1.0 / seq
        qkv_columns = sums(g_qkv).reshape(pairs, 3, PAIR)
        up_bias_grad = jnp.where(
            mine[None, :, None], up_bias_sum.reshape(dp, 1, hidden_rows), 0.0
        )
        vectors = [
            heads_only(qkv_columns[:, 0]), heads_only(qkv_columns[:, 2]), turn_sums[2] * share,
            up_bias_grad, sums(cotangent[0]), *first_sums,
            turn_sums[0] * share, turn_sums[1] * share,
        ]
        packed = jnp.concatenate(
            [v.reshape(dp, seq, m) for v, m in zip(vectors, small_sizes)], axis=2
        ).reshape(dp, seq * sum(small_sizes) // 128, 128)
        if boxed(dp):
            small_sum = scatter_far(scatter_near(packed, dp, 0), dp)
        else:
            small_sum = lax.psum_scatter(packed, "dp", scatter_dimension=0, tiled=False)
        small_grad = seq_reduce(small_sum.reshape(seq, -1), seq, F32)
        small_grads = [
            small_grad[offsets[i] : offsets[i] + small_sizes[i]] for i in range(9)
        ]
        return (
            output, input_grad[None], *weight_grads, out_grad, up_grad, down_sum, *small_grads
        )

    return body


def solution(mesh):
    both = ("dp", "seq")
    matrix, vector = P(both, None), P(both)
    dp, seq = mesh.shape["dp"], mesh.shape["seq"]
    layer = make_body(dp, seq)

    return jax.shard_map(
        layer,
        mesh=mesh,
        in_specs=(P("dp", "seq", None), P("dp", None), P("dp", "seq", None))
        + (matrix,) * 6
        + (vector,) * 9,
        out_specs=(P("dp", "seq", None),) * 2 + (matrix,) * 6 + (vector,) * 9,
        check_vma=False,
    )
```

time: 524 us -> 483 us (0.922)
  Pallas kernels: 91.3 us -> 148 us
  matrix products: 47.2 us -> 15.8 us
  other arithmetic: 67.6 us -> 38 us
  local copies, waits for them, and re-layouts: 44.1 us -> 28 us
  waiting for transfers between devices: 157 us -> 147 us
  starting transfers between devices: 105 us -> 98.1 us
    pallas_call x10 -> x16, Pallas kernels: 91.3 us -> 148 us  [the longest x3 43.7 us: attend_call(): pl.pallas_call(functools.partial(kernel, length // BLOCK), grid_spec=pltp...]
    dot_general x8 -> x2, matrix products: 47.2 us -> 15.8 us  [dot(): lax.dot_general(left, right, (contract, ((), ())), preferred_element_type...]
    squeeze x16 -> x0, local copies, waits for them, and re-layouts: 13.3 us -> none  [the longest x8 11.8 us: scatter_grads(): got = flip(grads[1], first, count)]
    reduce_sum x5 -> x2, other arithmetic: 12.9 us -> 2.71 us  [sums(): return jnp.sum(matrix.astype(F32), axis=0)]
    ppermute x59 -> x61, waiting for transfers between devices: 156 us -> 147 us  [flip(): return lax.ppermute(array, 'dp', [(i, i ^ bits) for i in range(count)])]
    ppermute x59 -> x61, starting transfers between devices: 103 us -> 95.9 us  [flip(): return lax.ppermute(array, 'dp', [(i, i ^ bits) for i in range(count)])]
  transfers between devices with their start and end apart: 72 -> 74, of which waited for: 29 -> 27; matrix products, arithmetic and copies ran while one was open for 22% -> 15% of each run, Pallas kernels for 18% -> 25%
where the time goes in v2:
time: 483 us; the launch traced here: 477 us
  Pallas kernels  148 us (31%)
  waiting for transfers between devices  147 us (30%)
  starting transfers between devices  98.1 us (20%)
  other arithmetic  38 us (8%)
  local copies, waits for them, and re-layouts  28 us (6%)
  matrix products  15.8 us (3%)
    ppermute x61, waiting for transfers between devices, flip(): return lax.ppermute(array, 'dp', [(i, i ^ bits) for i in range(count)])  147 us
    ppermute x61, starting transfers between devices, flip(): return lax.ppermute(array, 'dp', [(i, i ^ bits) for i in range(count)])  95.9 us
    pallas_call x3, Pallas kernels, attend_call(): pl.pallas_call(functools.partial(kernel, length // BLOCK), grid_spec=pltp...  43.7 us
    pallas_call x4, Pallas kernels, grad_blocks(): pl.pallas_call(functools.partial(grad_kernel, widths, ways), grid_spec=pl...  35.6 us
    pallas_call x1, Pallas kernels, back_of(): pl.pallas_call(functools.partial(back_kernel, n_steps), grid_spec=pltpu.P...  17.7 us
    dot_general x2, matrix products, dot(): lax.dot_general(left, right, (contract, ((), ())), preferred_element_type...  15.8 us
    pallas_call x1, Pallas kernels, up_of(): pl.pallas_call(up_kernel, grid_spec=pltpu.PrefetchScalarGridSpec(num_scal...  14.1 us
    pallas_call x1, Pallas kernels, turn_of(): pl.pallas_call(functools.partial(turn_kernel, n), grid_spec=pltpu.Prefetc...  10.9 us
  transfers between devices with their start and end apart: 74, of which 27 were waited for; matrix products, arithmetic and copies ran while one was open for 15% of the time, Pallas kernels for 25%

profile of v2, /device:TPU:0, one launch (start us, length us, event | category | flops | bytes accessed | tf_op | source)
XLA Modules:
  0.0 476.9 jit_solution(1258270837811832010)
XLA Ops:
  29.7 4.8 collective-permute-done.11.refs_3_
  39.1 10.0 %collective-permute-start.21 = (bf16[64,2048]{1,0:T(8,128)(2,1)S(1)}, bf16[64,2048]{1,0:T(8,128)(2,1)}, u32[]{:S(2)}, u32[]{:S(2)}) collective-permute-start(bf16[64,2048]{1,0:T(8,128)(2,1)S(1)} %maximum_select_fusion.5.refs_0_), channel_id=1, source_target_pairs={{0,8},{2,10},{4,12},{6,14},{8,0},{10,2},{12,4},{14,6},{16,24},{18,... | collective-permute-start | bytes 786440 | tf_op jit(solution)/shard_map/ppermute | solution.py:62
  52.1 4.7 collective-permute-done.10.refs_2_
  63.3 6.1 %collective-permute-done.22.refs_2_ = bf16[64,2048]{1,0:T(8,128)(2,1)} collective-permute-done((bf16[64,2048]{1,0:T(8,128)(2,1)S(1)}, bf16[64,2048]{1,0:T(8,128)(2,1)}, u32[]{:S(2)}, u32[]{:S(2)}) %collective-permute-start.22) | collective-permute-done | bytes 262176 | tf_op jit(solution)/shard_map/ppermute | solution.py:62
  75.7 4.9 %collective-permute-start.31 = (bf16[128,1024]{1,0:T(8,128)(2,1)S(1)}, bf16[128,1024]{1,0:T(8,128)(2,1)S(1)}, u32[]{:S(2)}, u32[]{:S(2)}) collective-permute-start(bf16[128,1024]{1,0:T(8,128)(2,1)S(1)} %copy-done.23), channel_id=1, source_target_pairs={{0,16},{2,18},{4,20},{6,22},{8,24},{10,26},{12,28},{14,30},{16,0},... | collective-permute-start | bytes 786440 | tf_op jit(solution)/shard_map/ppermute | solution.py:62
  89.2 7.3 %collective-permute-done.31.refs_2_ = bf16[128,1024]{1,0:T(8,128)(2,1)S(1)} collective-permute-done((bf16[128,1024]{1,0:T(8,128)(2,1)S(1)}, bf16[128,1024]{1,0:T(8,128)(2,1)S(1)}, u32[]{:S(2)}, u32[]{:S(2)}) %collective-permute-start.31) | collective-permute-done | bytes 262176 | tf_op jit(solution)/shard_map/ppermute | solution.py:62
  110.1 8.3 %shard_map.307 = (bf16[1024,1536]{1,0:T(8,128)(2,1)}, bf16[1024,1536]{1,0:T(8,128)(2,1)}, bf16[1024,512]{1,0:T(8,128)(2,1)}) custom-call(s32[1]{0:T(128)} %bitcast.21.me_ref, bf16[4,64,1024]{2,1,0:T(8,128)(2,1)} %get-tuple-element.73.refs_0_, bf16[4,64,1024]{2,1,0:T(8,128)(2,1)} %collective-permute-done.12.refs_1_, ...), custom_call_target="tpu_custom_call" | custom-call | tf_op jit(solution)/shard_map/pallas_call | solution.py:522
  118.5 13.7 %shard_map.308.refs_0_ = bf16[1024,512]{1,0:T(8,128)(2,1)} custom-call(s32[1]{0:T(128)} %constant.129.clone.1.first_ref, f32[8]{0:T(128)} %multiply_power_fusion.slope_ref, s32[1,1024]{1,0:T(1,128)} %row_ref.2, s32[1024,1]{1,0:T(8,128)} %copy.54.col_ref, bf16[1024,1536]{1,0:T(8,128)(2,1)} %get-tuple-element.77.qkv_ref), custom_call_target="tpu_custom_call" | custom-call | tf_op jit(solution)/shard_map/pallas_call | solution.py:414
  139.8 9.5 %collective-permute-done.33.refs_1_ = bf16[4,128,512]{2,1,0:T(8,128)(2,1)S(1)} collective-permute-done((bf16[4,128,512]{2,1,0:T(8,128)(2,1)}, bf16[4,128,512]{2,1,0:T(8,128)(2,1)S(1)}, u32[]{:S(2)}, u32[]{:S(2)}) %collective-permute-start.33) | collective-permute-done | bytes 524320 | tf_op jit(solution)/shard_map/ppermute | solution.py:62
  152.7 10.3 %collective-permute-done.26.refs_3_ = bf16[4,64,1024]{2,1,0:T(8,128)(2,1)} collective-permute-done((bf16[4,64,1024]{2,1,0:T(8,128)(2,1)}, bf16[4,64,1024]{2,1,0:T(8,128)(2,1)}, u32[]{:S(2)}, u32[]{:S(2)}) %collective-permute-start.26) | collective-permute-done | bytes 524320 | tf_op jit(solution)/shard_map/ppermute | solution.py:62
  169.3 8.9 %shard_map.309 = (bf16[1024,1024]{1,0:T(8,128)(2,1)}, f32[1024,1024]{1,0:T(8,128)}, bf16[1024,1024]{1,0:T(8,128)(2,1)}) custom-call(s32[3]{0:T(128)} %pad_add_fusion.me_ref, bf16[1024,512]{1,0:T(8,128)(2,1)} %shard_map.308.refs_0_, bf16[1024,512]{1,0:T(8,128)(2,1)} %collective-permute-done.18.refs_1_, bf16[1024,512]{1,0:T(8,128)(2,1)} %get-tuple-element.78.refs_2_.refs_5_, ...), custom_call_target="tpu_custom_call" | custom-call | tf_op jit(solution)/shard_map/pallas_call | solution.py:486
  178.3 14.1 %shard_map.311 = (bf16[1024,2048]{1,0:T(8,128)(2,1)}, bf16[1024,2048]{1,0:T(8,128)(2,1)}, bf16[1024,2048]{1,0:T(8,128)(2,1)}) custom-call(s32[1]{0:T(128)} %bitcast.21.me_ref, bf16[4,64,1024]{2,1,0:T(8,128)(2,1)} %get-tuple-element.84.refs_0_, bf16[4,64,1024]{2,1,0:T(8,128)(2,1)} %collective-permute-done.24.refs_1_, ...), custom_call_target="tpu_custom_call" | custom-call | tf_op jit(solution)/shard_map/pallas_call | solution.py:565
  192.4 9.5 %shard_map.320 = (bf16[2,4,128,512]{3,2,1,0:T(8,128)(2,1)}, bf16[2,4,128,512]{3,2,1,0:T(8,128)(2,1)}, bf16[2,4,128,512]{3,2,1,0:T(8,128)(2,1)}, bf16[2,4,128,512]{3,2,1,0:T(8,128)(2,1)}) custom-call(s32[2]{0:T(128)} %pad_add_fusion.1.me_ref, bf16[1024,2048]{1,0:T(8,128)(2,1)} %get-tuple-element.97.refs_0_, bf16[1024,1024]{1,0:T(8,128)(2,1)} %bitcast.332), custom_call_target="tpu_custom_call" | custom-call | tf_op jit(solution)/shard_map/pallas_call | solution.py:249
  202.7 17.7 %shard_map.313 = (bf16[1024,2048]{1,0:T(8,128)(2,1)}, f32[1,2048]{1,0:T(1,128)}, bf16[2048,1024]{1,0:T(8,128)(2,1)}, bf16[1024,1024]{1,0:T(8,128)(2,1)}) custom-call(s32[1]{0:T(128)} %bitcast.21.me_ref, bf16[4,128,512]{2,1,0:T(8,128)(2,1)} %get-tuple-element.90.refs_0_, bf16[4,128,512]{2,1,0:T(8,128)(2,1)} %copy-done.17, ...), custom_call_target="tpu_custom_call" | custom-call | tf_op jit(solution)/shard_map/pallas_call | solution.py:626
  220.3 10.6 %shard_map.319 = (bf16[2,4,64,1024]{3,2,1,0:T(8,128)(2,1)}, bf16[2,4,64,1024]{3,2,1,0:T(8,128)(2,1)}, bf16[2,4,64,1024]{3,2,1,0:T(8,128)(2,1)}, bf16[2,4,64,1024]{3,2,1,0:T(8,128)(2,1)}) custom-call(s32[2]{0:T(128)} %pad_add_fusion.1.me_ref, bf16[1024,1024]{1,0:T(8,128)(2,1)} %get-tuple-element.86.refs_8_.refs_0_, bf16[1024,2048]{1,0:T(8,128)(2,1)} %get-tuple-element.108.refs_1_), custom_call_target="tpu_custom_call" | custom-call | tf_op jit(solution)/shard_map/pallas_call | solution.py:249
  235.0 7.5 %fusion.96 = f32[1024,1024]{1,0:T(8,128)S(1)} fusion(bf16[1024,2048]{1,0:T(8,128)(2,1)} %get-tuple-element.97.refs_0_, bf16[2048,1024]{1,0:T(8,128)(2,1)} %get-tuple-element.98), kind=kOutput, calls=%fused_computation.229 | convolution fusion | flops 4294967296 | bytes 12582912 | tf_op jit(solution)/shard_map/dot_general | solution.py:22
  245.7 11.5 %collective-permute-done.55 = bf16[2,4,64,1024]{3,2,1,0:T(8,128)(2,1)S(1)} collective-permute-done((bf16[2,4,64,1024]{3,2,1,0:T(8,128)(2,1)}, bf16[2,4,64,1024]{3,2,1,0:T(8,128)(2,1)S(1)}, u32[]{:S(2)}, u32[]{:S(2)}) %collective-permute-start.55) | collective-permute-done | bytes 1048608 | tf_op jit(solution)/shard_map/ppermute | solution.py:62
  259.9 17.1 %collective-permute-done.63 = bf16[2,4,128,512]{3,2,1,0:T(8,128)(2,1)S(1)} collective-permute-done((bf16[2,4,128,512]{3,2,1,0:T(8,128)(2,1)}, bf16[2,4,128,512]{3,2,1,0:T(8,128)(2,1)S(1)}, u32[]{:S(2)}, u32[]{:S(2)}) %collective-permute-start.63) | collective-permute-done | bytes 1048608 | tf_op jit(solution)/shard_map/ppermute | solution.py:62
  282.2 9.2 %collective-permute-done.56 = bf16[4,64,1024]{2,1,0:T(8,128)(2,1)S(1)} collective-permute-done((bf16[4,64,1024]{2,1,0:T(8,128)(2,1)S(1)}, bf16[4,64,1024]{2,1,0:T(8,128)(2,1)S(1)}, u32[]{:S(2)}, u32[]{:S(2)}) %collective-permute-start.56) | collective-permute-done | bytes 524320 | tf_op jit(solution)/shard_map/ppermute | solution.py:62
  294.0 4.4 collective-permute-done.64
  307.4 17.0 %collective-permute-done.58 = bf16[64,2048]{1,0:T(8,128)(2,1)S(1)} collective-permute-done((bf16[64,2048]{1,0:T(8,128)(2,1)S(1)}, bf16[64,2048]{1,0:T(8,128)(2,1)S(1)}, u32[]{:S(2)}, u32[]{:S(2)}) %collective-permute-start.58) | collective-permute-done | bytes 262176 | tf_op jit(solution)/shard_map/ppermute | solution.py:62
  329.9 10.9 %shard_map.314 = (f32[1024,1024]{1,0:T(8,128)}, bf16[1024,1024]{1,0:T(8,128)(2,1)}, bf16[1024,512]{1,0:T(8,128)(2,1)}, f32[8,1024]{1,0:T(8,128)}) custom-call(s32[3]{0:T(128)} %pad_add_fusion.me_ref, bf16[1024,1024]{1,0:T(8,128)(2,1)} %get-tuple-element.95.refs_0_, bf16[1024,1024]{1,0:T(8,128)(2,1)} %copy-done.8, f32[1024,1024]{1,0:T(8,128)} %get-tuple-element.80.refs_2_, ...), custom_call_target="tpu_custom_call" | custom-call | tf_op jit(solution)/shard_map/pallas_call | solution.py:689
  340.9 15.1 %shard_map.315.refs_2_ = bf16[1024,768]{1,0:T(8,128)(2,1)} custom-call(s32[1]{0:T(128)} %constant.129.clone.1.first_ref, f32[8]{0:T(128)} %multiply_power_fusion.slope_ref, s32[1,1024]{1,0:T(1,128)} %row_ref.2, s32[1024,1]{1,0:T(8,128)} %copy.54.col_ref, bf16[1024,1536]{1,0:T(8,128)(2,1)} %get-tuple-element.77.qkv_ref, bf16[1024,512]{1,0:T(8,128)(2,1)} %get-tuple-element.96.g_ref), custom_call_target="tpu_custom_call" | custom-call | tf_op jit(solution)/shard_map/pallas_call | solution.py:414
  356.0 14.8 %shard_map.316.refs_1_ = bf16[1024,768]{1,0:T(8,128)(2,1)} custom-call(s32[1]{0:T(128)} %constant.142.clone.1.first_ref, f32[8]{0:T(128)} %multiply_power_fusion.slope_ref, s32[1,1024]{1,0:T(1,128)} %row_ref.2, s32[1024,1]{1,0:T(8,128)} %copy.54.col_ref, bf16[1024,1536]{1,0:T(8,128)(2,1)} %get-tuple-element.77.qkv_ref, bf16[1024,512]{1,0:T(8,128)(2,1)} %get-tuple-element.96.g_ref), custom_call_target="tpu_custom_call" | custom-call | tf_op jit(solution)/shard_map/pallas_call | solution.py:414
  374.6 8.3 %fusion.92 = (f32[1024]{0:T(1024)S(1)}, f32[1024]{0:T(1024)S(1)}, f32[1024,1024]{1,0:T(8,128)}) fusion(f32[1024]{0:T(1024)S(1)} %bitcast.362, f32[1024]{0:T(1024)S(1)} %bitcast.364, bf16[2,512,1024]{2,1,0:T(8,128)(2,1)S(1)} %copy-done.1, bf16[1024,1536]{1,0:T(8,128)(2,1)} %get-tuple-element.101, bf16[1024,768]{1,0:T(8,128)(2,1)} %shard_map.316.refs_1_, ...), kind=kOutput, calls=%fused_computation.225 | convolution fusion | flops 3233806336 | bytes 12599296 | tf_op jit(solution)/shard_map/dot_general | solution.py:22
  391.0 6.8 %shard_map.318 = (bf16[2,4,64,768]{3,2,1,0:T(8,128)(2,1)}, bf16[2,4,64,768]{3,2,1,0:T(8,128)(2,1)}) custom-call(s32[2]{0:T(128)} %pad_add_fusion.1.me_ref, bf16[1024,1024]{1,0:T(8,128)(2,1)} %add_convert_fusion.refs_8_.refs_0_, bf16[1024,768]{1,0:T(8,128)(2,1)} %shard_map.316.refs_1_), custom_call_target="tpu_custom_call" | custom-call | tf_op jit(solution)/shard_map/pallas_call | solution.py:249
  397.8 8.8 %shard_map.317 = (bf16[2,4,64,1280]{3,2,1,0:T(8,128)(2,1)}, bf16[2,4,64,1280]{3,2,1,0:T(8,128)(2,1)}) custom-call(s32[2]{0:T(128)} %pad_add_fusion.1.me_ref, bf16[1024,1024]{1,0:T(8,128)(2,1)} %add_convert_fusion.refs_8_.refs_0_, bf16[1024,1024]{1,0:T(8,128)(2,1)} %get-tuple-element.102.refs_1_, bf16[1024,768]{1,0:T(8,128)(2,1)} %shard_map.315.refs_2_, ...), custom_call_target="tpu_custom_call" | custom-call | tf_op jit(solution)/shard_map/pallas_call | solution.py:249
  409.9 4.6 fusion.17
  429.9 8.7 %collective-permute-done.42 = bf16[2,4,64,1280]{3,2,1,0:T(8,128)(2,1)} collective-permute-done((bf16[2,4,64,1280]{3,2,1,0:T(8,128)(2,1)}, bf16[2,4,64,1280]{3,2,1,0:T(8,128)(2,1)}, u32[]{:S(2)}, u32[]{:S(2)}) %collective-permute-start.42) | collective-permute-done | bytes 1310752 | tf_op jit(solution)/shard_map/ppermute | solution.py:62
  450.7 4.8 %collective-permute-done.43 = bf16[4,64,1280]{2,1,0:T(8,128)(2,1)S(1)} collective-permute-done((bf16[4,64,1280]{2,1,0:T(8,128)(2,1)S(1)}, bf16[4,64,1280]{2,1,0:T(8,128)(2,1)S(1)}, u32[]{:S(2)}, u32[]{:S(2)}) %collective-permute-start.43) | collective-permute-done | bytes 655392 | tf_op jit(solution)/shard_map/ppermute | solution.py:62
  460.2 4.4 collective-permute-done.46
  464.6 6.1 %collective-permute-done.45 = bf16[64,1280]{1,0:T(8,128)(2,1)S(1)} collective-permute-done((bf16[64,1280]{1,0:T(8,128)(2,1)S(1)}, bf16[64,1280]{1,0:T(8,128)(2,1)S(1)}, u32[]{:S(2)}, u32[]{:S(2)}) %collective-permute-start.45) | collective-permute-done | bytes 163872 | tf_op jit(solution)/shard_map/ppermute | solution.py:62
  (327 shorter events, 174.9 us)
Async XLA Ops:
  18.5 54.7 %collective-permute-start = (bf16[512,1024]{1,0:T(8,128)(2,1)}, bf16[512,1024]{1,0:T(8,128)(2,1)S(1)}, u32[]{:S(2)}, u32[]{:S(2)}) collective-permute-start(bf16[512,1024]{1,0:T(8,128)(2,1)} %bitcast.335), channel_id=1, source_target_pairs={{0,1},{1,0},{2,3},{3,2},{4,5},{5,4},{6,7},{7,6},{8,9},{9,8},{10,11... | collective-permute-start | bytes 3145736 | tf_op jit(solution)/shard_map/ppermute | solution.py:34
  24.9 24.2 %collective-permute-start.9 = (bf16[64,2048]{1,0:T(8,128)(2,1)}, bf16[64,2048]{1,0:T(8,128)(2,1)}, u32[]{:S(2)}, u32[]{:S(2)}) collective-permute-start(bf16[64,2048]{1,0:T(8,128)(2,1)} %maximum_select_fusion.4.refs_0_), channel_id=1, source_target_pairs={{0,8},{2,10},{4,12},{6,14},{8,0},{10,2},{12,4},{14,6},{16,24},{18,... | collective-permute-start | bytes 786440 | tf_op jit(solution)/shard_map/ppermute | solution.py:62
  26.1 30.7 %collective-permute-start.10 = (bf16[64,2048]{1,0:T(8,128)(2,1)}, bf16[64,2048]{1,0:T(8,128)(2,1)}, u32[]{:S(2)}, u32[]{:S(2)}) collective-permute-start(bf16[64,2048]{1,0:T(8,128)(2,1)} %maximum_select_fusion.4.refs_0_), channel_id=1, source_target_pairs={{0,16},{2,18},{4,20},{6,22},{8,24},{10,26},{12,28},{14,30},{16,0},... | collective-permute-start | bytes 786440 | tf_op jit(solution)/shard_map/ppermute | solution.py:62
  34.5 26.0 %collective-permute-start.23 = (bf16[64,2048]{1,0:T(8,128)(2,1)S(1)}, bf16[64,2048]{1,0:T(8,128)(2,1)}, u32[]{:S(2)}, u32[]{:S(2)}) collective-permute-start(bf16[64,2048]{1,0:T(8,128)(2,1)S(1)} %maximum_select_fusion.5.refs_0_), channel_id=1, source_target_pairs={{0,24},{2,26},{4,28},{6,30},{8,16},{10,18},{12,20},{14,22},{16,8},... | collective-permute-start | bytes 786440 | tf_op jit(solution)/shard_map/ppermute | solution.py:62
  39.1 24.2 %collective-permute-start.21 = (bf16[64,2048]{1,0:T(8,128)(2,1)S(1)}, bf16[64,2048]{1,0:T(8,128)(2,1)}, u32[]{:S(2)}, u32[]{:S(2)}) collective-permute-start(bf16[64,2048]{1,0:T(8,128)(2,1)S(1)} %maximum_select_fusion.5.refs_0_), channel_id=1, source_target_pairs={{0,8},{2,10},{4,12},{6,14},{8,0},{10,2},{12,4},{14,6},{16,24},{18,... | collective-permute-start | bytes 786440 | tf_op jit(solution)/shard_map/ppermute | solution.py:62
  63.3 38.0 %collective-permute-start.7 = (bf16[512,1024]{1,0:T(8,128)(2,1)S(1)}, bf16[512,1024]{1,0:T(8,128)(2,1)}, u32[]{:S(2)}, u32[]{:S(2)}) collective-permute-start(bf16[512,1024]{1,0:T(8,128)(2,1)S(1)} %bitcast.342), channel_id=1, source_target_pairs={{0,1},{1,0},{2,3},{3,2},{4,5},{5,4},{6,7},{7,6},{8,9},{9,8},{10,11... | collective-permute-start | bytes 3145736 | tf_op jit(solution)/shard_map/ppermute | solution.py:34
  87.3 44.9 %collective-permute-start.32 = (bf16[128,1024]{1,0:T(8,128)(2,1)S(1)}, bf16[128,1024]{1,0:T(8,128)(2,1)}, u32[]{:S(2)}, u32[]{:S(2)}) collective-permute-start(bf16[128,1024]{1,0:T(8,128)(2,1)S(1)} %copy-done.23), channel_id=1, source_target_pairs={{0,24},{2,26},{4,28},{6,30},{8,16},{10,18},{12,20},{14,22},{16,8},... | collective-permute-start | bytes 786440 | tf_op jit(solution)/shard_map/ppermute | solution.py:62
  97.2 35.1 %collective-permute-start.24 = (bf16[4,64,1024]{2,1,0:T(8,128)(2,1)}, bf16[4,64,1024]{2,1,0:T(8,128)(2,1)}, u32[]{:S(2)}, u32[]{:S(2)}) collective-permute-start(bf16[4,64,1024]{2,1,0:T(8,128)(2,1)} %get-tuple-element.84.refs_0_), channel_id=1, source_target_pairs={{0,2},{2,0},{4,6},{6,4},{8,10},{10,8},{12,14},{14,12},{16,18},{18,... | collective-permute-start | bytes 1572872 | tf_op jit(solution)/shard_map/ppermute | solution.py:62
  101.4 33.8 %collective-permute-start.25 = (bf16[4,64,1024]{2,1,0:T(8,128)(2,1)}, bf16[4,64,1024]{2,1,0:T(8,128)(2,1)}, u32[]{:S(2)}, u32[]{:S(2)}) collective-permute-start(bf16[4,64,1024]{2,1,0:T(8,128)(2,1)} %get-tuple-element.84.refs_0_), channel_id=1, source_target_pairs={{0,4},{2,6},{4,0},{6,2},{8,12},{10,14},{12,8},{14,10},{16,20},{18,... | collective-permute-start | bytes 1572872 | tf_op jit(solution)/shard_map/ppermute | solution.py:62
  104.7 32.0 %collective-permute-start.27 = (bf16[4,64,1024]{2,1,0:T(8,128)(2,1)}, bf16[4,64,1024]{2,1,0:T(8,128)(2,1)}, u32[]{:S(2)}, u32[]{:S(2)}) collective-permute-start(bf16[4,64,1024]{2,1,0:T(8,128)(2,1)} %get-tuple-element.85.refs_4_), channel_id=1, source_target_pairs={{0,4},{2,6},{4,0},{6,2},{8,12},{10,14},{12,8},{14,10},{16,20},{18,... | collective-permute-start | bytes 1572872 | tf_op jit(solution)/shard_map/ppermute | solution.py:62
  104.8 33.8 %collective-permute-start.28 = (bf16[4,64,1024]{2,1,0:T(8,128)(2,1)}, bf16[4,64,1024]{2,1,0:T(8,128)(2,1)}, u32[]{:S(2)}, u32[]{:S(2)}) collective-permute-start(bf16[4,64,1024]{2,1,0:T(8,128)(2,1)} %get-tuple-element.85.refs_4_), channel_id=1, source_target_pairs={{0,2},{2,0},{4,6},{6,4},{8,10},{10,8},{12,14},{14,12},{16,18},{18,... | collective-permute-start | bytes 1572872 | tf_op jit(solution)/shard_map/ppermute | solution.py:62
  132.2 31.3 %collective-permute-start.18 = (bf16[1024,512]{1,0:T(8,128)(2,1)}, bf16[1024,512]{1,0:T(8,128)(2,1)}, u32[]{:S(2)}, u32[]{:S(2)}) collective-permute-start(bf16[1024,512]{1,0:T(8,128)(2,1)} %shard_map.308.refs_0_), channel_id=1, source_target_pairs={{0,1},{1,0},{2,3},{3,2},{4,5},{5,4},{6,7},{7,6},{8,9},{9,8},{10,11... | collective-permute-start | bytes 3145736 | tf_op jit(solution)/shard_map/ppermute | solution.py:34
  132.3 33.2 %collective-permute-start.19 = (bf16[1024,512]{1,0:T(8,128)(2,1)S(1)}, bf16[1024,512]{1,0:T(8,128)(2,1)}, u32[]{:S(2)}, u32[]{:S(2)}) collective-permute-start(bf16[1024,512]{1,0:T(8,128)(2,1)S(1)} %copy-done.6), channel_id=1, source_target_pairs={{0,1},{1,0},{2,3},{3,2},{4,5},{5,4},{6,7},{7,6},{8,9},{9,8},{10,11... | collective-permute-start | bytes 3145736 | tf_op jit(solution)/shard_map/ppermute | solution.py:34
  138.6 24.4 %collective-permute-start.26 = (bf16[4,64,1024]{2,1,0:T(8,128)(2,1)}, bf16[4,64,1024]{2,1,0:T(8,128)(2,1)}, u32[]{:S(2)}, u32[]{:S(2)}) collective-permute-start(bf16[4,64,1024]{2,1,0:T(8,128)(2,1)} %collective-permute-done.24.refs_1_), channel_id=1, source_target_pairs={{0,4},{2,6},{4,0},{6,2},{8,12},{10,14},{12,8},{14,10},{16,20},{18,... | collective-permute-start | bytes 1572872 | tf_op jit(solution)/shard_map/ppermute | solution.py:62
  149.3 52.6 %collective-permute-start.34 = (bf16[4,128,512]{2,1,0:T(8,128)(2,1)}, bf16[4,128,512]{2,1,0:T(8,128)(2,1)}, u32[]{:S(2)}, u32[]{:S(2)}) collective-permute-start(bf16[4,128,512]{2,1,0:T(8,128)(2,1)} %get-tuple-element.90.refs_0_), channel_id=1, source_target_pairs={{0,4},{2,6},{4,0},{6,2},{8,12},{10,14},{12,8},{14,10},{16,20},{18,... | collective-permute-start | bytes 1572872 | tf_op jit(solution)/shard_map/ppermute | solution.py:62
  151.7 50.2 %collective-permute-start.37 = (bf16[4,128,512]{2,1,0:T(8,128)(2,1)}, bf16[4,128,512]{2,1,0:T(8,128)(2,1)}, u32[]{:S(2)}, u32[]{:S(2)}) collective-permute-start(bf16[4,128,512]{2,1,0:T(8,128)(2,1)} %get-tuple-element.91.refs_4_), channel_id=1, source_target_pairs={{0,2},{2,0},{4,6},{6,4},{8,10},{10,8},{12,14},{14,12},{16,18},{18,... | collective-permute-start | bytes 1572872 | tf_op jit(solution)/shard_map/ppermute | solution.py:62
  163.6 38.3 %collective-permute-start.35 = (bf16[4,128,512]{2,1,0:T(8,128)(2,1)S(1)}, bf16[4,128,512]{2,1,0:T(8,128)(2,1)}, u32[]{:S(2)}, u32[]{:S(2)}) collective-permute-start(bf16[4,128,512]{2,1,0:T(8,128)(2,1)S(1)} %collective-permute-done.33.refs_1_), channel_id=1, source_target_pairs={{0,4},{2,6},{4,0},{6,2},{8,12},{10,14},{12,8},{14,10},{16,20},{18,... | collective-permute-start | bytes 1572872 | tf_op jit(solution)/shard_map/ppermute | solution.py:62
  165.5 36.4 %collective-permute-start.38 = (bf16[4,128,512]{2,1,0:T(8,128)(2,1)S(1)}, bf16[4,128,512]{2,1,0:T(8,128)(2,1)S(1)}, u32[]{:S(2)}, u32[]{:S(2)}) collective-permute-start(bf16[4,128,512]{2,1,0:T(8,128)(2,1)S(1)} %collective-permute-done.36.refs_5_), channel_id=1, source_target_pairs={{0,2},{2,0},{4,6},{6,4},{8,10},{10,8},{12,14},{14,12},{16,18},{18,... | collective-permute-start | bytes 1572872 | tf_op jit(solution)/shard_map/ppermute | solution.py:62
  230.9 26.2 %collective-permute-start.55 = (bf16[2,4,64,1024]{3,2,1,0:T(8,128)(2,1)}, bf16[2,4,64,1024]{3,2,1,0:T(8,128)(2,1)S(1)}, u32[]{:S(2)}, u32[]{:S(2)}) collective-permute-start(bf16[2,4,64,1024]{3,2,1,0:T(8,128)(2,1)} %get-tuple-element.112), channel_id=1, source_target_pairs={{0,2},{2,0},{4,6},{6,4},{8,10},{10,8},{12,14},{14,12},{16,18},{18,... | collective-permute-start | bytes 3145736 | tf_op jit(solution)/shard_map/ppermute | solution.py:62
  231.5 26.2 %collective-permute-start.53 = (bf16[2,4,64,1024]{3,2,1,0:T(8,128)(2,1)}, bf16[2,4,64,1024]{3,2,1,0:T(8,128)(2,1)S(1)}, u32[]{:S(2)}, u32[]{:S(2)}) collective-permute-start(bf16[2,4,64,1024]{3,2,1,0:T(8,128)(2,1)} %get-tuple-element.110), channel_id=1, source_target_pairs={{0,4},{2,6},{4,0},{6,2},{8,12},{10,14},{12,8},{14,10},{16,20},{18,... | collective-permute-start | bytes 3145736 | tf_op jit(solution)/shard_map/ppermute | solution.py:62
  233.2 43.7 %collective-permute-start.63 = (bf16[2,4,128,512]{3,2,1,0:T(8,128)(2,1)}, bf16[2,4,128,512]{3,2,1,0:T(8,128)(2,1)S(1)}, u32[]{:S(2)}, u32[]{:S(2)}) collective-permute-start(bf16[2,4,128,512]{3,2,1,0:T(8,128)(2,1)} %get-tuple-element.116), channel_id=1, source_target_pairs={{0,2},{2,0},{4,6},{6,4},{8,10},{10,8},{12,14},{14,12},{16,18},{18,... | collective-permute-start | bytes 3145736 | tf_op jit(solution)/shard_map/ppermute | solution.py:62
  234.7 45.5 %collective-permute-start.61 = (bf16[2,4,128,512]{3,2,1,0:T(8,128)(2,1)}, bf16[2,4,128,512]{3,2,1,0:T(8,128)(2,1)S(1)}, u32[]{:S(2)}, u32[]{:S(2)}) collective-permute-start(bf16[2,4,128,512]{3,2,1,0:T(8,128)(2,1)} %get-tuple-element.114), channel_id=1, source_target_pairs={{0,4},{2,6},{4,0},{6,2},{8,12},{10,14},{12,8},{14,10},{16,20},{18,... | collective-permute-start | bytes 3145736 | tf_op jit(solution)/shard_map/ppermute | solution.py:62
  245.6 164.3 %collective-permute-start.40 = (f32[512,1024]{1,0:T(8,128)}, f32[512,1024]{1,0:T(8,128)}, u32[]{:S(2)}, u32[]{:S(2)}) collective-permute-start(f32[512,1024]{1,0:T(8,128)} %dynamic-slice_bitcast_fusion), channel_id=1, source_target_pairs={{0,1},{1,0},{2,3},{3,2},{4,5},{5,4},{6,7},{7,6},{8,9},{9,8},{10,11... | collective-permute-start | bytes 6291464 | tf_op jit(solution)/shard_map/ppermute | solution.py:34
  257.2 71.4 %collective-permute-start.39 = (bf16[1024,1024]{1,0:T(8,128)(2,1)S(1)}, bf16[1024,1024]{1,0:T(8,128)(2,1)S(1)}, u32[]{:S(2)}, u32[]{:S(2)}) collective-permute-start(bf16[1024,1024]{1,0:T(8,128)(2,1)S(1)} %copy-done.7), channel_id=1, source_target_pairs={{0,1},{1,0},{2,3},{3,2},{4,5},{5,4},{6,7},{7,6},{8,9},{9,8},{10,11... | collective-permute-start | bytes 6291464 | tf_op jit(solution)/shard_map/ppermute | solution.py:34
  257.7 33.7 %collective-permute-start.56 = (bf16[4,64,1024]{2,1,0:T(8,128)(2,1)S(1)}, bf16[4,64,1024]{2,1,0:T(8,128)(2,1)S(1)}, u32[]{:S(2)}, u32[]{:S(2)}) collective-permute-start(bf16[4,64,1024]{2,1,0:T(8,128)(2,1)S(1)} %get-tuple-element.141), channel_id=1, source_target_pairs={{0,4},{2,6},{4,0},{6,2},{8,12},{10,14},{12,8},{14,10},{16,20},{18,... | collective-permute-start | bytes 1572872 | tf_op jit(solution)/shard_map/ppermute | solution.py:62
  298.4 26.0 %collective-permute-start.58 = (bf16[64,2048]{1,0:T(8,128)(2,1)S(1)}, bf16[64,2048]{1,0:T(8,128)(2,1)S(1)}, u32[]{:S(2)}, u32[]{:S(2)}) collective-permute-start(bf16[64,2048]{1,0:T(8,128)(2,1)S(1)} %pad_maximum_fusion.3), channel_id=1, source_target_pairs={{0,16},{2,18},{4,20},{6,22},{8,24},{10,26},{12,28},{14,30},{16,0},... | collective-permute-start | bytes 786440 | tf_op jit(solution)/shard_map/ppermute | solution.py:62
  300.6 23.8 %collective-permute-start.57 = (bf16[64,2048]{1,0:T(8,128)(2,1)S(1)}, bf16[64,2048]{1,0:T(8,128)(2,1)S(1)}, u32[]{:S(2)}, u32[]{:S(2)}) collective-permute-start(bf16[64,2048]{1,0:T(8,128)(2,1)S(1)} %pad_maximum_fusion.2), channel_id=1, source_target_pairs={{0,8},{2,10},{4,12},{6,14},{8,0},{10,2},{12,4},{14,6},{16,24},{18,... | collective-permute-start | bytes 786440 | tf_op jit(solution)/shard_map/ppermute | solution.py:62
  305.3 82.3 %collective-permute-start.67 = (bf16[128,1024]{1,0:T(8,128)(2,1)}, bf16[128,1024]{1,0:T(8,128)(2,1)}, u32[]{:S(2)}, u32[]{:S(2)}) collective-permute-start(bf16[128,1024]{1,0:T(8,128)(2,1)} %pad_maximum_fusion.7), channel_id=1, source_target_pairs={{0,24},{2,26},{4,28},{6,30},{8,16},{10,18},{12,20},{14,22},{16,8},... | collective-permute-start | bytes 786440 | tf_op jit(solution)/shard_map/ppermute | solution.py:62
  324.4 64.6 %collective-permute-start.66 = (bf16[128,1024]{1,0:T(8,128)(2,1)}, bf16[128,1024]{1,0:T(8,128)(2,1)}, u32[]{:S(2)}, u32[]{:S(2)}) collective-permute-start(bf16[128,1024]{1,0:T(8,128)(2,1)} %pad_maximum_fusion.6), channel_id=1, source_target_pairs={{0,16},{2,18},{4,20},{6,22},{8,24},{10,26},{12,28},{14,30},{16,0},... | collective-permute-start | bytes 786440 | tf_op jit(solution)/shard_map/ppermute | solution.py:62
  324.4 64.6 %collective-permute-start.65 = (bf16[128,1024]{1,0:T(8,128)(2,1)}, bf16[128,1024]{1,0:T(8,128)(2,1)}, u32[]{:S(2)}, u32[]{:S(2)}) collective-permute-start(bf16[128,1024]{1,0:T(8,128)(2,1)} %pad_maximum_fusion.5), channel_id=1, source_target_pairs={{0,8},{2,10},{4,12},{6,14},{8,0},{10,2},{12,4},{14,6},{16,24},{18,... | collective-permute-start | bytes 786440 | tf_op jit(solution)/shard_map/ppermute | solution.py:62
  387.6 32.8 %collective-permute-start.60 = (f32[32,2048]{1,0:T(8,128)S(1)}, f32[32,2048]{1,0:T(8,128)S(1)}, u32[]{:S(2)}, u32[]{:S(2)}) collective-permute-start(f32[32,2048]{1,0:T(8,128)S(1)} %get-tuple-element.167), channel_id=1, source_target_pairs={{0,1},{1,0},{2,3},{3,2},{4,5},{5,4},{6,7},{7,6},{8,9},{9,8},{10,11... | collective-permute-start | bytes 786440 | tf_op jit(solution)/shard_map/ppermute | solution.py:34
  406.6 32.0 %collective-permute-start.42 = (bf16[2,4,64,1280]{3,2,1,0:T(8,128)(2,1)}, bf16[2,4,64,1280]{3,2,1,0:T(8,128)(2,1)}, u32[]{:S(2)}, u32[]{:S(2)}) collective-permute-start(bf16[2,4,64,1280]{3,2,1,0:T(8,128)(2,1)} %get-tuple-element.105), channel_id=1, source_target_pairs={{0,4},{2,6},{4,0},{6,2},{8,12},{10,14},{12,8},{14,10},{16,20},{18,... | collective-permute-start | bytes 3932168 | tf_op jit(solution)/shard_map/ppermute | solution.py:62
  (74 other events, 1039.3 us)

commit v3 on v2

--- a/solution.py
+++ b/solution.py
@@ -63,7 +63,7 @@
 
 
 def boxed(count):
-    return count >= 4 and not count & (count - 1)
+    return count == 16
 
 
 def vmem_specs(count):
@@ -178,6 +178,13 @@
     ids = jnp.arange(count)
     order = ((ids[:, None] ^ lax.axis_index("dp")) == ids[None, :]).astype(F32)
     return jnp.sum(order.reshape(count, count, 1, 1) * whole[None], axis=1)
+
+
+FAR_ORDER = (0, 2, 1, 3)
+
+
+def far_of(far, place):
+    return far ^ ((place & 1) * 2 + place // 2)
 
 
 def add_low(a, b):
@@ -241,7 +248,7 @@
     length, n_far = lefts[0].shape[0], count // 4
     depth = lefts[0].shape[1] // n_far
     shapes = [(2, n_far, depth // 4, high - low) for _, low, high in ways for _ in range(2)]
-    in_specs = [pl.BlockSpec((length, depth), lambda k, me: (0, (me[0] // 4) ^ k)) for _ in lefts]
+    in_specs = [pl.BlockSpec((length, depth), lambda k, me: (0, far_of(me[0] // 4, k))) for _ in lefts]
     in_specs += [pl.BlockSpec((length, w), lambda k, me: (0, 0)) for w in widths]
     if column:
         in_specs[-1] = pl.BlockSpec((length, widths[-1]), lambda k, me: (0, me[1]))
@@ -261,7 +268,7 @@
     )(jnp.stack(me), *lefts, *rights)
 
 
-def scatter_grads(lefts, rights, count, colours, column=0):
+def scatter_grads(lefts, rights, count, colours, column=0, stepwise=False):
     widths = [r.shape[1] for r in rights]
     if column:
         widths[-1] = column
@@ -285,10 +292,22 @@
         got = flip(give, first, count)
         late = flip(add_low(keep[1], got[1]), second, count)
         ends.append((add_low(keep[0], got[0]), late))
-    total = jnp.concatenate([k[0].astype(F32) + l[0].astype(F32) for k, l in ends], axis=1)
-    for k in range(1, count // 4):
-        part = jnp.concatenate([add_low(keep[k], late[k]) for keep, late in ends], axis=1)
-        total = total + flip(part, 4 * k, count).astype(F32)
+
+    def joined(at, stop, kind):
+        parts = [k[at:stop].astype(F32) + l[at:stop].astype(F32) for k, l in ends]
+        return jnp.concatenate(parts, axis=2).astype(kind)
+
+    if stepwise:
+        got = flip(joined(2, 4, BF), 4, count)
+        keep = joined(0, 2, BF)
+        last = flip(add_low(keep[1], got[1]), 8, count)
+        total = keep[0].astype(F32) + got[0].astype(F32) + last.astype(F32)
+    else:
+        total = joined(0, 1, F32)[0]
+        for place in range(1, 4):
+            part = joined(place, place + 1, BF)[0]
+            k = FAR_ORDER[place]
+            total = total + flip(part, 4 * k, count).astype(F32)
     sums, start = [], 0
     for width in widths:
         sums.append(total[:, start : start + width])
@@ -818,11 +837,11 @@
         )
         activated, hidden_slope, up_full = up_of(me_dp, up_pieces, second_low, u_own)
 
-        (down_sum,) = scatter_grads([activated], [grad_output], dp, (0, 1))
+        (down_sum,) = scatter_grads([activated], [grad_output], dp, (0,), stepwise=True)
         g_hidden, up_bias_sum, down_full, z_own = back_of(
             me_dp, down_pieces, grad_output, hidden_slope, up_full
         )
-        (up_sum,) = scatter_grads([second_low], [g_hidden], dp, (0, 1))
+        (up_sum,) = scatter_grads([second_low], [g_hidden], dp, (0, 1), stepwise=True)
         if seq == 2:
             z_other = trade(z_own)
         else:

time: 483 us -> 454 us (0.940)
  waiting for transfers between devices: 147 us -> 124 us
  starting transfers between devices: 98.1 us -> 91.5 us
    ppermute x61 -> x57, waiting for transfers between devices: 147 us -> 124 us  [flip(): return lax.ppermute(array, 'dp', [(i, i ^ bits) for i in range(count)])]
    ppermute x61 -> x57, starting transfers between devices: 95.9 us -> 89.5 us  [flip(): return lax.ppermute(array, 'dp', [(i, i ^ bits) for i in range(count)])]
    convert_element_type x12 -> x7, other arithmetic: 6.04 us -> 10.9 us  [add_low(): return (a.astype(F32) + b.astype(F32)).astype(b.dtype)]
  transfers between devices with their start and end apart: 74 -> 70, of which waited for: 27 -> 23; matrix products, arithmetic and copies ran while one was open for 15% -> 17% of each run, Pallas kernels for 25% -> 29%
where the time goes in v3:
time: 454 us; the launch traced here: 448 us
  Pallas kernels  148 us (33%)
  waiting for transfers between devices  124 us (27%)
  starting transfers between devices  91.5 us (20%)
  other arithmetic  41.2 us (9%)
  local copies, waits for them, and re-layouts  25.1 us (6%)
  matrix products  16 us (4%)
    ppermute x57, waiting for transfers between devices, flip(): return lax.ppermute(array, 'dp', [(i, i ^ bits) for i in range(count)])  124 us
    ppermute x57, starting transfers between devices, flip(): return lax.ppermute(array, 'dp', [(i, i ^ bits) for i in range(count)])  89.5 us
    pallas_call x3, Pallas kernels, attend_call(): pl.pallas_call(functools.partial(kernel, length // BLOCK), grid_spec=pltp...  43.3 us
    pallas_call x4, Pallas kernels, grad_blocks(): pl.pallas_call(functools.partial(grad_kernel, widths, ways), grid_spec=pl...  35.7 us
    pallas_call x1, Pallas kernels, back_of(): pl.pallas_call(functools.partial(back_kernel, n_steps), grid_spec=pltpu.P...  17.8 us
    dot_general x2, matrix products, dot(): lax.dot_general(left, right, (contract, ((), ())), preferred_element_type...  16 us
    pallas_call x1, Pallas kernels, up_of(): pl.pallas_call(up_kernel, grid_spec=pltpu.PrefetchScalarGridSpec(num_scal...  14.2 us
    pallas_call x1, Pallas kernels, turn_of(): pl.pallas_call(functools.partial(turn_kernel, n), grid_spec=pltpu.Prefetc...  11 us
  transfers between devices with their start and end apart: 70, of which 23 were waited for; matrix products, arithmetic and copies ran while one was open for 17% of the time, Pallas kernels for 29%

profile of v3, /device:TPU:0, one launch (start us, length us, event | category | flops | bytes accessed | tf_op | source)
XLA Modules:
  0.0 447.8 jit_solution(17034794304090457526)
XLA Ops:
  12.6 4.2 collective-permute-start.6
  29.7 4.8 %collective-permute-done.11.refs_3_ = bf16[64,2048]{1,0:T(8,128)(2,1)} collective-permute-done((bf16[64,2048]{1,0:T(8,128)(2,1)}, bf16[64,2048]{1,0:T(8,128)(2,1)}, u32[]{:S(2)}, u32[]{:S(2)}) %collective-permute-start.11) | collective-permute-done | bytes 262176 | tf_op jit(solution)/shard_map/ppermute | solution.py:62
  39.1 10.0 %collective-permute-start.21 = (bf16[64,2048]{1,0:T(8,128)(2,1)S(1)}, bf16[64,2048]{1,0:T(8,128)(2,1)}, u32[]{:S(2)}, u32[]{:S(2)}) collective-permute-start(bf16[64,2048]{1,0:T(8,128)(2,1)S(1)} %maximum_select_fusion.5.refs_0_), channel_id=1, source_target_pairs={{0,8},{2,10},{4,12},{6,14},{8,0},{10,2},{12,4},{14,6},{16,24},{18,... | collective-permute-start | bytes 786440 | tf_op jit(solution)/shard_map/ppermute | solution.py:62
  52.1 4.7 %collective-permute-done.10.refs_2_ = bf16[64,2048]{1,0:T(8,128)(2,1)} collective-permute-done((bf16[64,2048]{1,0:T(8,128)(2,1)}, bf16[64,2048]{1,0:T(8,128)(2,1)}, u32[]{:S(2)}, u32[]{:S(2)}) %collective-permute-start.10) | collective-permute-done | bytes 262176 | tf_op jit(solution)/shard_map/ppermute | solution.py:62
  63.3 6.2 %collective-permute-done.22.refs_2_ = bf16[64,2048]{1,0:T(8,128)(2,1)} collective-permute-done((bf16[64,2048]{1,0:T(8,128)(2,1)S(1)}, bf16[64,2048]{1,0:T(8,128)(2,1)}, u32[]{:S(2)}, u32[]{:S(2)}) %collective-permute-start.22) | collective-permute-done | bytes 262176 | tf_op jit(solution)/shard_map/ppermute | solution.py:62
  75.7 4.9 %collective-permute-start.31 = (bf16[128,1024]{1,0:T(8,128)(2,1)S(1)}, bf16[128,1024]{1,0:T(8,128)(2,1)S(1)}, u32[]{:S(2)}, u32[]{:S(2)}) collective-permute-start(bf16[128,1024]{1,0:T(8,128)(2,1)S(1)} %copy-done.21), channel_id=1, source_target_pairs={{0,16},{2,18},{4,20},{6,22},{8,24},{10,26},{12,28},{14,30},{16,0},... | collective-permute-start | bytes 786440 | tf_op jit(solution)/shard_map/ppermute | solution.py:62
  89.2 7.3 %collective-permute-done.31.refs_2_ = bf16[128,1024]{1,0:T(8,128)(2,1)S(1)} collective-permute-done((bf16[128,1024]{1,0:T(8,128)(2,1)S(1)}, bf16[128,1024]{1,0:T(8,128)(2,1)S(1)}, u32[]{:S(2)}, u32[]{:S(2)}) %collective-permute-start.31) | collective-permute-done | bytes 262176 | tf_op jit(solution)/shard_map/ppermute | solution.py:62
  101.4 3.3 collective-permute-start.25
  110.2 8.3 %shard_map.307 = (bf16[1024,1536]{1,0:T(8,128)(2,1)}, bf16[1024,1536]{1,0:T(8,128)(2,1)}, bf16[1024,512]{1,0:T(8,128)(2,1)}) custom-call(s32[1]{0:T(128)} %bitcast.21.me_ref, bf16[4,64,1024]{2,1,0:T(8,128)(2,1)} %get-tuple-element.71.refs_0_, bf16[4,64,1024]{2,1,0:T(8,128)(2,1)} %collective-permute-done.12.refs_1_, ...), custom_call_target="tpu_custom_call" | custom-call | tf_op jit(solution)/shard_map/pallas_call | solution.py:541
  118.5 13.7 %shard_map.308.refs_0_ = bf16[1024,512]{1,0:T(8,128)(2,1)} custom-call(s32[1]{0:T(128)} %constant.129.clone.1.first_ref, f32[8]{0:T(128)} %multiply_power_fusion.slope_ref, s32[1,1024]{1,0:T(1,128)} %row_ref.2, s32[1024,1]{1,0:T(8,128)} %copy.54.col_ref, bf16[1024,1536]{1,0:T(8,128)(2,1)} %get-tuple-element.75.qkv_ref), custom_call_target="tpu_custom_call" | custom-call | tf_op jit(solution)/shard_map/pallas_call | solution.py:433
  139.8 9.5 %collective-permute-done.33.refs_1_ = bf16[4,128,512]{2,1,0:T(8,128)(2,1)S(1)} collective-permute-done((bf16[4,128,512]{2,1,0:T(8,128)(2,1)}, bf16[4,128,512]{2,1,0:T(8,128)(2,1)S(1)}, u32[]{:S(2)}, u32[]{:S(2)}) %collective-permute-start.33) | collective-permute-done | bytes 524320 | tf_op jit(solution)/shard_map/ppermute | solution.py:62
  152.8 10.3 %collective-permute-done.26.refs_3_ = bf16[4,64,1024]{2,1,0:T(8,128)(2,1)} collective-permute-done((bf16[4,64,1024]{2,1,0:T(8,128)(2,1)}, bf16[4,64,1024]{2,1,0:T(8,128)(2,1)}, u32[]{:S(2)}, u32[]{:S(2)}) %collective-permute-start.26) | collective-permute-done | bytes 524320 | tf_op jit(solution)/shard_map/ppermute | solution.py:62
  169.4 9.0 %shard_map.309 = (bf16[1024,1024]{1,0:T(8,128)(2,1)}, f32[1024,1024]{1,0:T(8,128)}, bf16[1024,1024]{1,0:T(8,128)(2,1)}) custom-call(s32[3]{0:T(128)} %pad_add_fusion.me_ref, bf16[1024,512]{1,0:T(8,128)(2,1)} %shard_map.308.refs_0_, bf16[1024,512]{1,0:T(8,128)(2,1)} %collective-permute-done.18.refs_1_, bf16[1024,512]{1,0:T(8,128)(2,1)} %get-tuple-element.76.refs_2_.refs_5_, ...), custom_call_target="tpu_custom_call" | custom-call | tf_op jit(solution)/shard_map/pallas_call | solution.py:505
  178.4 14.2 %shard_map.311 = (bf16[1024,2048]{1,0:T(8,128)(2,1)}, bf16[1024,2048]{1,0:T(8,128)(2,1)}, bf16[1024,2048]{1,0:T(8,128)(2,1)}) custom-call(s32[1]{0:T(128)} %bitcast.21.me_ref, bf16[4,64,1024]{2,1,0:T(8,128)(2,1)} %get-tuple-element.82.refs_0_, bf16[4,64,1024]{2,1,0:T(8,128)(2,1)} %collective-permute-done.24.refs_1_, ...), custom_call_target="tpu_custom_call" | custom-call | tf_op jit(solution)/shard_map/pallas_call | solution.py:584
  193.4 17.8 %shard_map.313 = (bf16[1024,2048]{1,0:T(8,128)(2,1)}, f32[1,2048]{1,0:T(1,128)}, bf16[2048,1024]{1,0:T(8,128)(2,1)}, bf16[1024,1024]{1,0:T(8,128)(2,1)}) custom-call(s32[1]{0:T(128)} %bitcast.21.me_ref, bf16[4,128,512]{2,1,0:T(8,128)(2,1)} %get-tuple-element.88.refs_0_, bf16[4,128,512]{2,1,0:T(8,128)(2,1)} %copy-done.15, ...), custom_call_target="tpu_custom_call" | custom-call | tf_op jit(solution)/shard_map/pallas_call | solution.py:645
  211.3 10.6 %shard_map.319 = (bf16[2,4,64,1024]{3,2,1,0:T(8,128)(2,1)}, bf16[2,4,64,1024]{3,2,1,0:T(8,128)(2,1)}, bf16[2,4,64,1024]{3,2,1,0:T(8,128)(2,1)}, bf16[2,4,64,1024]{3,2,1,0:T(8,128)(2,1)}) custom-call(s32[2]{0:T(128)} %pad_add_fusion.1.me_ref, bf16[1024,1024]{1,0:T(8,128)(2,1)} %get-tuple-element.84.refs_8_.refs_0_, bf16[1024,2048]{1,0:T(8,128)(2,1)} %get-tuple-element.106.refs_1_), custom_call_target="tpu_custom_call" | custom-call | tf_op jit(solution)/shard_map/pallas_call | solution.py:256
  224.1 7.6 %fusion.72 = f32[1024,1024]{1,0:T(8,128)S(1)} fusion(bf16[1024,2048]{1,0:T(8,128)(2,1)} %get-tuple-element.95.refs_0_, bf16[2048,1024]{1,0:T(8,128)(2,1)} %get-tuple-element.96), kind=kOutput, calls=%fused_computation.183 | convolution fusion | flops 4294967296 | bytes 12582912 | tf_op jit(solution)/shard_map/dot_general | solution.py:22
  231.7 15.9 %collective-permute-done.55 = bf16[2,4,64,1024]{3,2,1,0:T(8,128)(2,1)S(1)} collective-permute-done((bf16[2,4,64,1024]{3,2,1,0:T(8,128)(2,1)}, bf16[2,4,64,1024]{3,2,1,0:T(8,128)(2,1)S(1)}, u32[]{:S(2)}, u32[]{:S(2)}) %collective-permute-start.55) | collective-permute-done | bytes 1048608 | tf_op jit(solution)/shard_map/ppermute | solution.py:62
  253.1 9.5 %shard_map.320 = (bf16[2,4,128,1024]{3,2,1,0:T(8,128)(2,1)}, bf16[2,4,128,1024]{3,2,1,0:T(8,128)(2,1)}) custom-call(s32[2]{0:T(128)} %pad_add_fusion.1.me_ref, bf16[1024,2048]{1,0:T(8,128)(2,1)} %get-tuple-element.95.refs_0_, bf16[1024,1024]{1,0:T(8,128)(2,1)} %bitcast.257), custom_call_target="tpu_custom_call" | custom-call | tf_op jit(solution)/shard_map/pallas_call | solution.py:256
  267.5 11.0 %shard_map.314 = (f32[1024,1024]{1,0:T(8,128)}, bf16[1024,1024]{1,0:T(8,128)(2,1)}, bf16[1024,512]{1,0:T(8,128)(2,1)}, f32[8,1024]{1,0:T(8,128)}) custom-call(s32[3]{0:T(128)} %pad_add_fusion.me_ref, bf16[1024,1024]{1,0:T(8,128)(2,1)} %get-tuple-element.93.refs_0_, bf16[1024,1024]{1,0:T(8,128)(2,1)} %collective-permute-done.39.refs_1_, ...), custom_call_target="tpu_custom_call" | custom-call | tf_op jit(solution)/shard_map/pallas_call | solution.py:708
  278.5 14.7 %shard_map.315.refs_2_ = bf16[1024,768]{1,0:T(8,128)(2,1)} custom-call(s32[1]{0:T(128)} %constant.129.clone.1.first_ref, f32[8]{0:T(128)} %multiply_power_fusion.slope_ref, s32[1,1024]{1,0:T(1,128)} %row_ref.2, s32[1024,1]{1,0:T(8,128)} %copy.54.col_ref, bf16[1024,1536]{1,0:T(8,128)(2,1)} %get-tuple-element.75.qkv_ref, bf16[1024,512]{1,0:T(8,128)(2,1)} %get-tuple-element.94.g_ref), custom_call_target="tpu_custom_call" | custom-call | tf_op jit(solution)/shard_map/pallas_call | solution.py:433
  293.2 14.9 %shard_map.316.refs_1_ = bf16[1024,768]{1,0:T(8,128)(2,1)} custom-call(s32[1]{0:T(128)} %constant.142.clone.1.first_ref, f32[8]{0:T(128)} %multiply_power_fusion.slope_ref, s32[1,1024]{1,0:T(1,128)} %row_ref.2, s32[1024,1]{1,0:T(8,128)} %copy.54.col_ref, bf16[1024,1536]{1,0:T(8,128)(2,1)} %get-tuple-element.75.qkv_ref, bf16[1024,512]{1,0:T(8,128)(2,1)} %get-tuple-element.94.g_ref), custom_call_target="tpu_custom_call" | custom-call | tf_op jit(solution)/shard_map/pallas_call | solution.py:433
  308.1 8.4 %fusion.68 = (f32[1024]{0:T(1024)S(1)}, f32[1024]{0:T(1024)S(1)}, f32[1024,1024]{1,0:T(8,128)}) fusion(f32[1024]{0:T(1024)S(1)} %bitcast.286, f32[1024]{0:T(1024)S(1)} %bitcast.288, bf16[2,512,1024]{2,1,0:T(8,128)(2,1)S(1)} %copy-done.1, bf16[1024,1536]{1,0:T(8,128)(2,1)} %get-tuple-element.99, bf16[1024,768]{1,0:T(8,128)(2,1)} %shard_map.316.refs_1_, ...), kind=kOutput, calls=%fused_computation.179 | convolution fusion | flops 3233806336 | bytes 12599296 | tf_op jit(solution)/shard_map/dot_general | solution.py:22
  323.7 4.2 add_convert_fusion.2
  335.1 7.0 %shard_map.318 = (bf16[2,4,64,768]{3,2,1,0:T(8,128)(2,1)}, bf16[2,4,64,768]{3,2,1,0:T(8,128)(2,1)}) custom-call(s32[2]{0:T(128)} %pad_add_fusion.1.me_ref, bf16[1024,1024]{1,0:T(8,128)(2,1)} %add_convert_fusion.refs_8_.refs_0_, bf16[1024,768]{1,0:T(8,128)(2,1)} %shard_map.316.refs_1_), custom_call_target="tpu_custom_call" | custom-call | tf_op jit(solution)/shard_map/pallas_call | solution.py:256
  342.1 8.6 %shard_map.317 = (bf16[2,4,64,1280]{3,2,1,0:T(8,128)(2,1)}, bf16[2,4,64,1280]{3,2,1,0:T(8,128)(2,1)}) custom-call(s32[2]{0:T(128)} %pad_add_fusion.1.me_ref, bf16[1024,1024]{1,0:T(8,128)(2,1)} %add_convert_fusion.refs_8_.refs_0_, bf16[1024,1024]{1,0:T(8,128)(2,1)} %get-tuple-element.100.refs_1_, bf16[1024,768]{1,0:T(8,128)(2,1)} %shard_map.315.refs_2_, ...), custom_call_target="tpu_custom_call" | custom-call | tf_op jit(solution)/shard_map/pallas_call | solution.py:256
  356.0 4.6 %fusion.18 = bf16[1,512,1024]{2,1,0:T(8,128)(2,1)} fusion(f32[512,1024]{1,0:T(8,128)} %collective-permute-done.40, f32[2,512,1024]{2,1,0:T(8,128)} %bitcast.265, s32[]{:T(128)S(6)} %select_n.161, f32[2,512,1024]{2,1,0:T(8,128)} %bitcast.260, f32[1024]{0:T(1024)S(1)} %reshape.357), kind=kLoop, calls=%fused_computation.38 | loop fusion | flops 2097152 | bytes 7344132 | tf_op jit(solution)/shard_map/broadcast_in_dim | solution.py:869
  365.4 6.1 %collective-permute-done.47 = bf16[2,4,64,768]{3,2,1,0:T(8,128)(2,1)} collective-permute-done((bf16[2,4,64,768]{3,2,1,0:T(8,128)(2,1)}, bf16[2,4,64,768]{3,2,1,0:T(8,128)(2,1)}, u32[]{:S(2)}, u32[]{:S(2)}) %collective-permute-start.47) | collective-permute-done | bytes 786464 | tf_op jit(solution)/shard_map/ppermute | solution.py:62
  374.8 18.7 %collective-permute-done.61 = bf16[4,128,1024]{2,1,0:T(8,128)(2,1)} collective-permute-done((bf16[4,128,1024]{2,1,0:T(8,128)(2,1)}, bf16[4,128,1024]{2,1,0:T(8,128)(2,1)}, u32[]{:S(2)}, u32[]{:S(2)}) %collective-permute-start.61) | collective-permute-done | bytes 1048608 | tf_op jit(solution)/shard_map/ppermute | solution.py:62
  404.4 8.8 %collective-permute-done.51 = bf16[64,768]{1,0:T(8,128)(2,1)S(1)} collective-permute-done((bf16[64,768]{1,0:T(8,128)(2,1)S(1)}, bf16[64,768]{1,0:T(8,128)(2,1)S(1)}, u32[]{:S(2)}, u32[]{:S(2)}) %collective-permute-start.51) | collective-permute-done | bytes 98336 | tf_op jit(solution)/shard_map/ppermute | solution.py:62
  415.1 3.3 collective-permute-start.46
  426.4 11.6 %collective-permute-done.44 = bf16[64,1280]{1,0:T(8,128)(2,1)S(1)} collective-permute-done((bf16[64,1280]{1,0:T(8,128)(2,1)S(1)}, bf16[64,1280]{1,0:T(8,128)(2,1)S(1)}, u32[]{:S(2)}, u32[]{:S(2)}) %collective-permute-start.44) | collective-permute-done | bytes 163872 | tf_op jit(solution)/shard_map/ppermute | solution.py:62
  (304 shorter events, 152.7 us)
Async XLA Ops:
  4.2 23.7 %collective-permute-start.20 = (bf16[32,2048]{1,0:T(8,128)(2,1)}, bf16[32,2048]{1,0:T(8,128)(2,1)S(1)}, u32[]{:S(2)}, u32[]{:S(2)}) collective-permute-start(bf16[32,2048]{1,0:T(8,128)(2,1)} %get-tuple-element.80), channel_id=1, source_target_pairs={{0,1},{1,0},{2,3},{3,2},{4,5},{5,4},{6,7},{7,6},{8,9},{9,8},{10,11... | collective-permute-start | bytes 393224 | tf_op jit(solution)/shard_map/ppermute | solution.py:34
  18.5 54.7 %collective-permute-start = (bf16[512,1024]{1,0:T(8,128)(2,1)}, bf16[512,1024]{1,0:T(8,128)(2,1)S(1)}, u32[]{:S(2)}, u32[]{:S(2)}) collective-permute-start(bf16[512,1024]{1,0:T(8,128)(2,1)} %bitcast.259), channel_id=1, source_target_pairs={{0,1},{1,0},{2,3},{3,2},{4,5},{5,4},{6,7},{7,6},{8,9},{9,8},{10,11... | collective-permute-start | bytes 3145736 | tf_op jit(solution)/shard_map/ppermute | solution.py:34
  24.9 24.2 %collective-permute-start.9 = (bf16[64,2048]{1,0:T(8,128)(2,1)}, bf16[64,2048]{1,0:T(8,128)(2,1)}, u32[]{:S(2)}, u32[]{:S(2)}) collective-permute-start(bf16[64,2048]{1,0:T(8,128)(2,1)} %maximum_select_fusion.4.refs_0_), channel_id=1, source_target_pairs={{0,8},{2,10},{4,12},{6,14},{8,0},{10,2},{12,4},{14,6},{16,24},{18,... | collective-permute-start | bytes 786440 | tf_op jit(solution)/shard_map/ppermute | solution.py:62
  26.1 30.7 %collective-permute-start.10 = (bf16[64,2048]{1,0:T(8,128)(2,1)}, bf16[64,2048]{1,0:T(8,128)(2,1)}, u32[]{:S(2)}, u32[]{:S(2)}) collective-permute-start(bf16[64,2048]{1,0:T(8,128)(2,1)} %maximum_select_fusion.4.refs_0_), channel_id=1, source_target_pairs={{0,16},{2,18},{4,20},{6,22},{8,24},{10,26},{12,28},{14,30},{16,0},... | collective-permute-start | bytes 786440 | tf_op jit(solution)/shard_map/ppermute | solution.py:62
  34.5 26.0 %collective-permute-start.23 = (bf16[64,2048]{1,0:T(8,128)(2,1)S(1)}, bf16[64,2048]{1,0:T(8,128)(2,1)}, u32[]{:S(2)}, u32[]{:S(2)}) collective-permute-start(bf16[64,2048]{1,0:T(8,128)(2,1)S(1)} %maximum_select_fusion.5.refs_0_), channel_id=1, source_target_pairs={{0,24},{2,26},{4,28},{6,30},{8,16},{10,18},{12,20},{14,22},{16,8},... | collective-permute-start | bytes 786440 | tf_op jit(solution)/shard_map/ppermute | solution.py:62
  39.1 24.2 %collective-permute-start.21 = (bf16[64,2048]{1,0:T(8,128)(2,1)S(1)}, bf16[64,2048]{1,0:T(8,128)(2,1)}, u32[]{:S(2)}, u32[]{:S(2)}) collective-permute-start(bf16[64,2048]{1,0:T(8,128)(2,1)S(1)} %maximum_select_fusion.5.refs_0_), channel_id=1, source_target_pairs={{0,8},{2,10},{4,12},{6,14},{8,0},{10,2},{12,4},{14,6},{16,24},{18,... | collective-permute-start | bytes 786440 | tf_op jit(solution)/shard_map/ppermute | solution.py:62
  63.3 38.1 %collective-permute-start.7 = (bf16[512,1024]{1,0:T(8,128)(2,1)S(1)}, bf16[512,1024]{1,0:T(8,128)(2,1)}, u32[]{:S(2)}, u32[]{:S(2)}) collective-permute-start(bf16[512,1024]{1,0:T(8,128)(2,1)S(1)} %bitcast.266), channel_id=1, source_target_pairs={{0,1},{1,0},{2,3},{3,2},{4,5},{5,4},{6,7},{7,6},{8,9},{9,8},{10,11... | collective-permute-start | bytes 3145736 | tf_op jit(solution)/shard_map/ppermute | solution.py:34
  87.3 44.9 %collective-permute-start.32 = (bf16[128,1024]{1,0:T(8,128)(2,1)S(1)}, bf16[128,1024]{1,0:T(8,128)(2,1)}, u32[]{:S(2)}, u32[]{:S(2)}) collective-permute-start(bf16[128,1024]{1,0:T(8,128)(2,1)S(1)} %copy-done.21), channel_id=1, source_target_pairs={{0,24},{2,26},{4,28},{6,30},{8,16},{10,18},{12,20},{14,22},{16,8},... | collective-permute-start | bytes 786440 | tf_op jit(solution)/shard_map/ppermute | solution.py:62
  97.2 35.1 %collective-permute-start.24 = (bf16[4,64,1024]{2,1,0:T(8,128)(2,1)}, bf16[4,64,1024]{2,1,0:T(8,128)(2,1)}, u32[]{:S(2)}, u32[]{:S(2)}) collective-permute-start(bf16[4,64,1024]{2,1,0:T(8,128)(2,1)} %get-tuple-element.82.refs_0_), channel_id=1, source_target_pairs={{0,2},{2,0},{4,6},{6,4},{8,10},{10,8},{12,14},{14,12},{16,18},{18,... | collective-permute-start | bytes 1572872 | tf_op jit(solution)/shard_map/ppermute | solution.py:62
  101.4 33.8 %collective-permute-start.25 = (bf16[4,64,1024]{2,1,0:T(8,128)(2,1)}, bf16[4,64,1024]{2,1,0:T(8,128)(2,1)}, u32[]{:S(2)}, u32[]{:S(2)}) collective-permute-start(bf16[4,64,1024]{2,1,0:T(8,128)(2,1)} %get-tuple-element.82.refs_0_), channel_id=1, source_target_pairs={{0,4},{2,6},{4,0},{6,2},{8,12},{10,14},{12,8},{14,10},{16,20},{18,... | collective-permute-start | bytes 1572872 | tf_op jit(solution)/shard_map/ppermute | solution.py:62
  104.7 32.0 %collective-permute-start.27 = (bf16[4,64,1024]{2,1,0:T(8,128)(2,1)}, bf16[4,64,1024]{2,1,0:T(8,128)(2,1)}, u32[]{:S(2)}, u32[]{:S(2)}) collective-permute-start(bf16[4,64,1024]{2,1,0:T(8,128)(2,1)} %get-tuple-element.83.refs_4_), channel_id=1, source_target_pairs={{0,4},{2,6},{4,0},{6,2},{8,12},{10,14},{12,8},{14,10},{16,20},{18,... | collective-permute-start | bytes 1572872 | tf_op jit(solution)/shard_map/ppermute | solution.py:62
  104.8 33.8 %collective-permute-start.28 = (bf16[4,64,1024]{2,1,0:T(8,128)(2,1)}, bf16[4,64,1024]{2,1,0:T(8,128)(2,1)}, u32[]{:S(2)}, u32[]{:S(2)}) collective-permute-start(bf16[4,64,1024]{2,1,0:T(8,128)(2,1)} %get-tuple-element.83.refs_4_), channel_id=1, source_target_pairs={{0,2},{2,0},{4,6},{6,4},{8,10},{10,8},{12,14},{14,12},{16,18},{18,... | collective-permute-start | bytes 1572872 | tf_op jit(solution)/shard_map/ppermute | solution.py:62
  132.2 31.3 %collective-permute-start.18 = (bf16[1024,512]{1,0:T(8,128)(2,1)}, bf16[1024,512]{1,0:T(8,128)(2,1)}, u32[]{:S(2)}, u32[]{:S(2)}) collective-permute-start(bf16[1024,512]{1,0:T(8,128)(2,1)} %shard_map.308.refs_0_), channel_id=1, source_target_pairs={{0,1},{1,0},{2,3},{3,2},{4,5},{5,4},{6,7},{7,6},{8,9},{9,8},{10,11... | collective-permute-start | bytes 3145736 | tf_op jit(solution)/shard_map/ppermute | solution.py:34
  132.3 33.2 %collective-permute-start.19 = (bf16[1024,512]{1,0:T(8,128)(2,1)S(1)}, bf16[1024,512]{1,0:T(8,128)(2,1)}, u32[]{:S(2)}, u32[]{:S(2)}) collective-permute-start(bf16[1024,512]{1,0:T(8,128)(2,1)S(1)} %copy-done.8), channel_id=1, source_target_pairs={{0,1},{1,0},{2,3},{3,2},{4,5},{5,4},{6,7},{7,6},{8,9},{9,8},{10,11... | collective-permute-start | bytes 3145736 | tf_op jit(solution)/shard_map/ppermute | solution.py:34
  138.6 24.4 %collective-permute-start.26 = (bf16[4,64,1024]{2,1,0:T(8,128)(2,1)}, bf16[4,64,1024]{2,1,0:T(8,128)(2,1)}, u32[]{:S(2)}, u32[]{:S(2)}) collective-permute-start(bf16[4,64,1024]{2,1,0:T(8,128)(2,1)} %collective-permute-done.24.refs_1_), channel_id=1, source_target_pairs={{0,4},{2,6},{4,0},{6,2},{8,12},{10,14},{12,8},{14,10},{16,20},{18,... | collective-permute-start | bytes 1572872 | tf_op jit(solution)/shard_map/ppermute | solution.py:62
  149.3 43.2 %collective-permute-start.34 = (bf16[4,128,512]{2,1,0:T(8,128)(2,1)}, bf16[4,128,512]{2,1,0:T(8,128)(2,1)}, u32[]{:S(2)}, u32[]{:S(2)}) collective-permute-start(bf16[4,128,512]{2,1,0:T(8,128)(2,1)} %get-tuple-element.88.refs_0_), channel_id=1, source_target_pairs={{0,4},{2,6},{4,0},{6,2},{8,12},{10,14},{12,8},{14,10},{16,20},{18,... | collective-permute-start | bytes 1572872 | tf_op jit(solution)/shard_map/ppermute | solution.py:62
  151.7 40.8 %collective-permute-start.37 = (bf16[4,128,512]{2,1,0:T(8,128)(2,1)}, bf16[4,128,512]{2,1,0:T(8,128)(2,1)}, u32[]{:S(2)}, u32[]{:S(2)}) collective-permute-start(bf16[4,128,512]{2,1,0:T(8,128)(2,1)} %get-tuple-element.89.refs_4_), channel_id=1, source_target_pairs={{0,2},{2,0},{4,6},{6,4},{8,10},{10,8},{12,14},{14,12},{16,18},{18,... | collective-permute-start | bytes 1572872 | tf_op jit(solution)/shard_map/ppermute | solution.py:62
  163.6 29.0 %collective-permute-start.35 = (bf16[4,128,512]{2,1,0:T(8,128)(2,1)S(1)}, bf16[4,128,512]{2,1,0:T(8,128)(2,1)}, u32[]{:S(2)}, u32[]{:S(2)}) collective-permute-start(bf16[4,128,512]{2,1,0:T(8,128)(2,1)S(1)} %collective-permute-done.33.refs_1_), channel_id=1, source_target_pairs={{0,4},{2,6},{4,0},{6,2},{8,12},{10,14},{12,8},{14,10},{16,20},{18,... | collective-permute-start | bytes 1572872 | tf_op jit(solution)/shard_map/ppermute | solution.py:62
  165.5 27.0 %collective-permute-start.38 = (bf16[4,128,512]{2,1,0:T(8,128)(2,1)S(1)}, bf16[4,128,512]{2,1,0:T(8,128)(2,1)S(1)}, u32[]{:S(2)}, u32[]{:S(2)}) collective-permute-start(bf16[4,128,512]{2,1,0:T(8,128)(2,1)S(1)} %collective-permute-done.36.refs_5_), channel_id=1, source_target_pairs={{0,2},{2,0},{4,6},{6,4},{8,10},{10,8},{12,14},{14,12},{16,18},{18,... | collective-permute-start | bytes 1572872 | tf_op jit(solution)/shard_map/ppermute | solution.py:62
  211.2 56.4 %collective-permute-start.39 = (bf16[1024,1024]{1,0:T(8,128)(2,1)}, bf16[1024,1024]{1,0:T(8,128)(2,1)}, u32[]{:S(2)}, u32[]{:S(2)}) collective-permute-start(bf16[1024,1024]{1,0:T(8,128)(2,1)} %get-tuple-element.93.refs_0_), channel_id=1, source_target_pairs={{0,1},{1,0},{2,3},{3,2},{4,5},{5,4},{6,7},{7,6},{8,9},{9,8},{10,11... | collective-permute-start | bytes 6291464 | tf_op jit(solution)/shard_map/ppermute | solution.py:34
  221.9 25.8 %collective-permute-start.55 = (bf16[2,4,64,1024]{3,2,1,0:T(8,128)(2,1)}, bf16[2,4,64,1024]{3,2,1,0:T(8,128)(2,1)S(1)}, u32[]{:S(2)}, u32[]{:S(2)}) collective-permute-start(bf16[2,4,64,1024]{3,2,1,0:T(8,128)(2,1)} %get-tuple-element.110), channel_id=1, source_target_pairs={{0,2},{2,0},{4,6},{6,4},{8,10},{10,8},{12,14},{14,12},{16,18},{18,... | collective-permute-start | bytes 3145736 | tf_op jit(solution)/shard_map/ppermute | solution.py:62
  222.4 27.4 %collective-permute-start.53 = (bf16[2,4,64,1024]{3,2,1,0:T(8,128)(2,1)}, bf16[2,4,64,1024]{3,2,1,0:T(8,128)(2,1)S(1)}, u32[]{:S(2)}, u32[]{:S(2)}) collective-permute-start(bf16[2,4,64,1024]{3,2,1,0:T(8,128)(2,1)} %get-tuple-element.108), channel_id=1, source_target_pairs={{0,4},{2,6},{4,0},{6,2},{8,12},{10,14},{12,8},{14,10},{16,20},{18,... | collective-permute-start | bytes 3145736 | tf_op jit(solution)/shard_map/ppermute | solution.py:62
  262.6 91.7 %collective-permute-start.40 = (f32[512,1024]{1,0:T(8,128)}, f32[512,1024]{1,0:T(8,128)}, u32[]{:S(2)}, u32[]{:S(2)}) collective-permute-start(f32[512,1024]{1,0:T(8,128)} %dynamic-slice_bitcast_fusion), channel_id=1, source_target_pairs={{0,1},{1,0},{2,3},{3,2},{4,5},{5,4},{6,7},{7,6},{8,9},{9,8},{10,11... | collective-permute-start | bytes 6291464 | tf_op jit(solution)/shard_map/ppermute | solution.py:34
  262.6 61.1 %collective-permute-start.60 = (bf16[2,4,128,1024]{3,2,1,0:T(8,128)(2,1)}, bf16[2,4,128,1024]{3,2,1,0:T(8,128)(2,1)}, u32[]{:S(2)}, u32[]{:S(2)}) collective-permute-start(bf16[2,4,128,1024]{3,2,1,0:T(8,128)(2,1)} %get-tuple-element.112), channel_id=1, source_target_pairs={{0,4},{2,6},{4,0},{6,2},{8,12},{10,14},{12,8},{14,10},{16,20},{18,... | collective-permute-start | bytes 6291464 | tf_op jit(solution)/shard_map/ppermute | solution.py:62
  267.2 52.5 %collective-permute-start.57 = (bf16[2,64,2048]{2,1,0:T(8,128)(2,1)}, bf16[2,64,2048]{2,1,0:T(8,128)(2,1)}, u32[]{:S(2)}, u32[]{:S(2)}) collective-permute-start(bf16[2,64,2048]{2,1,0:T(8,128)(2,1)} %pad_maximum_fusion.2), channel_id=1, source_target_pairs={{0,8},{2,10},{4,12},{6,14},{8,0},{10,2},{12,4},{14,6},{16,24},{18,... | collective-permute-start | bytes 1572872 | tf_op jit(solution)/shard_map/ppermute | solution.py:62
  321.5 31.4 %collective-permute-start.58 = (bf16[64,2048]{1,0:T(8,128)(2,1)}, bf16[64,2048]{1,0:T(8,128)(2,1)}, u32[]{:S(2)}, u32[]{:S(2)}) collective-permute-start(bf16[64,2048]{1,0:T(8,128)(2,1)} %fusion.38), channel_id=1, source_target_pairs={{0,16},{2,18},{4,20},{6,22},{8,24},{10,26},{12,28},{14,30},{16,0},... | collective-permute-start | bytes 786440 | tf_op jit(solution)/shard_map/ppermute | solution.py:62
  350.7 45.6 %collective-permute-start.41 = (bf16[512,1024]{1,0:T(8,128)(2,1)}, bf16[512,1024]{1,0:T(8,128)(2,1)S(1)}, u32[]{:S(2)}, u32[]{:S(2)}) collective-permute-start(bf16[512,1024]{1,0:T(8,128)(2,1)} %fusion.16), channel_id=1, source_target_pairs={{0,1},{1,0},{2,3},{3,2},{4,5},{5,4},{6,7},{7,6},{8,9},{9,8},{10,11... | collective-permute-start | bytes 3145736 | tf_op jit(solution)/shard_map/ppermute | solution.py:34
  352.2 41.3 %collective-permute-start.61 = (bf16[4,128,1024]{2,1,0:T(8,128)(2,1)}, bf16[4,128,1024]{2,1,0:T(8,128)(2,1)}, u32[]{:S(2)}, u32[]{:S(2)}) collective-permute-start(bf16[4,128,1024]{2,1,0:T(8,128)(2,1)} %get-tuple-element.129), channel_id=1, source_target_pairs={{0,2},{2,0},{4,6},{6,4},{8,10},{10,8},{12,14},{14,12},{16,18},{18,... | collective-permute-start | bytes 3145736 | tf_op jit(solution)/shard_map/ppermute | solution.py:62
  354.2 42.8 %collective-permute-start.42 = (bf16[2,4,64,1280]{3,2,1,0:T(8,128)(2,1)}, bf16[2,4,64,1280]{3,2,1,0:T(8,128)(2,1)}, u32[]{:S(2)}, u32[]{:S(2)}) collective-permute-start(bf16[2,4,64,1280]{3,2,1,0:T(8,128)(2,1)} %get-tuple-element.103), channel_id=1, source_target_pairs={{0,4},{2,6},{4,0},{6,2},{8,12},{10,14},{12,8},{14,10},{16,20},{18,... | collective-permute-start | bytes 3932168 | tf_op jit(solution)/shard_map/ppermute | solution.py:62
  373.2 26.6 %collective-permute-start.48 = (bf16[4,64,768]{2,1,0:T(8,128)(2,1)S(1)}, bf16[4,64,768]{2,1,0:T(8,128)(2,1)S(1)}, u32[]{:S(2)}, u32[]{:S(2)}) collective-permute-start(bf16[4,64,768]{2,1,0:T(8,128)(2,1)S(1)} %get-tuple-element.139), channel_id=1, source_target_pairs={{0,4},{2,6},{4,0},{6,2},{8,12},{10,14},{12,8},{14,10},{16,20},{18,... | collective-permute-start | bytes 1179656 | tf_op jit(solution)/shard_map/ppermute | solution.py:62
  395.1 24.4 %collective-permute-start.62 = (bf16[2,128,1024]{2,1,0:T(8,128)(2,1)S(1)}, bf16[2,128,1024]{2,1,0:T(8,128)(2,1)S(1)}, u32[]{:S(2)}, u32[]{:S(2)}) collective-permute-start(bf16[2,128,1024]{2,1,0:T(8,128)(2,1)S(1)} %get-tuple-element.133), channel_id=1, source_target_pairs={{0,8},{2,10},{4,12},{6,14},{8,0},{10,2},{12,4},{14,6},{16,24},{18,... | collective-permute-start | bytes 1572872 | tf_op jit(solution)/shard_map/ppermute | solution.py:62
  419.6 23.6 %collective-permute-start.63 = (bf16[128,1024]{1,0:T(8,128)(2,1)S(1)}, bf16[128,1024]{1,0:T(8,128)(2,1)S(1)}, u32[]{:S(2)}, u32[]{:S(2)}) collective-permute-start(bf16[128,1024]{1,0:T(8,128)(2,1)S(1)} %fusion.39), channel_id=1, source_target_pairs={{0,16},{2,18},{4,20},{6,22},{8,24},{10,26},{12,28},{14,30},{16,0},... | collective-permute-start | bytes 786440 | tf_op jit(solution)/shard_map/ppermute | solution.py:62
  (65 other events, 930.7 us)

commit v4 on v2

--- a/solution.py
+++ b/solution.py
@@ -648,14 +648,21 @@
     )(me, *pieces, grad_output, slope, up_full)
 
 
-def turn_kernel(n, me_ref, *refs):
+def turn_kernel(n, own_blocks, me_ref, *refs):
     own_ref, other_ref, middle_ref, dy_ref, gain_ref = refs[:5]
     weights = refs[5 : 5 + n]
     g_middle_ref, g_attn_ref, g_mixed_ref, sum_ref = refs[5 + n :]
     grad = own_ref[...].astype(F32) + other_ref[...].astype(F32)
     unit, inverse = normed(middle_ref[...])
     g_middle = dy_ref[...].astype(F32) + norm_back(grad, gain_ref[...], unit, inverse)
-    g_middle_ref[...] = g_middle
+    if own_blocks:
+
+        @pl.when(pl.program_id(0) // own_blocks == me_ref[0])
+        def _():
+            g_middle_ref[...] = g_middle
+
+    else:
+        g_middle_ref[...] = g_middle
     g_attn = g_middle.astype(BF)
     g_attn_ref[...] = g_attn
     total = None
@@ -683,22 +690,28 @@
         sum_ref[...] += sums
 
 
-def turn_of(me, own, other, middle, grad_output, gain, weights, head_cols):
+def turn_of(me, own, other, middle, grad_output, gain, weights, head_cols, local):
     n, (length, width) = len(weights), middle.shape
     rows = lambda w: pl.BlockSpec((ROWS, w), lambda i, me: (i, 0))
+    own_blocks = 0 if local % ROWS else local // ROWS
+    kept = rows(width)
+    if own_blocks:
+        kept = pl.BlockSpec(
+            (ROWS, width), lambda i, me: (jnp.clip(i - me[0] * own_blocks, 0, own_blocks - 1), 0)
+        )
     return pl.pallas_call(
-        functools.partial(turn_kernel, n),
+        functools.partial(turn_kernel, n, own_blocks),
         grid_spec=pltpu.PrefetchScalarGridSpec(
             num_scalar_prefetch=1,
             grid=(length // ROWS,),
             in_specs=[rows(width)] * 4
             + [pl.BlockSpec((1, width), lambda i, me: (0, 0))]
             + [pl.BlockSpec((head_cols, w.shape[1]), lambda i, me: (me[0], 0)) for w in weights],
-            out_specs=[rows(width), rows(width), rows(head_cols)]
+            out_specs=[kept, rows(width), rows(head_cols)]
             + [pl.BlockSpec((8, width), lambda i, me: (0, 0))],
         ),
         out_shape=[
-            jax.ShapeDtypeStruct((length, width), F32),
+            jax.ShapeDtypeStruct((local if own_blocks else length, width), F32),
             jax.ShapeDtypeStruct((length, width), BF),
             jax.ShapeDtypeStruct((length, head_cols), BF),
             jax.ShapeDtypeStruct((8, width), F32),
@@ -794,12 +807,13 @@
         unit_one, _ = normed(inputs)
         me_dp = lax.axis_index("dp").astype(jnp.int32)[None]
         first_low = (unit_one * gain_one + shift_one).astype(BF)
+        unit_low = unit_one.astype(BF)
         ids = (me_seq * heads + jnp.arange(heads) + 1).astype(F32)
         slopes = 2.0 ** (-8.0 * ids / HEADS)
         row, col = segments.reshape(1, length), segments.reshape(length, 1)
-        ready = (first_low, grad_output, qkv_shift, slopes, row, col, o_shift, u_own, d_shift)
+        ready = (unit_low, first_low, grad_output, qkv_shift, slopes, row, col, o_shift, u_own, d_shift)
         ready = lax.optimization_barrier(ready)
-        first_low, grad_output, qkv_shift, slopes, row, col, o_shift, u_own, d_shift = ready
+        unit_low, first_low, grad_output, qkv_shift, slopes, row, col, o_shift, u_own, d_shift = ready
         qkv, qkv_full, out_half = qkv_of(me_dp, q_pieces, first_low, qkv_shift, head_cols)
         if seq == 2:
             out_parts = [out_half, trade(out_half)]
@@ -828,7 +842,7 @@
         else:
             z_other = lax.psum(z_own.astype(F32), "seq") - z_own.astype(F32)
         g_middle, g_attn, g_mixed, turn_sums = turn_of(
-            me_parts, z_own, z_other, middle, grad_output, gain_two, out_parts, head_cols
+            me_parts, z_own, z_other, middle, grad_output, gain_two, out_parts, head_cols, local
         )
         groups = [range(pairs // 2), range(pairs // 2, pairs)] if pairs > 1 else [range(pairs)]
         g_qkv = [attend_back(slopes, row, col, qkv, g_mixed, group) for group in groups]
@@ -836,16 +850,22 @@
         qkv_sums = [first_sum] + [scatter_grads([first_low], [part], dp, (1,))[0] for part in g_qkv[1:]]
         g_qkv = jnp.concatenate(g_qkv, axis=1)
         g_first_part = dot(g_qkv, qkv_full, ((1,), (1,)))
-        first_sums = (jnp.sum(g_first_part * unit_one, axis=0), jnp.sum(g_first_part, axis=0))
+        first_sums = (
+            jnp.sum(g_first_part * unit_low.astype(F32), axis=0),
+            jnp.sum(g_first_part, axis=0),
+        )
+        g_first_part = g_first_part.astype(BF)
         g_first = seq_reduce(g_first_part.reshape(seq, local, width), seq, BF)
         unit_own, inverse_own = normed(tokens[0].astype(F32))
-        g_middle_own = pick(g_middle.reshape(seq, local, width), me_seq, 0)
+        g_middle_own = g_middle
+        if g_middle.shape[0] > local:
+            g_middle_own = pick(g_middle.reshape(seq, local, width), me_seq, 0)
         input_grad = g_middle_own + norm_back(g_first, gain_one, unit_own, inverse_own)
 
         late, _ = lax.optimization_barrier((activated, g_qkv))
-        lowered = matmul(late, down_full)
+        lowered = matmul(late, down_full).astype(BF)
         lowered = lowered.reshape(seq, local, width)
-        lowered = seq_reduce(lowered, seq, F32)
+        lowered = seq_reduce(lowered, seq, BF)
         middle_own = pick(middle.reshape(seq, local, width), me_seq, 0)
         output = (middle_own + lowered + d_shift).astype(BF)[None]
 

time: 483 us -> 459 us (0.950)
  waiting for transfers between devices: 147 us -> 122 us
    ppermute x61, waiting for transfers between devices: 147 us -> 122 us  [flip(): return lax.ppermute(array, 'dp', [(i, i ^ bits) for i in range(count)])]
  transfers between devices with their start and end apart: 74 -> 74, of which waited for: 27 -> 25; matrix products, arithmetic and copies ran while one was open for 15% -> 16% of each run, Pallas kernels for 25% -> 27%
where the time goes in v4:
time: 459 us; the launch traced here: 453 us
  Pallas kernels  148 us (32%)
  waiting for transfers between devices  122 us (27%)
  starting transfers between devices  99 us (22%)
  other arithmetic  41.9 us (9%)
  local copies, waits for them, and re-layouts  24.1 us (5%)
  matrix products  15.9 us (3%)
    ppermute x61, waiting for transfers between devices, flip(): return lax.ppermute(array, 'dp', [(i, i ^ bits) for i in range(count)])  122 us
    ppermute x61, starting transfers between devices, flip(): return lax.ppermute(array, 'dp', [(i, i ^ bits) for i in range(count)])  97.2 us
    pallas_call x3, Pallas kernels, attend_call(): pl.pallas_call(functools.partial(kernel, length // BLOCK), grid_spec=pltp...  43.4 us
    pallas_call x4, Pallas kernels, grad_blocks(): pl.pallas_call(functools.partial(grad_kernel, widths, ways), grid_spec=pl...  35.7 us
    pallas_call x1, Pallas kernels, back_of(): pl.pallas_call(functools.partial(back_kernel, n_steps), grid_spec=pltpu.P...  17.6 us
    dot_general x2, matrix products, dot(): lax.dot_general(left, right, (contract, ((), ())), preferred_element_type...  15.9 us
    pallas_call x1, Pallas kernels, up_of(): pl.pallas_call(up_kernel, grid_spec=pltpu.PrefetchScalarGridSpec(num_scal...  14.1 us
    pallas_call x1, Pallas kernels, turn_of(): pl.pallas_call(functools.partial(turn_kernel, n, own_blocks), grid_spec=p...  11.1 us
  transfers between devices with their start and end apart: 74, of which 25 were waited for; matrix products, arithmetic and copies ran while one was open for 16% of the time, Pallas kernels for 27%

profile of v4, /device:TPU:0, one launch (start us, length us, event | category | flops | bytes accessed | tf_op | source)
XLA Modules:
  0.0 452.7 jit_solution(14680123624270666829)
XLA Ops:
  12.6 4.2 collective-permute-start.6
  29.7 4.8 %collective-permute-done.11.refs_3_ = bf16[64,2048]{1,0:T(8,128)(2,1)} collective-permute-done((bf16[64,2048]{1,0:T(8,128)(2,1)}, bf16[64,2048]{1,0:T(8,128)(2,1)}, u32[]{:S(2)}, u32[]{:S(2)}) %collective-permute-start.11) | collective-permute-done | bytes 262176 | tf_op jit(solution)/shard_map/ppermute | solution.py:62
  39.1 10.0 %collective-permute-start.21 = (bf16[64,2048]{1,0:T(8,128)(2,1)S(1)}, bf16[64,2048]{1,0:T(8,128)(2,1)}, u32[]{:S(2)}, u32[]{:S(2)}) collective-permute-start(bf16[64,2048]{1,0:T(8,128)(2,1)S(1)} %maximum_select_fusion.5.refs_0_), channel_id=1, source_target_pairs={{0,8},{2,10},{4,12},{6,14},{8,0},{10,2},{12,4},{14,6},{16,24},{18,... | collective-permute-start | bytes 786440 | tf_op jit(solution)/shard_map/ppermute | solution.py:62
  52.1 4.7 %collective-permute-done.10.refs_2_ = bf16[64,2048]{1,0:T(8,128)(2,1)} collective-permute-done((bf16[64,2048]{1,0:T(8,128)(2,1)}, bf16[64,2048]{1,0:T(8,128)(2,1)}, u32[]{:S(2)}, u32[]{:S(2)}) %collective-permute-start.10) | collective-permute-done | bytes 262176 | tf_op jit(solution)/shard_map/ppermute | solution.py:62
  63.3 6.2 %collective-permute-done.22.refs_2_ = bf16[64,2048]{1,0:T(8,128)(2,1)} collective-permute-done((bf16[64,2048]{1,0:T(8,128)(2,1)S(1)}, bf16[64,2048]{1,0:T(8,128)(2,1)}, u32[]{:S(2)}, u32[]{:S(2)}) %collective-permute-start.22) | collective-permute-done | bytes 262176 | tf_op jit(solution)/shard_map/ppermute | solution.py:62
  75.7 4.9 %collective-permute-start.31 = (bf16[128,1024]{1,0:T(8,128)(2,1)S(1)}, bf16[128,1024]{1,0:T(8,128)(2,1)S(1)}, u32[]{:S(2)}, u32[]{:S(2)}) collective-permute-start(bf16[128,1024]{1,0:T(8,128)(2,1)S(1)} %copy-done.25), channel_id=1, source_target_pairs={{0,16},{2,18},{4,20},{6,22},{8,24},{10,26},{12,28},{14,30},{16,0},... | collective-permute-start | bytes 786440 | tf_op jit(solution)/shard_map/ppermute | solution.py:62
  89.3 7.2 %collective-permute-done.31.refs_2_ = bf16[128,1024]{1,0:T(8,128)(2,1)S(1)} collective-permute-done((bf16[128,1024]{1,0:T(8,128)(2,1)S(1)}, bf16[128,1024]{1,0:T(8,128)(2,1)S(1)}, u32[]{:S(2)}, u32[]{:S(2)}) %collective-permute-start.31) | collective-permute-done | bytes 262176 | tf_op jit(solution)/shard_map/ppermute | solution.py:62
  110.8 8.7 %shard_map.307 = (bf16[1024,1536]{1,0:T(8,128)(2,1)}, bf16[1024,1536]{1,0:T(8,128)(2,1)}, bf16[1024,512]{1,0:T(8,128)(2,1)}) custom-call(s32[1]{0:T(128)} %bitcast.21.me_ref, bf16[4,64,1024]{2,1,0:T(8,128)(2,1)} %get-tuple-element.74.refs_0_, bf16[4,64,1024]{2,1,0:T(8,128)(2,1)} %collective-permute-done.12.refs_1_, ...), custom_call_target="tpu_custom_call" | custom-call | tf_op jit(solution)/shard_map/pallas_call | solution.py:522
  119.5 13.7 %shard_map.308.refs_0_ = bf16[1024,512]{1,0:T(8,128)(2,1)} custom-call(s32[1]{0:T(128)} %constant.129.clone.1.first_ref, f32[8]{0:T(128)} %multiply_power_fusion.slope_ref, s32[1,1024]{1,0:T(1,128)} %row_ref.2, s32[1024,1]{1,0:T(8,128)} %copy.54.col_ref, bf16[1024,1536]{1,0:T(8,128)(2,1)} %get-tuple-element.78.qkv_ref), custom_call_target="tpu_custom_call" | custom-call | tf_op jit(solution)/shard_map/pallas_call | solution.py:414
  140.8 9.5 %collective-permute-done.33.refs_1_ = bf16[4,128,512]{2,1,0:T(8,128)(2,1)S(1)} collective-permute-done((bf16[4,128,512]{2,1,0:T(8,128)(2,1)}, bf16[4,128,512]{2,1,0:T(8,128)(2,1)S(1)}, u32[]{:S(2)}, u32[]{:S(2)}) %collective-permute-start.33) | collective-permute-done | bytes 524320 | tf_op jit(solution)/shard_map/ppermute | solution.py:62
  153.8 10.3 %collective-permute-done.26.refs_3_ = bf16[4,64,1024]{2,1,0:T(8,128)(2,1)} collective-permute-done((bf16[4,64,1024]{2,1,0:T(8,128)(2,1)}, bf16[4,64,1024]{2,1,0:T(8,128)(2,1)}, u32[]{:S(2)}, u32[]{:S(2)}) %collective-permute-start.26) | collective-permute-done | bytes 524320 | tf_op jit(solution)/shard_map/ppermute | solution.py:62
  170.4 8.9 %shard_map.309 = (bf16[1024,1024]{1,0:T(8,128)(2,1)}, f32[1024,1024]{1,0:T(8,128)}, bf16[1024,1024]{1,0:T(8,128)(2,1)}) custom-call(s32[3]{0:T(128)} %pad_add_fusion.me_ref, bf16[1024,512]{1,0:T(8,128)(2,1)} %shard_map.308.refs_0_, bf16[1024,512]{1,0:T(8,128)(2,1)} %collective-permute-done.18.refs_1_, bf16[1024,512]{1,0:T(8,128)(2,1)} %get-tuple-element.79.refs_2_.refs_5_, ...), custom_call_target="tpu_custom_call" | custom-call | tf_op jit(solution)/shard_map/pallas_call | solution.py:486
  179.3 14.1 %shard_map.311 = (bf16[1024,2048]{1,0:T(8,128)(2,1)}, bf16[1024,2048]{1,0:T(8,128)(2,1)}, bf16[1024,2048]{1,0:T(8,128)(2,1)}) custom-call(s32[1]{0:T(128)} %bitcast.21.me_ref, bf16[4,64,1024]{2,1,0:T(8,128)(2,1)} %get-tuple-element.85.refs_0_, bf16[4,64,1024]{2,1,0:T(8,128)(2,1)} %collective-permute-done.24.refs_1_, ...), custom_call_target="tpu_custom_call" | custom-call | tf_op jit(solution)/shard_map/pallas_call | solution.py:565
  193.4 9.4 %shard_map.320 = (bf16[2,4,128,512]{3,2,1,0:T(8,128)(2,1)}, bf16[2,4,128,512]{3,2,1,0:T(8,128)(2,1)}, bf16[2,4,128,512]{3,2,1,0:T(8,128)(2,1)}, bf16[2,4,128,512]{3,2,1,0:T(8,128)(2,1)}) custom-call(s32[2]{0:T(128)} %pad_add_fusion.1.me_ref, bf16[1024,2048]{1,0:T(8,128)(2,1)} %get-tuple-element.98.refs_0_, bf16[1024,1024]{1,0:T(8,128)(2,1)} %bitcast.317), custom_call_target="tpu_custom_call" | custom-call | tf_op jit(solution)/shard_map/pallas_call | solution.py:249
  203.7 17.6 %shard_map.313 = (bf16[1024,2048]{1,0:T(8,128)(2,1)}, f32[1,2048]{1,0:T(1,128)}, bf16[2048,1024]{1,0:T(8,128)(2,1)}, bf16[1024,1024]{1,0:T(8,128)(2,1)}) custom-call(s32[1]{0:T(128)} %bitcast.21.me_ref, bf16[4,128,512]{2,1,0:T(8,128)(2,1)} %get-tuple-element.91.refs_0_, bf16[4,128,512]{2,1,0:T(8,128)(2,1)} %copy-done.20, ...), custom_call_target="tpu_custom_call" | custom-call | tf_op jit(solution)/shard_map/pallas_call | solution.py:626
  221.3 10.6 %shard_map.319 = (bf16[2,4,64,1024]{3,2,1,0:T(8,128)(2,1)}, bf16[2,4,64,1024]{3,2,1,0:T(8,128)(2,1)}, bf16[2,4,64,1024]{3,2,1,0:T(8,128)(2,1)}, bf16[2,4,64,1024]{3,2,1,0:T(8,128)(2,1)}) custom-call(s32[2]{0:T(128)} %pad_add_fusion.1.me_ref, bf16[1024,1024]{1,0:T(8,128)(2,1)} %get-tuple-element.87.refs_8_.refs_0_, bf16[1024,2048]{1,0:T(8,128)(2,1)} %get-tuple-element.109.refs_1_), custom_call_target="tpu_custom_call" | custom-call | tf_op jit(solution)/shard_map/pallas_call | solution.py:249
  235.9 8.0 %convolution_convert_fusion = bf16[1024,1024]{1,0:T(8,128)(2,1)S(1)} fusion(bf16[1024,2048]{1,0:T(8,128)(2,1)} %get-tuple-element.98.refs_0_, bf16[2048,1024]{1,0:T(8,128)(2,1)} %get-tuple-element.99), kind=kOutput, calls=%fused_computation.31 | convolution fusion | flops 4296015872 | bytes 10485760 | tf_op jit(solution)/shard_map/dot_general | solution.py:22
  244.2 13.9 %collective-permute-done.55 = bf16[2,4,64,1024]{3,2,1,0:T(8,128)(2,1)S(1)} collective-permute-done((bf16[2,4,64,1024]{3,2,1,0:T(8,128)(2,1)}, bf16[2,4,64,1024]{3,2,1,0:T(8,128)(2,1)S(1)}, u32[]{:S(2)}, u32[]{:S(2)}) %collective-permute-start.55) | collective-permute-done | bytes 1048608 | tf_op jit(solution)/shard_map/ppermute | solution.py:62
  260.8 17.1 %collective-permute-done.63 = bf16[2,4,128,512]{3,2,1,0:T(8,128)(2,1)S(1)} collective-permute-done((bf16[2,4,128,512]{3,2,1,0:T(8,128)(2,1)}, bf16[2,4,128,512]{3,2,1,0:T(8,128)(2,1)S(1)}, u32[]{:S(2)}, u32[]{:S(2)}) %collective-permute-start.63) | collective-permute-done | bytes 1048608 | tf_op jit(solution)/shard_map/ppermute | solution.py:62
  286.3 6.0 %collective-permute-done.56 = bf16[4,64,1024]{2,1,0:T(8,128)(2,1)S(1)} collective-permute-done((bf16[4,64,1024]{2,1,0:T(8,128)(2,1)S(1)}, bf16[4,64,1024]{2,1,0:T(8,128)(2,1)S(1)}, u32[]{:S(2)}, u32[]{:S(2)}) %collective-permute-start.56) | collective-permute-done | bytes 524320 | tf_op jit(solution)/shard_map/ppermute | solution.py:62
  307.3 11.1 %shard_map.314 = (f32[512,1024]{1,0:T(8,128)}, bf16[1024,1024]{1,0:T(8,128)(2,1)}, bf16[1024,512]{1,0:T(8,128)(2,1)}, f32[8,1024]{1,0:T(8,128)}) custom-call(s32[3]{0:T(128)} %pad_add_fusion.me_ref, bf16[1024,1024]{1,0:T(8,128)(2,1)} %get-tuple-element.96.refs_0_, bf16[1024,1024]{1,0:T(8,128)(2,1)} %copy-done.9, f32[1024,1024]{1,0:T(8,128)} %get-tuple-element.81.refs_2_, ...), custom_call_target="tpu_custom_call" | custom-call | tf_op jit(solution)/shard_map/pallas_call | solution.py:702
  318.3 14.6 %shard_map.315.refs_2_ = bf16[1024,768]{1,0:T(8,128)(2,1)} custom-call(s32[1]{0:T(128)} %constant.129.clone.1.first_ref, f32[8]{0:T(128)} %multiply_power_fusion.slope_ref, s32[1,1024]{1,0:T(1,128)} %row_ref.2, s32[1024,1]{1,0:T(8,128)} %copy.54.col_ref, bf16[1024,1536]{1,0:T(8,128)(2,1)} %get-tuple-element.78.qkv_ref, bf16[1024,512]{1,0:T(8,128)(2,1)} %get-tuple-element.97.g_ref), custom_call_target="tpu_custom_call" | custom-call | tf_op jit(solution)/shard_map/pallas_call | solution.py:414
  333.0 15.1 %shard_map.316.refs_1_ = bf16[1024,768]{1,0:T(8,128)(2,1)} custom-call(s32[1]{0:T(128)} %constant.142.clone.1.first_ref, f32[8]{0:T(128)} %multiply_power_fusion.slope_ref, s32[1,1024]{1,0:T(1,128)} %row_ref.2, s32[1024,1]{1,0:T(8,128)} %copy.54.col_ref, bf16[1024,1536]{1,0:T(8,128)(2,1)} %get-tuple-element.78.qkv_ref, bf16[1024,512]{1,0:T(8,128)(2,1)} %get-tuple-element.97.g_ref), custom_call_target="tpu_custom_call" | custom-call | tf_op jit(solution)/shard_map/pallas_call | solution.py:414
  350.6 7.9 %fusion.92 = (f32[1024]{0:T(1024)S(1)}, f32[1024]{0:T(1024)S(1)}, bf16[1024,1024]{1,0:T(8,128)(2,1)}) fusion(bf16[1024,1024]{1,0:T(8,128)(2,1)} %get-tuple-element.120, bf16[1024,1536]{1,0:T(8,128)(2,1)} %get-tuple-element.102, bf16[1024,768]{1,0:T(8,128)(2,1)S(1)} %copy-done.2, bf16[1024,768]{1,0:T(8,128)(2,1)} %shard_map.315.refs_2_), kind=kOutput, calls=%fused_computation.226 | convolution fusion | flops 3232757760 | bytes 10493952 | tf_op jit(solution)/shard_map/dot_general | solution.py:22
  369.1 8.7 %shard_map.317 = (bf16[2,4,64,1280]{3,2,1,0:T(8,128)(2,1)}, bf16[2,4,64,1280]{3,2,1,0:T(8,128)(2,1)}) custom-call(s32[2]{0:T(128)} %pad_add_fusion.1.me_ref, bf16[1024,1024]{1,0:T(8,128)(2,1)} %get-tuple-element.76.refs_8_.refs_0_, bf16[1024,1024]{1,0:T(8,128)(2,1)} %get-tuple-element.103.refs_1_, bf16[1024,768]{1,0:T(8,128)(2,1)} %shard_map.315.refs_2_, ...), custom_call_target="tpu_custom_call" | custom-call | tf_op jit(solution)/shard_map/pallas_call | solution.py:249
  381.7 7.1 %shard_map.318 = (bf16[2,4,64,768]{3,2,1,0:T(8,128)(2,1)}, bf16[2,4,64,768]{3,2,1,0:T(8,128)(2,1)}) custom-call(s32[2]{0:T(128)} %pad_add_fusion.1.me_ref, bf16[1024,1024]{1,0:T(8,128)(2,1)} %get-tuple-element.76.refs_8_.refs_0_, bf16[1024,768]{1,0:T(8,128)(2,1)} %shard_map.316.refs_1_), custom_call_target="tpu_custom_call" | custom-call | tf_op jit(solution)/shard_map/pallas_call | solution.py:249
  401.3 7.5 %collective-permute-done.47 = bf16[2,4,64,768]{3,2,1,0:T(8,128)(2,1)} collective-permute-done((bf16[2,4,64,768]{3,2,1,0:T(8,128)(2,1)}, bf16[2,4,64,768]{3,2,1,0:T(8,128)(2,1)}, u32[]{:S(2)}, u32[]{:S(2)}) %collective-permute-start.47) | collective-permute-done | bytes 786464 | tf_op jit(solution)/shard_map/ppermute | solution.py:62
  415.4 5.3 %collective-permute-done.48 = bf16[4,64,768]{2,1,0:T(8,128)(2,1)S(1)} collective-permute-done((bf16[4,64,768]{2,1,0:T(8,128)(2,1)S(1)}, bf16[4,64,768]{2,1,0:T(8,128)(2,1)S(1)}, u32[]{:S(2)}, u32[]{:S(2)}) %collective-permute-start.48) | collective-permute-done | bytes 393248 | tf_op jit(solution)/shard_map/ppermute | solution.py:62
  428.2 3.3 collective-permute-start.46
  432.7 4.9 %collective-permute-done.50 = bf16[64,768]{1,0:T(8,128)(2,1)S(1)} collective-permute-done((bf16[64,768]{1,0:T(8,128)(2,1)S(1)}, bf16[64,768]{1,0:T(8,128)(2,1)S(1)}, u32[]{:S(2)}, u32[]{:S(2)}) %collective-permute-start.50) | collective-permute-done | bytes 98336 | tf_op jit(solution)/shard_map/ppermute | solution.py:62
  437.7 7.5 %collective-permute-done.45 = bf16[64,1280]{1,0:T(8,128)(2,1)S(1)} collective-permute-done((bf16[64,1280]{1,0:T(8,128)(2,1)S(1)}, bf16[64,1280]{1,0:T(8,128)(2,1)S(1)}, u32[]{:S(2)}, u32[]{:S(2)}) %collective-permute-start.45) | collective-permute-done | bytes 163872 | tf_op jit(solution)/shard_map/ppermute | solution.py:62
  445.5 3.4 fusion.11
  (325 shorter events, 165.0 us)
Async XLA Ops:
  18.5 54.7 %collective-permute-start = (bf16[512,1024]{1,0:T(8,128)(2,1)}, bf16[512,1024]{1,0:T(8,128)(2,1)S(1)}, u32[]{:S(2)}, u32[]{:S(2)}) collective-permute-start(bf16[512,1024]{1,0:T(8,128)(2,1)} %bitcast.320), channel_id=1, source_target_pairs={{0,1},{1,0},{2,3},{3,2},{4,5},{5,4},{6,7},{7,6},{8,9},{9,8},{10,11... | collective-permute-start | bytes 3145736 | tf_op jit(solution)/shard_map/ppermute | solution.py:34
  24.9 24.2 %collective-permute-start.9 = (bf16[64,2048]{1,0:T(8,128)(2,1)}, bf16[64,2048]{1,0:T(8,128)(2,1)}, u32[]{:S(2)}, u32[]{:S(2)}) collective-permute-start(bf16[64,2048]{1,0:T(8,128)(2,1)} %maximum_select_fusion.4.refs_0_), channel_id=1, source_target_pairs={{0,8},{2,10},{4,12},{6,14},{8,0},{10,2},{12,4},{14,6},{16,24},{18,... | collective-permute-start | bytes 786440 | tf_op jit(solution)/shard_map/ppermute | solution.py:62
  26.1 30.7 %collective-permute-start.10 = (bf16[64,2048]{1,0:T(8,128)(2,1)}, bf16[64,2048]{1,0:T(8,128)(2,1)}, u32[]{:S(2)}, u32[]{:S(2)}) collective-permute-start(bf16[64,2048]{1,0:T(8,128)(2,1)} %maximum_select_fusion.4.refs_0_), channel_id=1, source_target_pairs={{0,16},{2,18},{4,20},{6,22},{8,24},{10,26},{12,28},{14,30},{16,0},... | collective-permute-start | bytes 786440 | tf_op jit(solution)/shard_map/ppermute | solution.py:62
  34.5 26.0 %collective-permute-start.23 = (bf16[64,2048]{1,0:T(8,128)(2,1)S(1)}, bf16[64,2048]{1,0:T(8,128)(2,1)}, u32[]{:S(2)}, u32[]{:S(2)}) collective-permute-start(bf16[64,2048]{1,0:T(8,128)(2,1)S(1)} %maximum_select_fusion.5.refs_0_), channel_id=1, source_target_pairs={{0,24},{2,26},{4,28},{6,30},{8,16},{10,18},{12,20},{14,22},{16,8},... | collective-permute-start | bytes 786440 | tf_op jit(solution)/shard_map/ppermute | solution.py:62
  39.1 24.1 %collective-permute-start.21 = (bf16[64,2048]{1,0:T(8,128)(2,1)S(1)}, bf16[64,2048]{1,0:T(8,128)(2,1)}, u32[]{:S(2)}, u32[]{:S(2)}) collective-permute-start(bf16[64,2048]{1,0:T(8,128)(2,1)S(1)} %maximum_select_fusion.5.refs_0_), channel_id=1, source_target_pairs={{0,8},{2,10},{4,12},{6,14},{8,0},{10,2},{12,4},{14,6},{16,24},{18,... | collective-permute-start | bytes 786440 | tf_op jit(solution)/shard_map/ppermute | solution.py:62
  63.3 38.7 %collective-permute-start.7 = (bf16[512,1024]{1,0:T(8,128)(2,1)S(1)}, bf16[512,1024]{1,0:T(8,128)(2,1)}, u32[]{:S(2)}, u32[]{:S(2)}) collective-permute-start(bf16[512,1024]{1,0:T(8,128)(2,1)S(1)} %bitcast.325), channel_id=1, source_target_pairs={{0,1},{1,0},{2,3},{3,2},{4,5},{5,4},{6,7},{7,6},{8,9},{9,8},{10,11... | collective-permute-start | bytes 3145736 | tf_op jit(solution)/shard_map/ppermute | solution.py:34
  87.4 45.9 %collective-permute-start.32 = (bf16[128,1024]{1,0:T(8,128)(2,1)S(1)}, bf16[128,1024]{1,0:T(8,128)(2,1)}, u32[]{:S(2)}, u32[]{:S(2)}) collective-permute-start(bf16[128,1024]{1,0:T(8,128)(2,1)S(1)} %copy-done.25), channel_id=1, source_target_pairs={{0,24},{2,26},{4,28},{6,30},{8,16},{10,18},{12,20},{14,22},{16,8},... | collective-permute-start | bytes 786440 | tf_op jit(solution)/shard_map/ppermute | solution.py:62
  97.2 36.1 %collective-permute-start.24 = (bf16[4,64,1024]{2,1,0:T(8,128)(2,1)}, bf16[4,64,1024]{2,1,0:T(8,128)(2,1)}, u32[]{:S(2)}, u32[]{:S(2)}) collective-permute-start(bf16[4,64,1024]{2,1,0:T(8,128)(2,1)} %get-tuple-element.85.refs_0_), channel_id=1, source_target_pairs={{0,2},{2,0},{4,6},{6,4},{8,10},{10,8},{12,14},{14,12},{16,18},{18,... | collective-permute-start | bytes 1572872 | tf_op jit(solution)/shard_map/ppermute | solution.py:62
  102.0 34.2 %collective-permute-start.25 = (bf16[4,64,1024]{2,1,0:T(8,128)(2,1)}, bf16[4,64,1024]{2,1,0:T(8,128)(2,1)}, u32[]{:S(2)}, u32[]{:S(2)}) collective-permute-start(bf16[4,64,1024]{2,1,0:T(8,128)(2,1)} %get-tuple-element.85.refs_0_), channel_id=1, source_target_pairs={{0,4},{2,6},{4,0},{6,2},{8,12},{10,14},{12,8},{14,10},{16,20},{18,... | collective-permute-start | bytes 1572872 | tf_op jit(solution)/shard_map/ppermute | solution.py:62
  105.4 32.3 %collective-permute-start.27 = (bf16[4,64,1024]{2,1,0:T(8,128)(2,1)}, bf16[4,64,1024]{2,1,0:T(8,128)(2,1)}, u32[]{:S(2)}, u32[]{:S(2)}) collective-permute-start(bf16[4,64,1024]{2,1,0:T(8,128)(2,1)} %get-tuple-element.86.refs_4_), channel_id=1, source_target_pairs={{0,4},{2,6},{4,0},{6,2},{8,12},{10,14},{12,8},{14,10},{16,20},{18,... | collective-permute-start | bytes 1572872 | tf_op jit(solution)/shard_map/ppermute | solution.py:62
  105.5 34.2 %collective-permute-start.28 = (bf16[4,64,1024]{2,1,0:T(8,128)(2,1)}, bf16[4,64,1024]{2,1,0:T(8,128)(2,1)}, u32[]{:S(2)}, u32[]{:S(2)}) collective-permute-start(bf16[4,64,1024]{2,1,0:T(8,128)(2,1)} %get-tuple-element.86.refs_4_), channel_id=1, source_target_pairs={{0,2},{2,0},{4,6},{6,4},{8,10},{10,8},{12,14},{14,12},{16,18},{18,... | collective-permute-start | bytes 1572872 | tf_op jit(solution)/shard_map/ppermute | solution.py:62
  133.3 31.3 %collective-permute-start.18 = (bf16[1024,512]{1,0:T(8,128)(2,1)}, bf16[1024,512]{1,0:T(8,128)(2,1)}, u32[]{:S(2)}, u32[]{:S(2)}) collective-permute-start(bf16[1024,512]{1,0:T(8,128)(2,1)} %shard_map.308.refs_0_), channel_id=1, source_target_pairs={{0,1},{1,0},{2,3},{3,2},{4,5},{5,4},{6,7},{7,6},{8,9},{9,8},{10,11... | collective-permute-start | bytes 3145736 | tf_op jit(solution)/shard_map/ppermute | solution.py:34
  133.3 33.2 %collective-permute-start.19 = (bf16[1024,512]{1,0:T(8,128)(2,1)S(1)}, bf16[1024,512]{1,0:T(8,128)(2,1)}, u32[]{:S(2)}, u32[]{:S(2)}) collective-permute-start(bf16[1024,512]{1,0:T(8,128)(2,1)S(1)} %copy-done.6), channel_id=1, source_target_pairs={{0,1},{1,0},{2,3},{3,2},{4,5},{5,4},{6,7},{7,6},{8,9},{9,8},{10,11... | collective-permute-start | bytes 3145736 | tf_op jit(solution)/shard_map/ppermute | solution.py:34
  139.6 24.4 %collective-permute-start.26 = (bf16[4,64,1024]{2,1,0:T(8,128)(2,1)}, bf16[4,64,1024]{2,1,0:T(8,128)(2,1)}, u32[]{:S(2)}, u32[]{:S(2)}) collective-permute-start(bf16[4,64,1024]{2,1,0:T(8,128)(2,1)} %collective-permute-done.24.refs_1_), channel_id=1, source_target_pairs={{0,4},{2,6},{4,0},{6,2},{8,12},{10,14},{12,8},{14,10},{16,20},{18,... | collective-permute-start | bytes 1572872 | tf_op jit(solution)/shard_map/ppermute | solution.py:62
  150.3 52.5 %collective-permute-start.34 = (bf16[4,128,512]{2,1,0:T(8,128)(2,1)}, bf16[4,128,512]{2,1,0:T(8,128)(2,1)}, u32[]{:S(2)}, u32[]{:S(2)}) collective-permute-start(bf16[4,128,512]{2,1,0:T(8,128)(2,1)} %get-tuple-element.91.refs_0_), channel_id=1, source_target_pairs={{0,4},{2,6},{4,0},{6,2},{8,12},{10,14},{12,8},{14,10},{16,20},{18,... | collective-permute-start | bytes 1572872 | tf_op jit(solution)/shard_map/ppermute | solution.py:62
  152.7 50.1 %collective-permute-start.37 = (bf16[4,128,512]{2,1,0:T(8,128)(2,1)}, bf16[4,128,512]{2,1,0:T(8,128)(2,1)}, u32[]{:S(2)}, u32[]{:S(2)}) collective-permute-start(bf16[4,128,512]{2,1,0:T(8,128)(2,1)} %get-tuple-element.92.refs_4_), channel_id=1, source_target_pairs={{0,2},{2,0},{4,6},{6,4},{8,10},{10,8},{12,14},{14,12},{16,18},{18,... | collective-permute-start | bytes 1572872 | tf_op jit(solution)/shard_map/ppermute | solution.py:62
  164.6 38.3 %collective-permute-start.35 = (bf16[4,128,512]{2,1,0:T(8,128)(2,1)S(1)}, bf16[4,128,512]{2,1,0:T(8,128)(2,1)}, u32[]{:S(2)}, u32[]{:S(2)}) collective-permute-start(bf16[4,128,512]{2,1,0:T(8,128)(2,1)S(1)} %collective-permute-done.33.refs_1_), channel_id=1, source_target_pairs={{0,4},{2,6},{4,0},{6,2},{8,12},{10,14},{12,8},{14,10},{16,20},{18,... | collective-permute-start | bytes 1572872 | tf_op jit(solution)/shard_map/ppermute | solution.py:62
  166.5 36.3 %collective-permute-start.38 = (bf16[4,128,512]{2,1,0:T(8,128)(2,1)S(1)}, bf16[4,128,512]{2,1,0:T(8,128)(2,1)S(1)}, u32[]{:S(2)}, u32[]{:S(2)}) collective-permute-start(bf16[4,128,512]{2,1,0:T(8,128)(2,1)S(1)} %collective-permute-done.36.refs_5_), channel_id=1, source_target_pairs={{0,2},{2,0},{4,6},{6,4},{8,10},{10,8},{12,14},{14,12},{16,18},{18,... | collective-permute-start | bytes 1572872 | tf_op jit(solution)/shard_map/ppermute | solution.py:62
  231.8 26.2 %collective-permute-start.55 = (bf16[2,4,64,1024]{3,2,1,0:T(8,128)(2,1)}, bf16[2,4,64,1024]{3,2,1,0:T(8,128)(2,1)S(1)}, u32[]{:S(2)}, u32[]{:S(2)}) collective-permute-start(bf16[2,4,64,1024]{3,2,1,0:T(8,128)(2,1)} %get-tuple-element.113), channel_id=1, source_target_pairs={{0,2},{2,0},{4,6},{6,4},{8,10},{10,8},{12,14},{14,12},{16,18},{18,... | collective-permute-start | bytes 3145736 | tf_op jit(solution)/shard_map/ppermute | solution.py:62
  232.4 26.2 %collective-permute-start.53 = (bf16[2,4,64,1024]{3,2,1,0:T(8,128)(2,1)}, bf16[2,4,64,1024]{3,2,1,0:T(8,128)(2,1)S(1)}, u32[]{:S(2)}, u32[]{:S(2)}) collective-permute-start(bf16[2,4,64,1024]{3,2,1,0:T(8,128)(2,1)} %get-tuple-element.111), channel_id=1, source_target_pairs={{0,4},{2,6},{4,0},{6,2},{8,12},{10,14},{12,8},{14,10},{16,20},{18,... | collective-permute-start | bytes 3145736 | tf_op jit(solution)/shard_map/ppermute | solution.py:62
  234.1 43.7 %collective-permute-start.63 = (bf16[2,4,128,512]{3,2,1,0:T(8,128)(2,1)}, bf16[2,4,128,512]{3,2,1,0:T(8,128)(2,1)S(1)}, u32[]{:S(2)}, u32[]{:S(2)}) collective-permute-start(bf16[2,4,128,512]{3,2,1,0:T(8,128)(2,1)} %get-tuple-element.117), channel_id=1, source_target_pairs={{0,2},{2,0},{4,6},{6,4},{8,10},{10,8},{12,14},{14,12},{16,18},{18,... | collective-permute-start | bytes 3145736 | tf_op jit(solution)/shard_map/ppermute | solution.py:62
  235.6 45.5 %collective-permute-start.61 = (bf16[2,4,128,512]{3,2,1,0:T(8,128)(2,1)}, bf16[2,4,128,512]{3,2,1,0:T(8,128)(2,1)S(1)}, u32[]{:S(2)}, u32[]{:S(2)}) collective-permute-start(bf16[2,4,128,512]{3,2,1,0:T(8,128)(2,1)} %get-tuple-element.115), channel_id=1, source_target_pairs={{0,4},{2,6},{4,0},{6,2},{8,12},{10,14},{12,8},{14,10},{16,20},{18,... | collective-permute-start | bytes 3145736 | tf_op jit(solution)/shard_map/ppermute | solution.py:62
  244.0 39.1 %collective-permute-start.40 = (bf16[512,1024]{1,0:T(8,128)(2,1)S(1)}, bf16[512,1024]{1,0:T(8,128)(2,1)S(1)}, u32[]{:S(2)}, u32[]{:S(2)}) collective-permute-start(bf16[512,1024]{1,0:T(8,128)(2,1)S(1)} %dynamic-slice_bitcast_fusion.1), channel_id=1, source_target_pairs={{0,1},{1,0},{2,3},{3,2},{4,5},{5,4},{6,7},{7,6},{8,9},{9,8},{10,11... | collective-permute-start | bytes 3145736 | tf_op jit(solution)/shard_map/ppermute | solution.py:34
  258.1 46.6 %collective-permute-start.39 = (bf16[1024,1024]{1,0:T(8,128)(2,1)S(1)}, bf16[1024,1024]{1,0:T(8,128)(2,1)S(1)}, u32[]{:S(2)}, u32[]{:S(2)}) collective-permute-start(bf16[1024,1024]{1,0:T(8,128)(2,1)S(1)} %copy-done.8), channel_id=1, source_target_pairs={{0,1},{1,0},{2,3},{3,2},{4,5},{5,4},{6,7},{7,6},{8,9},{9,8},{10,11... | collective-permute-start | bytes 6291464 | tf_op jit(solution)/shard_map/ppermute | solution.py:34
  258.6 33.7 %collective-permute-start.56 = (bf16[4,64,1024]{2,1,0:T(8,128)(2,1)S(1)}, bf16[4,64,1024]{2,1,0:T(8,128)(2,1)S(1)}, u32[]{:S(2)}, u32[]{:S(2)}) collective-permute-start(bf16[4,64,1024]{2,1,0:T(8,128)(2,1)S(1)} %get-tuple-element.146), channel_id=1, source_target_pairs={{0,4},{2,6},{4,0},{6,2},{8,12},{10,14},{12,8},{14,10},{16,20},{18,... | collective-permute-start | bytes 1572872 | tf_op jit(solution)/shard_map/ppermute | solution.py:62
  294.8 65.6 %collective-permute-start.59 = (bf16[64,2048]{1,0:T(8,128)(2,1)}, bf16[64,2048]{1,0:T(8,128)(2,1)}, u32[]{:S(2)}, u32[]{:S(2)}) collective-permute-start(bf16[64,2048]{1,0:T(8,128)(2,1)} %pad_maximum_fusion.4), channel_id=1, source_target_pairs={{0,24},{2,26},{4,28},{6,30},{8,16},{10,18},{12,20},{14,22},{16,8},... | collective-permute-start | bytes 786440 | tf_op jit(solution)/shard_map/ppermute | solution.py:62
  296.3 66.5 %collective-permute-start.58 = (bf16[64,2048]{1,0:T(8,128)(2,1)}, bf16[64,2048]{1,0:T(8,128)(2,1)}, u32[]{:S(2)}, u32[]{:S(2)}) collective-permute-start(bf16[64,2048]{1,0:T(8,128)(2,1)} %pad_maximum_fusion.3), channel_id=1, source_target_pairs={{0,16},{2,18},{4,20},{6,22},{8,24},{10,26},{12,28},{14,30},{16,0},... | collective-permute-start | bytes 786440 | tf_op jit(solution)/shard_map/ppermute | solution.py:62
  299.3 65.3 %collective-permute-start.57 = (bf16[64,2048]{1,0:T(8,128)(2,1)}, bf16[64,2048]{1,0:T(8,128)(2,1)}, u32[]{:S(2)}, u32[]{:S(2)}) collective-permute-start(bf16[64,2048]{1,0:T(8,128)(2,1)} %pad_maximum_fusion.2), channel_id=1, source_target_pairs={{0,8},{2,10},{4,12},{6,14},{8,0},{10,2},{12,4},{14,6},{16,24},{18,... | collective-permute-start | bytes 786440 | tf_op jit(solution)/shard_map/ppermute | solution.py:62
  302.4 77.2 %collective-permute-start.67 = (bf16[128,1024]{1,0:T(8,128)(2,1)}, bf16[128,1024]{1,0:T(8,128)(2,1)}, u32[]{:S(2)}, u32[]{:S(2)}) collective-permute-start(bf16[128,1024]{1,0:T(8,128)(2,1)} %pad_maximum_fusion.7), channel_id=1, source_target_pairs={{0,24},{2,26},{4,28},{6,30},{8,16},{10,18},{12,20},{14,22},{16,8},... | collective-permute-start | bytes 786440 | tf_op jit(solution)/shard_map/ppermute | solution.py:62
  305.9 73.7 %collective-permute-start.66 = (bf16[128,1024]{1,0:T(8,128)(2,1)}, bf16[128,1024]{1,0:T(8,128)(2,1)}, u32[]{:S(2)}, u32[]{:S(2)}) collective-permute-start(bf16[128,1024]{1,0:T(8,128)(2,1)} %pad_maximum_fusion.6), channel_id=1, source_target_pairs={{0,16},{2,18},{4,20},{6,22},{8,24},{10,26},{12,28},{14,30},{16,0},... | collective-permute-start | bytes 786440 | tf_op jit(solution)/shard_map/ppermute | solution.py:62
  369.1 26.3 %collective-permute-start.60 = (f32[32,2048]{1,0:T(8,128)}, f32[32,2048]{1,0:T(8,128)}, u32[]{:S(2)}, u32[]{:S(2)}) collective-permute-start(f32[32,2048]{1,0:T(8,128)} %get-tuple-element.172), channel_id=1, source_target_pairs={{0,1},{1,0},{2,3},{3,2},{4,5},{5,4},{6,7},{7,6},{8,9},{9,8},{10,11... | collective-permute-start | bytes 786440 | tf_op jit(solution)/shard_map/ppermute | solution.py:34
  377.8 33.2 %collective-permute-start.42 = (bf16[2,4,64,1280]{3,2,1,0:T(8,128)(2,1)}, bf16[2,4,64,1280]{3,2,1,0:T(8,128)(2,1)}, u32[]{:S(2)}, u32[]{:S(2)}) collective-permute-start(bf16[2,4,64,1280]{3,2,1,0:T(8,128)(2,1)} %get-tuple-element.106), channel_id=1, source_target_pairs={{0,4},{2,6},{4,0},{6,2},{8,12},{10,14},{12,8},{14,10},{16,20},{18,... | collective-permute-start | bytes 3932168 | tf_op jit(solution)/shard_map/ppermute | solution.py:62
  (73 other events, 1009.7 us)
